TPU v7x, 128 devices: a whole 4x4x4 slice. The times are simulated.
128 devices in a mesh: group: 8 (over z, core), dev: 16 (over y, x).
Axes of the slice: x: 4, y: 4, z: 4, core: 2. Of those that a mesh axis runs over, the one named last changes fastest.
Arguments:
- points: bfloat16 [196608, 512], P(('group', 'dev')), may hold values from -5 to 5
- targets: float32 [8, 196608], P(None, ('group', 'dev')), may hold values from -16 to 16
- partner_tiles: int32 [8, 16, 8, 2], replicated, may hold values from -1 to 5, as said below
Outputs:
- solution: float32 [8, 196608], P(None, ('group', 'dev'))
- residual: float32 [8, 196608], P(None, ('group', 'dev'))
Inputs may be any that keep to these rules, and one draw needn't show every extreme that they name: `partner_tiles`: entry [g, v, h, c] names a tile of block (h, v) whose points are coupled with every point of block (g, v), or is -1. For one v and two groups at most one of the two blocks names tiles of the other, and no block names tiles of its own group. The tiles named in [g, v, h] are distinct and stand before its -1 entries. In every draw some block names 2 tiles of one other group.
All inputs are finite; a program needn't handle non-finite values.
Results may differ from a plain program's by a relative error of at most 0.0003.
Values may be sent and summed in bfloat16 or wider, within the bound.
No kernel may reach another device: no remote copies, remote signals or barrier semaphores. Data moves between devices by JAX's collectives and lax.ppermute only.
A program may use at most 192 MiB of HBM per device.

v0:
```python
import jax
import jax.numpy as jnp
from jax import lax
from jax.experimental import pallas as pl
from jax.experimental.pallas import tpu as pltpu
from jax.sharding import PartitionSpec as P


TILE = 256
EXTRA = 8
SCALE = 3.9
C4 = 4.0 / SCALE**5
CUT = 5.0 * SCALE / 4.0
NT = (((1,), (1,)), ((), ()))
NN = (((1,), (0,)), ((), ()))
F32 = jnp.float32
BF16 = jnp.bfloat16
STAGES = ((2, 6, 1), (3, 7), (4, 5))
SWAPS = STAGES[0] + STAGES[1] + STAGES[2]

SMEM = pl.BlockSpec(memory_space=pltpu.SMEM)
ANY = pl.BlockSpec(memory_space=pl.ANY)
HBM = pl.BlockSpec(memory_space=pltpu.HBM)
VM = pl.BlockSpec(memory_space=pltpu.VMEM)


def mm(a, b, dims):
    return lax.dot_general(a, b, dims, preferred_element_type=F32)


def col_norms(x):
    x = x.astype(F32)
    return jnp.broadcast_to(jnp.sum(x * x, axis=1, keepdims=True), (x.shape[0], 128))


def kernel_tile(a, b_scaled, na, nb):
    q = mm(a, b_scaled, NT) + (jnp.concatenate([na, na], axis=1) + nb)
    q = jnp.maximum(q, 1e-30)
    u = jnp.maximum(SCALE - q * lax.rsqrt(q), 0.0)
    t = u * u
    return (t * t * (CUT - u)).astype(BF16)


def split(v):
    hi = v.astype(BF16)
    lo = (v - hi.astype(F32)).astype(BF16)
    return jnp.concatenate([hi, lo], axis=0)


def rhs_ones(rows, one):
    v = rows.astype(F32)
    return jnp.concatenate([v[:, 0:TILE], v[:, TILE:], jnp.full((16, TILE), one, F32)], axis=0).astype(BF16)


def fold(acc):
    return (acc[0:8] + acc[8:16]) * C4


def fold_ones(acc):
    return jnp.concatenate([acc[0:8] + acc[8:16], acc[16:24]], axis=0) * C4


def span(t):
    return pl.ds(pl.multiple_of(t * TILE, TILE), TILE)


def params(mib=12):
    return pltpu.CompilerParams(vmem_limit_bytes=mib * 1024 * 1024)


def f32(*shape):
    return jax.ShapeDtypeStruct(shape, F32)


def vmem_bf16(*shape):
    return pltpu.VMEM(shape, BF16)


def prep(partners, points, targets):
    n, d = points.shape
    nt = n // TILE

    def body(p_hbm, pts_ref, r_hbm, table_ref, msg_ref, *refs):
        outs, (r_ref, p_ref, sems) = refs[:-3], refs[-3:]
        g = lax.axis_index("group")
        dev = lax.axis_index("dev")
        copies = [pltpu.make_async_copy(r_hbm, r_ref, sems.at[nt])]
        for t in range(nt):
            s = slice(t * TILE, (t + 1) * TILE)
            copies.append(pltpu.make_async_copy(pts_ref.at[s, :], msg_ref.at[t, pl.ds(0, TILE), :], sems.at[t]))
        table_copy = pltpu.make_async_copy(p_hbm, p_ref, sems.at[nt + 1])
        table_copy.start()
        for cp in copies:
            cp.start()
        table_copy.wait()
        for h in range(8):
            for c in range(2):
                table_ref[h * 2 + c] = p_ref[h, g, c, dev]
                table_ref[16 + h * 2 + c] = p_ref[g, h, c, dev]
        for cp in copies:
            cp.wait()
        for t in range(nt):
            s = slice(t * TILE, (t + 1) * TILE)
            v = r_ref[:, s]
            hi = v.astype(BF16).astype(F32)
            msg_ref[t, TILE:, :] = jnp.concatenate([hi, v - hi], axis=1).astype(BF16)
        for k, out in zip(SWAPS, outs):
            for c in range(2):
                out[c] = msg_ref[jnp.maximum(p_ref[g ^ k, g, c, dev], 0)]

    return pl.pallas_call(
        body,
        out_shape=[jax.ShapeDtypeStruct((32,), jnp.int32), vmem_bf16(nt, TILE + EXTRA, d)]
        + [vmem_bf16(2, TILE + EXTRA, d) for _ in SWAPS],
        in_specs=[HBM, HBM, HBM],
        out_specs=[SMEM] + [VM] * (1 + len(SWAPS)),
        scratch_shapes=[
            pltpu.VMEM((8, n), F32),
            pltpu.SMEM(partners.shape, jnp.int32),
            pltpu.SemaphoreType.DMA((nt + 2,)),
        ],
        compiler_params=params(),
        name="prep",
    )(*(pltpu.with_memory_space_constraint(x, pltpu.HBM) for x in (partners, points, targets)))


def gate(held, arrived):
    m = len(held)

    def body(*refs):
        pass

    return pl.pallas_call(
        body,
        out_shape=[vmem_bf16(*x.shape) for x in held],
        in_specs=[VM] * m + [ANY] * len(arrived),
        out_specs=[VM] * m,
        input_output_aliases={i: i for i in range(m)},
        compiler_params=params(4),
        name="gate",
    )(*held, *arrived)


def local_first(own):
    nt, _, _ = own.shape
    n = nt * TILE

    def body(a_ref, k_ref, acc_ref, na, nb, va):
        for i in range(nt):
            s = slice(i * TILE, (i + 1) * TILE)
            x = col_norms(a_ref[i, 0:TILE, :])
            na[s, :] = x
            nb[:, s] = x.T[0:8]
            va[:, s] = rhs_ones(a_ref[i, TILE:, :], 1.0)

        def step(t, carry):
            s = span(t)
            b = a_ref[t, 0:TILE, :] * jnp.asarray(-2.0, BF16)
            for i in range(nt):
                c = slice(i * TILE, (i + 1) * TILE)
                k_ref[t, c, :] = kernel_tile(a_ref[i, 0:TILE, :], b, na[c, :], nb[0:1, s])
            acc_ref[:, s] = fold_ones(mm(va[...], k_ref[t], NN))
            return carry

        lax.fori_loop(0, nt, step, 0)

    return pl.pallas_call(
        body,
        out_shape=(vmem_bf16(nt, n, TILE), f32(16, n)),
        in_specs=[VM],
        out_specs=(VM, VM),
        scratch_shapes=[pltpu.VMEM((n, 128), F32), pltpu.VMEM((8, n), F32), pltpu.VMEM((32, n), BF16)],
        compiler_params=params(),
        name="local_first",
    )(own)


def band_first(left, own, right, after):
    nt, _, _ = own.shape
    n = nt * TILE
    m = len(after)

    def body(l_ref, a_ref, b_ref, *refs):
        k_ref, col_ref, rowl_ref, rowo_ref, na, nb, va, vb, acc = refs[m:]
        v = lax.axis_index("dev")
        has_left = (v > 0).astype(F32)
        has_right = (v < lax.axis_size("dev") - 1).astype(F32)
        for i in range(nt):
            s = slice(i * TILE, (i + 1) * TILE)
            e = slice(n + i * TILE, n + (i + 1) * TILE)
            na[s, :] = col_norms(l_ref[i, 0:TILE, :])
            na[e, :] = col_norms(a_ref[i, 0:TILE, :])
            nb[:, s] = col_norms(b_ref[i, 0:TILE, :]).T[0:8]
            va[:, s] = rhs_ones(l_ref[i, TILE:, :], has_left)
            va[:, e] = rhs_ones(a_ref[i, TILE:, :], 1.0)
            vb[:, s] = rhs_ones(b_ref[i, TILE:, :], has_right)
        acc[...] = jnp.zeros_like(acc)

        def step(t, carry):
            s = span(t)
            b = b_ref[t, 0:TILE, :] * jnp.asarray(-2.0, BF16)
            for j, x in enumerate((l_ref, a_ref)):
                for i in range(nt):
                    e = slice((j * nt + i) * TILE, (j * nt + i + 1) * TILE)
                    k_ref[t, e, :] = kernel_tile(x[i, 0:TILE, :], b, na[e, :], nb[0:1, s])
            k = k_ref[t]
            col_ref[:, s] = fold_ones(mm(va[...], k, NN))
            acc[...] += mm(vb[:, s], k, NT)
            return carry

        lax.fori_loop(0, nt, step, 0)
        rows = fold_ones(acc[...])
        rowl_ref[...] = rows[:, 0:n]
        rowo_ref[...] = rows[:, n:]

    return pl.pallas_call(
        body,
        out_shape=(vmem_bf16(nt, 2 * n, TILE), f32(16, n), f32(16, n), f32(16, n)),
        in_specs=[VM] * 3 + [ANY] * m,
        out_specs=(VM,) * 4,
        scratch_shapes=[
            pltpu.VMEM((2 * n, 128), F32),
            pltpu.VMEM((8, n), F32),
            pltpu.VMEM((32, 2 * n), BF16),
            pltpu.VMEM((32, n), BF16),
            pltpu.VMEM((32, 2 * n), F32),
        ],
        compiler_params=params(),
        name="band_first",
    )(left, own, right, *after)


def cross_first(ks, table, own, tiles, after, held=()):
    nt, _, d = own.shape
    n = nt * TILE
    m = len(ks)
    slots = 2 * m
    p = len(held)

    def body(q_ref, a_ref, _, *refs):
        tile_refs = refs[:m]
        k_ref, row_ref, *cols = refs[m + p : 2 * m + p + 2]
        buf, jobs, sems, na, va, acc, nb, col = refs[2 * m + 2 * p + 2 :]
        g = lax.axis_index("group")
        count = jnp.int32(0)
        for i, k in enumerate(ks):
            for c in range(2):
                live = q_ref[16 + (g ^ k) * 2 + c] >= 0

                @pl.when(live)
                def _(count=count, i=i, k=k, c=c):
                    pltpu.make_async_copy(tile_refs[i].at[c], buf.at[count], sems.at[count]).start()
                    jobs[count] = 2 * i + c

                count = count + live.astype(jnp.int32)
        for i in range(nt):
            s = slice(i * TILE, (i + 1) * TILE)
            na[s, :] = col_norms(a_ref[i, 0:TILE, :])
            va[:, s] = rhs_ones(a_ref[i, TILE:, :], 1.0)
        acc[...] = jnp.zeros_like(acc)

        def step(j, carry):
            pltpu.make_async_copy(tile_refs[0].at[0], buf.at[j], sems.at[j]).wait()
            b = buf[j, 0:TILE, :]
            nb[...] = col_norms(b).T[0:8]
            b = b * jnp.asarray(-2.0, BF16)
            vb = rhs_ones(buf[j, TILE:, :], 1.0)
            for i in range(nt):
                c = slice(i * TILE, (i + 1) * TILE)
                k_ref[j, c, :] = kernel_tile(a_ref[i, 0:TILE, :], b, na[c, :], nb[0:1, :])
            k = k_ref[j]
            col[jobs[j]] = fold_ones(mm(va[...], k, NN))
            acc[...] += mm(vb, k, NT)
            return carry

        lax.fori_loop(0, count, step, 0)
        row_ref[...] = fold_ones(acc[...])
        for i, out in enumerate(cols):
            out[...] = col[2 * i : 2 * i + 2]

    return pl.pallas_call(
        body,
        out_shape=[vmem_bf16(slots, n, TILE), f32(16, n)] + [f32(2, 16, TILE)] * (m + p),
        in_specs=[SMEM, VM, ANY] + [ANY] * m + [VM] * p,
        out_specs=[VM] * (2 + m + p),
        input_output_aliases={3 + m + i: 2 + m + i for i in range(p)},
        scratch_shapes=[
            pltpu.VMEM((slots, TILE + EXTRA, d), BF16),
            pltpu.SMEM((slots,), jnp.int32),
            pltpu.SemaphoreType.DMA((slots,)),
            pltpu.VMEM((n, 128), F32),
            pltpu.VMEM((32, n), BF16),
            pltpu.VMEM((32, n), F32),
            pltpu.VMEM((8, TILE), F32),
            pltpu.VMEM((slots, 16, TILE), F32),
        ],
        compiler_params=params(),
    )(table, own, after, *tiles, *held)


def combine(table, r, parts, ret):
    n = r.shape[1]
    m = len(parts)

    def body(q_ref, r_ref, *refs):
        part_refs, (*x_refs, w_ref, deg_ref, sum_ref, acc) = refs[:m], refs[m:]
        x_refs, out_refs = x_refs[:7], x_refs[7:]
        g = lax.axis_index("group")
        total = part_refs[0][...]
        for p in part_refs[1:]:
            total = total + p[...]
        acc[...] = total
        for k, x in zip(SWAPS, x_refs):
            for c in range(2):
                t = q_ref[(g ^ k) * 2 + c]

                @pl.when(t >= 0)
                def _(x=x, c=c, t=t):
                    acc[:, span(t)] = acc[:, span(t)] + x[c]

        rv = r_ref[...]
        deg = acc[8:16, :]
        w = 0.5 * (deg * rv - acc[0:8, :])
        w_ref[...] = w
        deg_ref[...] = deg
        for k, out in zip(SWAPS, out_refs):
            for c in range(2):
                t = jnp.maximum(q_ref[(g ^ k) * 2 + c], 0)
                out[c * 8 : c * 8 + 8, :] = w_ref[:, span(t)]
        lane = lax.broadcasted_iota(jnp.int32, (8, 128), 1)
        sums = jnp.zeros((8, 128), F32)
        for k, v in enumerate((rv * rv, rv * w, w * w, 0.5 * deg * w * w)):
            sums = jnp.where(lane == k, jnp.sum(v, axis=1, keepdims=True), sums)
        sum_ref[...] = sums

    return pl.pallas_call(
        body,
        out_shape=[f32(16, TILE)] * 7 + [f32(8, n), f32(8, n), f32(8, 128)],
        in_specs=[SMEM] + [VM] * (m + 8),
        out_specs=[VM] * 10,
        scratch_shapes=[pltpu.VMEM((16, n), F32)],
        compiler_params=params(),
        name="combine",
    )(table, r, *parts, *ret)


def local_second(k_local, w):
    nt, n, _ = k_local.shape

    def body(k_ref, w_ref, out_ref):
        va = split(w_ref[...])
        for t in range(nt):
            out_ref[:, t * TILE : (t + 1) * TILE] = fold(mm(va, k_ref[t], NN))

    return pl.pallas_call(
        body,
        out_shape=f32(8, n),
        in_specs=[VM, VM],
        out_specs=VM,
        compiler_params=params(),
        name="local_second",
    )(k_local, w)


def band_second(k_band, w_left, w, w_right, after):
    nt, n2, _ = k_band.shape
    n = n2 // 2

    def body(k_ref, wl_ref, w_ref, wb_ref, _, col_ref, rowl_ref, rowo_ref, va, acc):
        va[:, 0:n] = split(wl_ref[...])
        va[:, n:] = split(w_ref[...])
        vb = split(wb_ref[...])
        for t in range(nt):
            s = slice(t * TILE, (t + 1) * TILE)
            col_ref[:, s] = fold(mm(va[...], k_ref[t], NN))
            new = mm(vb[:, s], k_ref[t], NT)
            acc[...] = new if t == 0 else acc[...] + new
        rows = fold(acc[...])
        rowl_ref[...] = rows[:, 0:n]
        rowo_ref[...] = rows[:, n:]

    return pl.pallas_call(
        body,
        out_shape=(f32(8, n), f32(8, n), f32(8, n)),
        in_specs=[VM] * 4 + [ANY],
        out_specs=(VM,) * 3,
        scratch_shapes=[pltpu.VMEM((16, n2), BF16), pltpu.VMEM((16, n2), F32)],
        compiler_params=params(),
        name="band_second",
    )(k_band, w_left, w, w_right, after)


def cross_second(table, k_caches, w, xw, sums, loc, row_left, row_own, w_left):
    n = w.shape[1]

    def body(
        q_ref, ka_ref, kb_ref, kc_ref, w_ref, sum_ref, loc_ref, rl_ref, ro_ref, wl_ref, *refs
    ):
        xw_refs, (col_ref, row_ref, va, acc, jobs, xw_ref) = refs[:7], refs[7:]
        g = lax.axis_index("group")
        for k, x in zip(SWAPS, xw_refs):
            xw_ref[g ^ k] = x[...]
        va[...] = split(w_ref[...])
        acc[...] = jnp.zeros_like(acc)
        for ks, k_ref in zip(STAGES, (ka_ref, kb_ref, kc_ref)):
            count = jnp.int32(0)
            for k in ks:
                for c in range(2):
                    live = q_ref[16 + (g ^ k) * 2 + c] >= 0

                    @pl.when(live)
                    def _(count=count, k=k, c=c):
                        jobs[count] = (g ^ k) * 2 + c

                    count = count + live.astype(jnp.int32)

            def step(j, carry, k_ref=k_ref):
                slot = jobs[j]
                h, c = slot >> 1, slot & 1
                rows = pl.ds(pl.multiple_of(c * 8, 8), 8)
                k = k_ref[j]
                col_ref[h, rows, :] = fold(mm(va[...], k, NN))
                acc[...] += mm(split(xw_ref[h, rows, :]), k, NT)
                return carry

            lax.fori_loop(0, count, step, 0)
        row = fold(acc[...])
        row_ref[...] = row
        pairs = w_ref[...] * (0.5 * loc_ref[...] + ro_ref[...] + row) + wl_ref[...] * rl_ref[...]
        lane = lax.broadcasted_iota(jnp.int32, (8, 128), 1)
        pay = jnp.where(lane == 3, sum_ref[...] - jnp.sum(pairs, axis=1, keepdims=True), sum_ref[...])
        for h in range(8):
            col_ref[h, 16:24, 0:128] = pay
            col_ref[h, 16:24, 128:] = jnp.zeros((8, 128), F32)

    return pl.pallas_call(
        body,
        out_shape=(f32(8, 24, TILE), f32(8, n)),
        in_specs=[SMEM] + [VM] * 16,
        out_specs=(VM, VM),
        scratch_shapes=[
            pltpu.VMEM((16, n), BF16),
            pltpu.VMEM((16, n), F32),
            pltpu.SMEM((16,), jnp.int32),
            pltpu.VMEM((8, 16, TILE), F32),
        ],
        compiler_params=params(),
        name="cross_second",
    )(table, *k_caches, w, sums, loc, row_left, row_own, w_left, *xw)


def group_sum(table, w, deg, parts, ret):
    n = w.shape[1]
    m = len(parts)

    def body(q_ref, w_ref, deg_ref, *refs):
        part_refs, (x_ref, w2_ref, out_ref, acc) = refs[:m], refs[m:]
        total = part_refs[0][...]
        for p in part_refs[1:]:
            total = total + p[...]
        acc[...] = total
        for h in range(8):
            for c in range(2):
                t = q_ref[h * 2 + c]

                @pl.when(t >= 0)
                def _(h=h, c=c, t=t):
                    acc[:, span(t)] = acc[:, span(t)] + x_ref[h, c * 8 : c * 8 + 8, :]

        w2_ref[...] = 0.5 * (deg_ref[...] * w_ref[...] - acc[...])
        sums = x_ref[0, 16:24, 0:128]
        for h in range(1, 8):
            sums = sums + x_ref[h, 16:24, 0:128]
        for v in range(16):
            out_ref[v] = sums

    return pl.pallas_call(
        body,
        out_shape=(f32(8, n), f32(16, 8, 128)),
        in_specs=[SMEM] + [VM] * (3 + m),
        out_specs=(VM, VM),
        scratch_shapes=[pltpu.VMEM((8, n), F32)],
        compiler_params=params(),
        name="group_sum",
    )(table, w, deg, *parts, ret)


def finish(gathered, r, w, w2):
    n = r.shape[1]

    def body(g_ref, r_ref, w_ref, w2_ref, sol_ref, res_ref):
        sums = g_ref[0]
        for v in range(1, 16):
            sums = sums + g_ref[v]
        rho, mu, nu, xi = (sums[:, k : k + 1] for k in range(4))
        rv = r_ref[...]
        wv = w_ref[...]
        first = rho / (rho + mu)
        gap = (nu - mu * (mu / rho)) * (first * first)
        beta = gap / rho
        cr = mu / (rho + mu) + beta
        curvature = cr * cr * (rho + mu) - 2.0 * cr * first * (mu + nu) + first * first * (nu + xi)
        second = gap / curvature
        sol_ref[...] = (first + second * cr) * rv - (second * first) * wv
        res_ref[...] = (
            (mu / (rho + mu) - second * cr) * rv
            + (second * (first - cr) - first) * wv
            + (second * first) * w2_ref[...]
        )

    return pl.pallas_call(
        body,
        out_shape=(f32(8, n), f32(8, n)),
        in_specs=[VM] * 4,
        out_specs=(VM, VM),
        compiler_params=params(),
        name="finish",
    )(gathered, r, w, w2)


def on_device(points, targets, partner_tiles):
    dev_count = lax.axis_size("dev")
    to_right = [(i, i + 1) for i in range(dev_count - 1)]
    to_left = [(i + 1, i) for i in range(dev_count - 1)]

    def right_of(x):
        return lax.ppermute(x, "dev", to_left)

    def left_of(x):
        return lax.ppermute(x, "dev", to_right)

    def swap(x, k):
        return lax.ppermute(x, "group", [(i, i ^ k) for i in range(8)])

    def trade(x, axis="group"):
        return lax.all_to_all(x, axis, split_axis=0, concat_axis=0, tiled=True)

    table, own, *outgoing = prep(jnp.transpose(partner_tiles, (0, 2, 3, 1)), points, targets)
    arrived = {}
    for x, k in zip(outgoing, SWAPS[:5]):
        arrived[k] = swap(x, k)
    left = left_of(own)
    right = right_of(own)
    k_local, acc_local = local_first(own)

    def cross(stage, after, held=()):
        return cross_first(stage, table, own, [arrived[k] for k in stage], after, held)

    k_a, row_a, *col_a = cross(STAGES[0], acc_local)
    for x, k in zip(gate(outgoing[5:], [row_a, arrived[3], arrived[7]]), STAGES[2]):
        arrived[k] = swap(x, k)
    k_b, row_b, *col_b = cross(STAGES[1], row_a, col_a)
    ret_near = []
    for x, k in zip(col_b, STAGES[1] + STAGES[0]):
        ret_near.append(swap(x, k))
    k_band, to_r, to_l, acc_band = band_first(left, own, right, [row_b])
    from_left, from_right = left_of(to_r), right_of(to_l)
    k_c, row_c, *col_c = cross(STAGES[2], acc_band)
    ret = ret_near[2:] + ret_near[:2] + [swap(x, k) for x, k in zip(col_c, STAGES[2])]
    *xw_out, w, deg, sums = combine(
        table, targets, (acc_local, acc_band, from_left, from_right, row_a, row_b, row_c), ret
    )
    w_left, w_right = left_of(w), right_of(w)
    xw = [swap(x, k) for x, k in zip(xw_out, SWAPS)]
    loc2 = local_second(k_local, w)
    col_r, rowl_b, rowo_b = band_second(k_band, w_left, w, w_right, loc2)
    from_left2 = left_of(col_r)
    from_right2 = right_of(rowl_b)
    col_x, row_x = cross_second(table, (k_a, k_b, k_c), w, xw, sums, loc2, rowl_b, rowo_b, w_left)
    w2, column = group_sum(table, w, deg, (loc2, rowo_b, row_x, from_left2, from_right2), trade(col_x))
    return finish(trade(column, "dev"), targets, w, w2)


def solution(mesh):
    return jax.shard_map(
        on_device,
        mesh=mesh,
        in_specs=(P(("group", "dev"), None), P(None, ("group", "dev")), P()),
        out_specs=(P(None, ("group", "dev")), P(None, ("group", "dev"))),
        check_vma=False,
    )
```

profile of v0, /device:TPU:0, one launch (start us, length us, event | category | flops | bytes accessed | tf_op | source)
XLA Modules:
  0.0 149.6 jit_solution(7679482474947741213)
XLA Ops:
  0.6 2.6 %prep.1 = (s32[32]{0:T(128)S(1)}, bf16[6,264,512]{2,1,0:T(8,128)(2,1)S(1)}, bf16[2,264,512]{2,1,0:T(8,128)(2,1)S(1)}, bf16[2,264,512]{2,1,0:T(8,128)(2,1)S(1)}, ...) custom-call(s32[8,8,2,16]{3,2,1,0:T(2,128)} %bitcast.1, ...), custom_call_target="tpu_custom_call" | custom-call | tf_op jit(solution)/shard_map/prep/pallas_call | solution.py:111
  3.2 1.3 collective-permute-start.1
  4.5 4.6 %collective-permute-start = (bf16[6,264,512]{2,1,0:T(8,128)(2,1)S(1)}, bf16[6,264,512]{2,1,0:T(8,128)(2,1)S(1)}, u32[]{:S(2)}, u32[]{:S(2)}) collective-permute-start(bf16[6,264,512]{2,1,0:T(8,128)(2,1)S(1)} %get-tuple-element.53.a_ref), channel_id=1, source_target_pairs={{0,1},{1,2},{2,3},{3,4},{4,5},{5,6},{6,7},{7,8},{8,9},{9,10},{10,1... | collective-permute-start | bytes 4866056 | tf_op jit(solution)/shard_map/ppermute | solution.py:530
  9.1 2.1 %collective-permute-start.2 = (bf16[2,264,512]{2,1,0:T(8,128)(2,1)S(1)}, bf16[2,264,512]{2,1,0:T(8,128)(2,1)S(1)}, u32[]{:S(2)}, u32[]{:S(2)}) collective-permute-start(bf16[2,264,512]{2,1,0:T(8,128)(2,1)S(1)} %get-tuple-element.55), channel_id=1, source_target_pairs={{0,32},{16,48},{32,0},{48,16},{64,96},{80,112},{96,64},{112,80},{1... | collective-permute-start | bytes 1622024 | tf_op jit(solution)/shard_map/ppermute | solution.py:533
  11.3 2.5 %collective-permute-start.3 = (bf16[2,264,512]{2,1,0:T(8,128)(2,1)S(1)}, bf16[2,264,512]{2,1,0:T(8,128)(2,1)S(1)}, u32[]{:S(2)}, u32[]{:S(2)}) collective-permute-start(bf16[2,264,512]{2,1,0:T(8,128)(2,1)S(1)} %get-tuple-element.56), channel_id=1, source_target_pairs={{0,96},{16,112},{32,64},{48,80},{64,32},{80,48},{96,0},{112,16},{1... | collective-permute-start | bytes 1622024 | tf_op jit(solution)/shard_map/ppermute | solution.py:533
  13.8 9.2 %collective-permute-done.2.refs_0_ = bf16[2,264,512]{2,1,0:T(8,128)(2,1)S(1)} collective-permute-done((bf16[2,264,512]{2,1,0:T(8,128)(2,1)S(1)}, bf16[2,264,512]{2,1,0:T(8,128)(2,1)S(1)}, u32[]{:S(2)}, u32[]{:S(2)}) %collective-permute-start.2) | collective-permute-done | bytes 540704 | tf_op jit(solution)/shard_map/ppermute | solution.py:533
  23.0 2.7 %collective-permute-done.3.refs_1_ = bf16[2,264,512]{2,1,0:T(8,128)(2,1)S(1)} collective-permute-done((bf16[2,264,512]{2,1,0:T(8,128)(2,1)S(1)}, bf16[2,264,512]{2,1,0:T(8,128)(2,1)S(1)}, u32[]{:S(2)}, u32[]{:S(2)}) %collective-permute-start.3) | collective-permute-done | bytes 540704 | tf_op jit(solution)/shard_map/ppermute | solution.py:533
  25.6 1.3 collective-permute-start.6
  27.0 6.7 %local_first.1 = (bf16[6,1536,256]{2,1,0:T(8,128)(2,1)S(1)}, f32[16,1536]{1,0:T(8,128)S(1)}) custom-call(bf16[6,264,512]{2,1,0:T(8,128)(2,1)S(1)} %get-tuple-element.53.a_ref), custom_call_target="tpu_custom_call" | custom-call | tf_op jit(solution)/shard_map/local_first/pallas_call | solution.py:167
  33.7 1.0 shard_map.50
  34.7 2.5 %collective-permute-done.5.refs_0_.refs_3_ = bf16[2,264,512]{2,1,0:T(8,128)(2,1)S(1)} collective-permute-done((bf16[2,264,512]{2,1,0:T(8,128)(2,1)S(1)}, bf16[2,264,512]{2,1,0:T(8,128)(2,1)S(1)}, u32[]{:S(2)}, u32[]{:S(2)}) %collective-permute-start.5) | collective-permute-done | bytes 540704 | tf_op jit(solution)/shard_map/ppermute | solution.py:533
  37.3 4.0 %collective-permute-done.6.refs_1_.refs_4_ = bf16[2,264,512]{2,1,0:T(8,128)(2,1)S(1)} collective-permute-done((bf16[2,264,512]{2,1,0:T(8,128)(2,1)S(1)}, bf16[2,264,512]{2,1,0:T(8,128)(2,1)S(1)}, u32[]{:S(2)}, u32[]{:S(2)}) %collective-permute-start.6) | collective-permute-done | bytes 540704 | tf_op jit(solution)/shard_map/ppermute | solution.py:533
  41.3 0.7 collective-permute-start.9
  42.0 2.1 %collective-permute-start.10 = (bf16[2,264,512]{2,1,0:T(8,128)(2,1)S(1)}, bf16[2,264,512]{2,1,0:T(8,128)(2,1)S(1)}, u32[]{:S(2)}, u32[]{:S(2)}) collective-permute-start(bf16[2,264,512]{2,1,0:T(8,128)(2,1)S(1)} %get-tuple-element.71), channel_id=1, source_target_pairs={{0,80},{16,64},{32,112},{48,96},{64,16},{80,0},{96,48},{112,32},{1... | collective-permute-start | bytes 1622024 | tf_op jit(solution)/shard_map/ppermute | solution.py:533
  44.1 1.0 shard_map.51
  45.1 2.0 %collective-permute-start.11 = (f32[2,16,256]{2,1,0:T(8,128)S(1)}, f32[2,16,256]{2,1,0:T(8,128)S(1)}, u32[]{:S(2)}, u32[]{:S(2)}) collective-permute-start(f32[2,16,256]{2,1,0:T(8,128)S(1)} %get-tuple-element.73), channel_id=1, source_target_pairs={{0,32},{16,48},{32,0},{48,16},{64,96},{80,112},{96,64},{112,80},{1... | collective-permute-start | bytes 98312 | tf_op jit(solution)/shard_map/ppermute | solution.py:533
  47.1 14.8 %band_first.1 = (bf16[6,3072,256]{2,1,0:T(8,128)(2,1)S(1)}, f32[16,1536]{1,0:T(8,128)S(1)}, f32[16,1536]{1,0:T(8,128)S(1)}, f32[16,1536]{1,0:T(8,128)S(1)}) custom-call(bf16[6,264,512]{2,1,0:T(8,128)(2,1)S(1)} %collective-permute-done.l_ref, bf16[6,264,512]{2,1,0:T(8,128)(2,1)S(1)} %get-tuple-element.53.a_ref, ...), custom_call_target="tpu_custom_call" | custom-call | tf_op jit(solution)/shard_map/band_first/pallas_call | solution.py:216
  61.9 6.7 %collective-permute-start.7 = (f32[16,1536]{1,0:T(8,128)S(1)}, f32[16,1536]{1,0:T(8,128)S(1)}, u32[]{:S(2)}, u32[]{:S(2)}) collective-permute-start(f32[16,1536]{1,0:T(8,128)S(1)} %get-tuple-element.66), channel_id=1, source_target_pairs={{0,1},{1,2},{2,3},{3,4},{4,5},{5,6},{6,7},{7,8},{8,9},{9,10},{10,1... | collective-permute-start | bytes 294920 | tf_op jit(solution)/shard_map/ppermute | solution.py:530
  68.6 1.3 collective-permute-start.8
  69.9 2.4 %collective-permute-start.12 = (f32[2,16,256]{2,1,0:T(8,128)S(1)}, f32[2,16,256]{2,1,0:T(8,128)S(1)}, u32[]{:S(2)}, u32[]{:S(2)}) collective-permute-start(f32[2,16,256]{2,1,0:T(8,128)S(1)} %get-tuple-element.74), channel_id=1, source_target_pairs={{0,96},{16,112},{32,64},{48,80},{64,32},{80,48},{96,0},{112,16},{1... | collective-permute-start | bytes 98312 | tf_op jit(solution)/shard_map/ppermute | solution.py:533
  72.3 1.5 %collective-permute-start.14 = (f32[2,16,256]{2,1,0:T(8,128)S(1)}, f32[2,16,256]{2,1,0:T(8,128)S(1)}, u32[]{:S(2)}, u32[]{:S(2)}) collective-permute-start(f32[2,16,256]{2,1,0:T(8,128)S(1)} %get-tuple-element.76), channel_id=1, source_target_pairs={{0,48},{16,32},{32,16},{48,0},{64,112},{80,96},{96,80},{112,64},{1... | collective-permute-start | bytes 98312 | tf_op jit(solution)/shard_map/ppermute | solution.py:533
  73.8 1.2 shard_map.52
  75.0 0.1 collective-permute-done.12.refs_8_
  75.1 2.8 %collective-permute-start.15 = (f32[2,16,256]{2,1,0:T(8,128)S(1)}, f32[2,16,256]{2,1,0:T(8,128)S(1)}, u32[]{:S(2)}, u32[]{:S(2)}) collective-permute-start(f32[2,16,256]{2,1,0:T(8,128)S(1)} %get-tuple-element.77), channel_id=1, source_target_pairs={{0,112},{16,96},{32,80},{48,64},{64,48},{80,32},{96,16},{112,0},{1... | collective-permute-start | bytes 98312 | tf_op jit(solution)/shard_map/ppermute | solution.py:533
  77.9 4.4 %collective-permute-start.16 = (f32[2,16,256]{2,1,0:T(8,128)S(1)}, f32[2,16,256]{2,1,0:T(8,128)S(1)}, u32[]{:S(2)}, u32[]{:S(2)}) collective-permute-start(f32[2,16,256]{2,1,0:T(8,128)S(1)} %get-tuple-element.78), channel_id=1, source_target_pairs={{0,64},{16,80},{32,96},{48,112},{64,0},{80,16},{96,32},{112,48},{1... | collective-permute-start | bytes 98312 | tf_op jit(solution)/shard_map/ppermute | solution.py:533
  82.3 1.9 %collective-permute-done.16.refs_12_ = f32[2,16,256]{2,1,0:T(8,128)S(1)} collective-permute-done((f32[2,16,256]{2,1,0:T(8,128)S(1)}, f32[2,16,256]{2,1,0:T(8,128)S(1)}, u32[]{:S(2)}, u32[]{:S(2)}) %collective-permute-start.16) | collective-permute-done | bytes 32800 | tf_op jit(solution)/shard_map/ppermute | solution.py:533
  84.1 3.0 %collective-permute-done.17.refs_13_ = f32[2,16,256]{2,1,0:T(8,128)S(1)} collective-permute-done((f32[2,16,256]{2,1,0:T(8,128)S(1)}, f32[2,16,256]{2,1,0:T(8,128)S(1)}, u32[]{:S(2)}, u32[]{:S(2)}) %collective-permute-start.17) | collective-permute-done | bytes 32800 | tf_op jit(solution)/shard_map/ppermute | solution.py:533
  87.1 0.8 combine.1
  87.9 1.3 collective-permute-start.19
  89.2 4.5 %collective-permute-start.18 = (f32[8,1536]{1,0:T(8,128)S(1)}, f32[8,1536]{1,0:T(8,128)S(1)}, u32[]{:S(2)}, u32[]{:S(2)}) collective-permute-start(f32[8,1536]{1,0:T(8,128)S(1)} %get-tuple-element.80.w_ref), channel_id=1, source_target_pairs={{0,1},{1,2},{2,3},{3,4},{4,5},{5,6},{6,7},{7,8},{8,9},{9,10},{10,1... | collective-permute-start | bytes 147464 | tf_op jit(solution)/shard_map/ppermute | solution.py:530
  93.9 2.4 %collective-permute-start.21 = (f32[16,256]{1,0:T(8,128)S(1)}, f32[16,256]{1,0:T(8,128)S(1)}, u32[]{:S(2)}, u32[]{:S(2)}) collective-permute-start(f32[16,256]{1,0:T(8,128)S(1)} %get-tuple-element.91), channel_id=1, source_target_pairs={{0,96},{16,112},{32,64},{48,80},{64,32},{80,48},{96,0},{112,16},{1... | collective-permute-start | bytes 49160 | tf_op jit(solution)/shard_map/ppermute | solution.py:533
  96.3 1.3 collective-permute-done.20.refs_0_
  97.6 0.3 collective-permute-start.23
  98.0 1.0 collective-permute-done.21.refs_1_
  98.9 0.9 collective-permute-start.24
  99.8 1.7 %collective-permute-start.25 = (f32[16,256]{1,0:T(8,128)S(1)}, f32[16,256]{1,0:T(8,128)S(1)}, u32[]{:S(2)}, u32[]{:S(2)}) collective-permute-start(f32[16,256]{1,0:T(8,128)S(1)} %get-tuple-element.95), channel_id=1, source_target_pairs={{0,64},{16,80},{32,96},{48,112},{64,0},{80,16},{96,32},{112,48},{1... | collective-permute-start | bytes 49160 | tf_op jit(solution)/shard_map/ppermute | solution.py:533
  101.4 2.8 %collective-permute-start.26 = (f32[16,256]{1,0:T(8,128)S(1)}, f32[16,256]{1,0:T(8,128)S(1)}, u32[]{:S(2)}, u32[]{:S(2)}) collective-permute-start(f32[16,256]{1,0:T(8,128)S(1)} %get-tuple-element.96), channel_id=1, source_target_pairs={{0,80},{16,64},{32,112},{48,96},{64,16},{80,0},{96,48},{112,32},{1... | collective-permute-start | bytes 49160 | tf_op jit(solution)/shard_map/ppermute | solution.py:533
  104.2 0.7 local_second.1._.loc_ref.refs_0_
  105.0 3.8 %band_second.1 = (f32[8,1536]{1,0:T(8,128)S(1)}, f32[8,1536]{1,0:T(8,128)S(1)}, f32[8,1536]{1,0:T(8,128)S(1)}) custom-call(bf16[6,3072,256]{2,1,0:T(8,128)(2,1)S(1)} %get-tuple-element.83.k_ref, f32[8,1536]{1,0:T(8,128)S(1)} %collective-permute-done.18.wl_ref, f32[8,1536]{1,0:T(8,128)S(1)} %get-tuple-element.80.w_ref, ...), custom_call_target="tpu_custom_call" | custom-call | tf_op jit(solution)/shard_map/band_second/pallas_call | solution.py:382
  108.8 1.4 cross_second.1
  110.2 6.8 %all-to-all-start = ((f32[8,24,256]{2,1,0:T(8,128)}), f32[8,24,256]{2,1,0:T(8,128)S(1)}, u32[]{:S(2)}, u32[]{:S(2)}) async-start(f32[8,24,256]{2,1,0:T(8,128)} %get-tuple-element.99), calls=%async_computation | async-start | bytes 393216 | tf_op jit(solution)/shard_map/all_to_all | solution.py:536
  117.0 6.5 %collective-permute-start.27 = (f32[8,1536]{1,0:T(8,128)S(1)}, f32[8,1536]{1,0:T(8,128)S(1)}, u32[]{:S(2)}, u32[]{:S(2)}) collective-permute-start(f32[8,1536]{1,0:T(8,128)S(1)} %get-tuple-element.98), channel_id=1, source_target_pairs={{0,1},{1,2},{2,3},{3,4},{4,5},{5,6},{6,7},{7,8},{8,9},{9,10},{10,1... | collective-permute-start | bytes 147464 | tf_op jit(solution)/shard_map/ppermute | solution.py:530
  123.5 1.3 collective-permute-start.28
  124.8 0.4 collective-permute-done.27.refs_3_
  125.2 4.5 %collective-permute-done.28.refs_4_ = f32[8,1536]{1,0:T(8,128)S(1)} collective-permute-done((f32[8,1536]{1,0:T(8,128)S(1)}, f32[8,1536]{1,0:T(8,128)S(1)}, u32[]{:S(2)}, u32[]{:S(2)}) %collective-permute-start.28) | collective-permute-done | bytes 49184 | tf_op jit(solution)/shard_map/ppermute | solution.py:527
  129.7 0.7 group_sum.1
  130.5 18.0 %all_to_all.10.g_ref = f32[16,8,128]{2,1,0:T(8,128)S(1)} all-to-all(f32[16,8,128]{2,1,0:T(8,128)S(1)} %get-tuple-element.100), channel_id=1, replica_groups=mesh['group'=8,'dev'=16] {'dev'}, dimensions={0} | all-to-all | bytes 131072 | tf_op jit(solution)/shard_map/all_to_all | solution.py:536
  148.5 1.1 finish.1
  (28 shorter events, 0.2 us)
Async XLA Ops:
  3.2 43.9 %collective-permute-start.1 = (bf16[6,264,512]{2,1,0:T(8,128)(2,1)S(1)}, bf16[6,264,512]{2,1,0:T(8,128)(2,1)S(1)}, u32[]{:S(2)}, u32[]{:S(2)}) collective-permute-start(bf16[6,264,512]{2,1,0:T(8,128)(2,1)S(1)} %get-tuple-element.53.a_ref), channel_id=1, source_target_pairs={{1,0},{2,1},{3,2},{4,3},{5,4},{6,5},{7,6},{8,7},{9,8},{10,9},{11,1... | collective-permute-start | bytes 4866056 | tf_op jit(solution)/shard_map/ppermute | solution.py:527
  4.5 42.6 %collective-permute-start = (bf16[6,264,512]{2,1,0:T(8,128)(2,1)S(1)}, bf16[6,264,512]{2,1,0:T(8,128)(2,1)S(1)}, u32[]{:S(2)}, u32[]{:S(2)}) collective-permute-start(bf16[6,264,512]{2,1,0:T(8,128)(2,1)S(1)} %get-tuple-element.53.a_ref), channel_id=1, source_target_pairs={{0,1},{1,2},{2,3},{3,4},{4,5},{5,6},{6,7},{7,8},{8,9},{9,10},{10,1... | collective-permute-start | bytes 4866056 | tf_op jit(solution)/shard_map/ppermute | solution.py:530
  9.1 13.8 %collective-permute-start.2 = (bf16[2,264,512]{2,1,0:T(8,128)(2,1)S(1)}, bf16[2,264,512]{2,1,0:T(8,128)(2,1)S(1)}, u32[]{:S(2)}, u32[]{:S(2)}) collective-permute-start(bf16[2,264,512]{2,1,0:T(8,128)(2,1)S(1)} %get-tuple-element.55), channel_id=1, source_target_pairs={{0,32},{16,48},{32,0},{48,16},{64,96},{80,112},{96,64},{112,80},{1... | collective-permute-start | bytes 1622024 | tf_op jit(solution)/shard_map/ppermute | solution.py:533
  11.3 14.4 %collective-permute-start.3 = (bf16[2,264,512]{2,1,0:T(8,128)(2,1)S(1)}, bf16[2,264,512]{2,1,0:T(8,128)(2,1)S(1)}, u32[]{:S(2)}, u32[]{:S(2)}) collective-permute-start(bf16[2,264,512]{2,1,0:T(8,128)(2,1)S(1)} %get-tuple-element.56), channel_id=1, source_target_pairs={{0,96},{16,112},{32,64},{48,80},{64,32},{80,48},{96,0},{112,16},{1... | collective-permute-start | bytes 1622024 | tf_op jit(solution)/shard_map/ppermute | solution.py:533
  13.8 19.9 %collective-permute-start.4 = (bf16[2,264,512]{2,1,0:T(8,128)(2,1)S(1)}, bf16[2,264,512]{2,1,0:T(8,128)(2,1)S(1)}, u32[]{:S(2)}, u32[]{:S(2)}) collective-permute-start(bf16[2,264,512]{2,1,0:T(8,128)(2,1)S(1)} %get-tuple-element.57), channel_id=1, source_target_pairs={{0,16},{16,0},{32,48},{48,32},{64,80},{80,64},{96,112},{112,96},{1... | collective-permute-start | bytes 1622024 | tf_op jit(solution)/shard_map/ppermute | solution.py:533
  23.0 14.3 %collective-permute-start.5 = (bf16[2,264,512]{2,1,0:T(8,128)(2,1)S(1)}, bf16[2,264,512]{2,1,0:T(8,128)(2,1)S(1)}, u32[]{:S(2)}, u32[]{:S(2)}) collective-permute-start(bf16[2,264,512]{2,1,0:T(8,128)(2,1)S(1)} %get-tuple-element.59), channel_id=1, source_target_pairs={{0,48},{16,32},{32,16},{48,0},{64,112},{80,96},{96,80},{112,64},{1... | collective-permute-start | bytes 1622024 | tf_op jit(solution)/shard_map/ppermute | solution.py:533
  25.6 15.7 %collective-permute-start.6 = (bf16[2,264,512]{2,1,0:T(8,128)(2,1)S(1)}, bf16[2,264,512]{2,1,0:T(8,128)(2,1)S(1)}, u32[]{:S(2)}, u32[]{:S(2)}) collective-permute-start(bf16[2,264,512]{2,1,0:T(8,128)(2,1)S(1)} %get-tuple-element.60), channel_id=1, source_target_pairs={{0,112},{16,96},{32,80},{48,64},{64,48},{80,32},{96,16},{112,0},{1... | collective-permute-start | bytes 1622024 | tf_op jit(solution)/shard_map/ppermute | solution.py:533
  41.3 31.0 %collective-permute-start.9 = (bf16[2,264,512]{2,1,0:T(8,128)(2,1)S(1)}, bf16[2,264,512]{2,1,0:T(8,128)(2,1)S(1)}, u32[]{:S(2)}, u32[]{:S(2)}) collective-permute-start(bf16[2,264,512]{2,1,0:T(8,128)(2,1)S(1)} %get-tuple-element.70), channel_id=1, source_target_pairs={{0,64},{16,80},{32,96},{48,112},{64,0},{80,16},{96,32},{112,48},{1... | collective-permute-start | bytes 1622024 | tf_op jit(solution)/shard_map/ppermute | solution.py:533
  42.0 30.3 %collective-permute-start.10 = (bf16[2,264,512]{2,1,0:T(8,128)(2,1)S(1)}, bf16[2,264,512]{2,1,0:T(8,128)(2,1)S(1)}, u32[]{:S(2)}, u32[]{:S(2)}) collective-permute-start(bf16[2,264,512]{2,1,0:T(8,128)(2,1)S(1)} %get-tuple-element.71), channel_id=1, source_target_pairs={{0,80},{16,64},{32,112},{48,96},{64,16},{80,0},{96,48},{112,32},{1... | collective-permute-start | bytes 1622024 | tf_op jit(solution)/shard_map/ppermute | solution.py:533
  45.1 24.8 %collective-permute-start.11 = (f32[2,16,256]{2,1,0:T(8,128)S(1)}, f32[2,16,256]{2,1,0:T(8,128)S(1)}, u32[]{:S(2)}, u32[]{:S(2)}) collective-permute-start(f32[2,16,256]{2,1,0:T(8,128)S(1)} %get-tuple-element.73), channel_id=1, source_target_pairs={{0,32},{16,48},{32,0},{48,16},{64,96},{80,112},{96,64},{112,80},{1... | collective-permute-start | bytes 98312 | tf_op jit(solution)/shard_map/ppermute | solution.py:533
  47.1 40.0 %copy-start = (f32[8,1536]{1,0:T(8,128)S(1)}, f32[8,1536]{1,0:T(8,128)}, u32[]{:S(2)}) copy-start(f32[8,1536]{1,0:T(8,128)} %r_ref.3) | copy-start | bytes 147460
  61.9 25.2 %collective-permute-start.7 = (f32[16,1536]{1,0:T(8,128)S(1)}, f32[16,1536]{1,0:T(8,128)S(1)}, u32[]{:S(2)}, u32[]{:S(2)}) collective-permute-start(f32[16,1536]{1,0:T(8,128)S(1)} %get-tuple-element.66), channel_id=1, source_target_pairs={{0,1},{1,2},{2,3},{3,4},{4,5},{5,6},{6,7},{7,8},{8,9},{9,10},{10,1... | collective-permute-start | bytes 294920 | tf_op jit(solution)/shard_map/ppermute | solution.py:530
  68.6 18.5 %collective-permute-start.8 = (f32[16,1536]{1,0:T(8,128)S(1)}, f32[16,1536]{1,0:T(8,128)S(1)}, u32[]{:S(2)}, u32[]{:S(2)}) collective-permute-start(f32[16,1536]{1,0:T(8,128)S(1)} %get-tuple-element.67), channel_id=1, source_target_pairs={{1,0},{2,1},{3,2},{4,3},{5,4},{6,5},{7,6},{8,7},{9,8},{10,9},{11,1... | collective-permute-start | bytes 294920 | tf_op jit(solution)/shard_map/ppermute | solution.py:527
  69.9 5.2 %collective-permute-start.12 = (f32[2,16,256]{2,1,0:T(8,128)S(1)}, f32[2,16,256]{2,1,0:T(8,128)S(1)}, u32[]{:S(2)}, u32[]{:S(2)}) collective-permute-start(f32[2,16,256]{2,1,0:T(8,128)S(1)} %get-tuple-element.74), channel_id=1, source_target_pairs={{0,96},{16,112},{32,64},{48,80},{64,32},{80,48},{96,0},{112,16},{1... | collective-permute-start | bytes 98312 | tf_op jit(solution)/shard_map/ppermute | solution.py:533
  72.3 5.6 %collective-permute-start.13 = (f32[2,16,256]{2,1,0:T(8,128)S(1)}, f32[2,16,256]{2,1,0:T(8,128)S(1)}, u32[]{:S(2)}, u32[]{:S(2)}) collective-permute-start(f32[2,16,256]{2,1,0:T(8,128)S(1)} %get-tuple-element.75), channel_id=1, source_target_pairs={{0,16},{16,0},{32,48},{48,32},{64,80},{80,64},{96,112},{112,96},{1... | collective-permute-start | bytes 98312 | tf_op jit(solution)/shard_map/ppermute | solution.py:533
  72.3 9.9 %collective-permute-start.14 = (f32[2,16,256]{2,1,0:T(8,128)S(1)}, f32[2,16,256]{2,1,0:T(8,128)S(1)}, u32[]{:S(2)}, u32[]{:S(2)}) collective-permute-start(f32[2,16,256]{2,1,0:T(8,128)S(1)} %get-tuple-element.76), channel_id=1, source_target_pairs={{0,48},{16,32},{32,16},{48,0},{64,112},{80,96},{96,80},{112,64},{1... | collective-permute-start | bytes 98312 | tf_op jit(solution)/shard_map/ppermute | solution.py:533
  75.1 7.2 %collective-permute-start.15 = (f32[2,16,256]{2,1,0:T(8,128)S(1)}, f32[2,16,256]{2,1,0:T(8,128)S(1)}, u32[]{:S(2)}, u32[]{:S(2)}) collective-permute-start(f32[2,16,256]{2,1,0:T(8,128)S(1)} %get-tuple-element.77), channel_id=1, source_target_pairs={{0,112},{16,96},{32,80},{48,64},{64,48},{80,32},{96,16},{112,0},{1... | collective-permute-start | bytes 98312 | tf_op jit(solution)/shard_map/ppermute | solution.py:533
  77.9 6.3 %collective-permute-start.16 = (f32[2,16,256]{2,1,0:T(8,128)S(1)}, f32[2,16,256]{2,1,0:T(8,128)S(1)}, u32[]{:S(2)}, u32[]{:S(2)}) collective-permute-start(f32[2,16,256]{2,1,0:T(8,128)S(1)} %get-tuple-element.78), channel_id=1, source_target_pairs={{0,64},{16,80},{32,96},{48,112},{64,0},{80,16},{96,32},{112,48},{1... | collective-permute-start | bytes 98312 | tf_op jit(solution)/shard_map/ppermute | solution.py:533
  82.3 4.8 %collective-permute-start.17 = (f32[2,16,256]{2,1,0:T(8,128)S(1)}, f32[2,16,256]{2,1,0:T(8,128)S(1)}, u32[]{:S(2)}, u32[]{:S(2)}) collective-permute-start(f32[2,16,256]{2,1,0:T(8,128)S(1)} %get-tuple-element.79), channel_id=1, source_target_pairs={{0,80},{16,64},{32,112},{48,96},{64,16},{80,0},{96,48},{112,32},{1... | collective-permute-start | bytes 98312 | tf_op jit(solution)/shard_map/ppermute | solution.py:533
  87.9 11.8 %collective-permute-start.19 = (f32[8,1536]{1,0:T(8,128)S(1)}, f32[8,1536]{1,0:T(8,128)S(1)}, u32[]{:S(2)}, u32[]{:S(2)}) collective-permute-start(f32[8,1536]{1,0:T(8,128)S(1)} %get-tuple-element.80.w_ref), channel_id=1, source_target_pairs={{1,0},{2,1},{3,2},{4,3},{5,4},{6,5},{7,6},{8,7},{9,8},{10,9},{11,1... | collective-permute-start | bytes 147464 | tf_op jit(solution)/shard_map/ppermute | solution.py:527
  89.2 12.2 %collective-permute-start.18 = (f32[8,1536]{1,0:T(8,128)S(1)}, f32[8,1536]{1,0:T(8,128)S(1)}, u32[]{:S(2)}, u32[]{:S(2)}) collective-permute-start(f32[8,1536]{1,0:T(8,128)S(1)} %get-tuple-element.80.w_ref), channel_id=1, source_target_pairs={{0,1},{1,2},{2,3},{3,4},{4,5},{5,6},{6,7},{7,8},{8,9},{9,10},{10,1... | collective-permute-start | bytes 147464 | tf_op jit(solution)/shard_map/ppermute | solution.py:530
  93.8 3.8 %collective-permute-start.20 = (f32[16,256]{1,0:T(8,128)S(1)}, f32[16,256]{1,0:T(8,128)S(1)}, u32[]{:S(2)}, u32[]{:S(2)}) collective-permute-start(f32[16,256]{1,0:T(8,128)S(1)} %get-tuple-element.90), channel_id=1, source_target_pairs={{0,32},{16,48},{32,0},{48,16},{64,96},{80,112},{96,64},{112,80},{1... | collective-permute-start | bytes 49160 | tf_op jit(solution)/shard_map/ppermute | solution.py:533
  93.9 5.0 %collective-permute-start.21 = (f32[16,256]{1,0:T(8,128)S(1)}, f32[16,256]{1,0:T(8,128)S(1)}, u32[]{:S(2)}, u32[]{:S(2)}) collective-permute-start(f32[16,256]{1,0:T(8,128)S(1)} %get-tuple-element.91), channel_id=1, source_target_pairs={{0,96},{16,112},{32,64},{48,80},{64,32},{80,48},{96,0},{112,16},{1... | collective-permute-start | bytes 49160 | tf_op jit(solution)/shard_map/ppermute | solution.py:533
  96.3 12.4 %collective-permute-start.22 = (f32[16,256]{1,0:T(8,128)S(1)}, f32[16,256]{1,0:T(8,128)S(1)}, u32[]{:S(2)}, u32[]{:S(2)}) collective-permute-start(f32[16,256]{1,0:T(8,128)S(1)} %get-tuple-element.92), channel_id=1, source_target_pairs={{0,16},{16,0},{32,48},{48,32},{64,80},{80,64},{96,112},{112,96},{1... | collective-permute-start | bytes 49160 | tf_op jit(solution)/shard_map/ppermute | solution.py:533
  97.6 11.1 %collective-permute-start.23 = (f32[16,256]{1,0:T(8,128)S(1)}, f32[16,256]{1,0:T(8,128)S(1)}, u32[]{:S(2)}, u32[]{:S(2)}) collective-permute-start(f32[16,256]{1,0:T(8,128)S(1)} %get-tuple-element.93), channel_id=1, source_target_pairs={{0,48},{16,32},{32,16},{48,0},{64,112},{80,96},{96,80},{112,64},{1... | collective-permute-start | bytes 49160 | tf_op jit(solution)/shard_map/ppermute | solution.py:533
  98.9 9.9 %collective-permute-start.24 = (f32[16,256]{1,0:T(8,128)S(1)}, f32[16,256]{1,0:T(8,128)S(1)}, u32[]{:S(2)}, u32[]{:S(2)}) collective-permute-start(f32[16,256]{1,0:T(8,128)S(1)} %get-tuple-element.94), channel_id=1, source_target_pairs={{0,112},{16,96},{32,80},{48,64},{64,48},{80,32},{96,16},{112,0},{1... | collective-permute-start | bytes 49160 | tf_op jit(solution)/shard_map/ppermute | solution.py:533
  99.8 9.0 %collective-permute-start.25 = (f32[16,256]{1,0:T(8,128)S(1)}, f32[16,256]{1,0:T(8,128)S(1)}, u32[]{:S(2)}, u32[]{:S(2)}) collective-permute-start(f32[16,256]{1,0:T(8,128)S(1)} %get-tuple-element.95), channel_id=1, source_target_pairs={{0,64},{16,80},{32,96},{48,112},{64,0},{80,16},{96,32},{112,48},{1... | collective-permute-start | bytes 49160 | tf_op jit(solution)/shard_map/ppermute | solution.py:533
  101.4 7.4 %collective-permute-start.26 = (f32[16,256]{1,0:T(8,128)S(1)}, f32[16,256]{1,0:T(8,128)S(1)}, u32[]{:S(2)}, u32[]{:S(2)}) collective-permute-start(f32[16,256]{1,0:T(8,128)S(1)} %get-tuple-element.96), channel_id=1, source_target_pairs={{0,80},{16,64},{32,112},{48,96},{64,16},{80,0},{96,48},{112,32},{1... | collective-permute-start | bytes 49160 | tf_op jit(solution)/shard_map/ppermute | solution.py:533
  110.2 19.5 %all-to-all-start = ((f32[8,24,256]{2,1,0:T(8,128)}), f32[8,24,256]{2,1,0:T(8,128)S(1)}, u32[]{:S(2)}, u32[]{:S(2)}) async-start(f32[8,24,256]{2,1,0:T(8,128)} %get-tuple-element.99), calls=%async_computation | async-start | bytes 393216 | tf_op jit(solution)/shard_map/all_to_all | solution.py:536
  117.0 8.2 %collective-permute-start.27 = (f32[8,1536]{1,0:T(8,128)S(1)}, f32[8,1536]{1,0:T(8,128)S(1)}, u32[]{:S(2)}, u32[]{:S(2)}) collective-permute-start(f32[8,1536]{1,0:T(8,128)S(1)} %get-tuple-element.98), channel_id=1, source_target_pairs={{0,1},{1,2},{2,3},{3,4},{4,5},{5,6},{6,7},{7,8},{8,9},{9,10},{10,1... | collective-permute-start | bytes 147464 | tf_op jit(solution)/shard_map/ppermute | solution.py:530
  123.5 6.3 %collective-permute-start.28 = (f32[8,1536]{1,0:T(8,128)S(1)}, f32[8,1536]{1,0:T(8,128)S(1)}, u32[]{:S(2)}, u32[]{:S(2)}) collective-permute-start(f32[8,1536]{1,0:T(8,128)S(1)} %get-tuple-element.89.rl_ref), channel_id=1, source_target_pairs={{1,0},{2,1},{3,2},{4,3},{5,4},{6,5},{7,6},{8,7},{9,8},{10,9},{11,1... | collective-permute-start | bytes 147464 | tf_op jit(solution)/shard_map/ppermute | solution.py:527
where the time goes:
time: 150 us
  starting transfers between devices  64.3 us (43%)
  Pallas kernels  35.7 us (24%)
  waiting for transfers between devices  30.7 us (20%)
  blocking collectives  18 us (12%)
    ppermute x21, starting transfers between devices, swap(): return lax.ppermute(x, 'group', [(i, i ^ k) for i in range(8)])  30 us
    ppermute x21, waiting for transfers between devices, swap(): return lax.ppermute(x, 'group', [(i, i ^ k) for i in range(8)])  25.7 us
    ppermute x4, starting transfers between devices, left_of(): return lax.ppermute(x, 'dev', to_right)  22.3 us
    all_to_all x1, blocking collectives, trade(): return lax.all_to_all(x, axis, split_axis=0, concat_axis=0, tiled=True)  18 us
    pallas_call x1, Pallas kernels, band_first(): pl.pallas_call(body, out_shape=(vmem_bf16(nt, 2 * n, TILE), f32(16, n), f...  14.8 us
    all_to_all x1, starting transfers between devices, trade(): return lax.all_to_all(x, axis, split_axis=0, concat_axis=0, tiled=True)  6.82 us
    pallas_call x1, Pallas kernels, local_first(): pl.pallas_call(body, out_shape=(vmem_bf16(nt, n, TILE), f32(16, n)), in_s...  6.67 us
    ppermute x4, starting transfers between devices, right_of(): return lax.ppermute(x, 'dev', to_left)  5.16 us
  transfers between devices with their start and end apart: 30, of which 11 were waited for; matrix products, arithmetic and copies ran while one was open for 0% of the time, Pallas kernels for 19%

commit v1 on v0

--- a/solution.py
+++ b/solution.py
@@ -162,7 +162,7 @@
             acc_ref[:, s] = fold_ones(mm(va[...], k_ref[t], NN))
             return carry
 
-        lax.fori_loop(0, nt, step, 0)
+        lax.fori_loop(0, nt, step, 0, unroll=2)
 
     return pl.pallas_call(
         body,
@@ -208,7 +208,7 @@
             acc[...] += mm(vb[:, s], k, NT)
             return carry
 
-        lax.fori_loop(0, nt, step, 0)
+        lax.fori_loop(0, nt, step, 0, unroll=2)
         rows = fold_ones(acc[...])
         rowl_ref[...] = rows[:, 0:n]
         rowo_ref[...] = rows[:, n:]
@@ -304,7 +304,7 @@
 
     def body(q_ref, r_ref, *refs):
         part_refs, (*x_refs, w_ref, deg_ref, sum_ref, acc) = refs[:m], refs[m:]
-        x_refs, out_refs = x_refs[:7], x_refs[7:]
+        x_refs, xw_ref = x_refs[:7], x_refs[7]
         g = lax.axis_index("group")
         total = part_refs[0][...]
         for p in part_refs[1:]:
@@ -323,10 +323,10 @@
         w = 0.5 * (deg * rv - acc[0:8, :])
         w_ref[...] = w
         deg_ref[...] = deg
-        for k, out in zip(SWAPS, out_refs):
+        for h in range(8):
             for c in range(2):
-                t = jnp.maximum(q_ref[(g ^ k) * 2 + c], 0)
-                out[c * 8 : c * 8 + 8, :] = w_ref[:, span(t)]
+                t = jnp.maximum(q_ref[h * 2 + c], 0)
+                xw_ref[h, c * 8 : c * 8 + 8, :] = w_ref[:, span(t)]
         lane = lax.broadcasted_iota(jnp.int32, (8, 128), 1)
         sums = jnp.zeros((8, 128), F32)
         for k, v in enumerate((rv * rv, rv * w, w * w, 0.5 * deg * w * w)):
@@ -335,19 +335,19 @@
 
     return pl.pallas_call(
         body,
-        out_shape=[f32(16, TILE)] * 7 + [f32(8, n), f32(8, n), f32(8, 128)],
+        out_shape=[f32(8, 16, TILE), f32(8, n), f32(8, n), f32(8, 128)],
         in_specs=[SMEM] + [VM] * (m + 8),
-        out_specs=[VM] * 10,
+        out_specs=[VM] * 4,
         scratch_shapes=[pltpu.VMEM((16, n), F32)],
         compiler_params=params(),
         name="combine",
     )(table, r, *parts, *ret)
 
 
-def local_second(k_local, w):
+def local_second(k_local, w, after):
     nt, n, _ = k_local.shape
 
-    def body(k_ref, w_ref, out_ref):
+    def body(k_ref, w_ref, _, out_ref):
         va = split(w_ref[...])
         for t in range(nt):
             out_ref[:, t * TILE : (t + 1) * TILE] = fold(mm(va, k_ref[t], NN))
@@ -355,11 +355,11 @@
     return pl.pallas_call(
         body,
         out_shape=f32(8, n),
-        in_specs=[VM, VM],
+        in_specs=[VM, VM, ANY],
         out_specs=VM,
         compiler_params=params(),
         name="local_second",
-    )(k_local, w)
+    )(k_local, w, after)
 
 
 def band_second(k_band, w_left, w, w_right, after):
@@ -396,10 +396,8 @@
     def body(
         q_ref, ka_ref, kb_ref, kc_ref, w_ref, sum_ref, loc_ref, rl_ref, ro_ref, wl_ref, *refs
     ):
-        xw_refs, (col_ref, row_ref, va, acc, jobs, xw_ref) = refs[:7], refs[7:]
+        xw_ref, col_ref, row_ref, va, acc, jobs = refs
         g = lax.axis_index("group")
-        for k, x in zip(SWAPS, xw_refs):
-            xw_ref[g ^ k] = x[...]
         va[...] = split(w_ref[...])
         acc[...] = jnp.zeros_like(acc)
         for ks, k_ref in zip(STAGES, (ka_ref, kb_ref, kc_ref)):
@@ -436,17 +434,16 @@
     return pl.pallas_call(
         body,
         out_shape=(f32(8, 24, TILE), f32(8, n)),
-        in_specs=[SMEM] + [VM] * 16,
+        in_specs=[SMEM] + [VM] * 10,
         out_specs=(VM, VM),
         scratch_shapes=[
             pltpu.VMEM((16, n), BF16),
             pltpu.VMEM((16, n), F32),
             pltpu.SMEM((16,), jnp.int32),
-            pltpu.VMEM((8, 16, TILE), F32),
         ],
         compiler_params=params(),
         name="cross_second",
-    )(table, *k_caches, w, sums, loc, row_left, row_own, w_left, *xw)
+    )(table, *k_caches, w, sums, loc, row_left, row_own, w_left, xw)
 
 
 def group_sum(table, w, deg, parts, ret):
@@ -557,12 +554,13 @@
     from_left, from_right = left_of(to_r), right_of(to_l)
     k_c, row_c, *col_c = cross(STAGES[2], acc_band)
     ret = ret_near[2:] + ret_near[:2] + [swap(x, k) for x, k in zip(col_c, STAGES[2])]
-    *xw_out, w, deg, sums = combine(
+    xw_out, w, deg, sums = combine(
         table, targets, (acc_local, acc_band, from_left, from_right, row_a, row_b, row_c), ret
     )
-    w_left, w_right = left_of(w), right_of(w)
-    xw = [swap(x, k) for x, k in zip(xw_out, SWAPS)]
-    loc2 = local_second(k_local, w)
+    w_left = left_of(w)
+    w_right = right_of(w)
+    xw = trade(xw_out)
+    loc2 = local_second(k_local, w, xw)
     col_r, rowl_b, rowo_b = band_second(k_band, w_left, w, w_right, loc2)
     from_left2 = left_of(col_r)
     from_right2 = right_of(rowl_b)

time: 150 us -> 162 us (1.080)
  local copies, waits for them, and re-layouts: 0.01 us -> 17.7 us
  waiting for transfers between devices: 30.7 us -> 25.8 us
    unnamed x2 -> x24, local copies, waits for them, and re-layouts: 0.01 us -> 17.7 us
    ppermute x21 -> x14, waiting for transfers between devices: 25.7 us -> 19.8 us  [swap(): return lax.ppermute(x, 'group', [(i, i ^ k) for i in range(8)])]
    all_to_all x1 -> x2, starting transfers between devices: 6.82 us -> 12.4 us  [trade(): return lax.all_to_all(x, axis, split_axis=0, concat_axis=0, tiled=True)]
    ppermute x21 -> x14, starting transfers between devices: 30 us -> 25.3 us  [swap(): return lax.ppermute(x, 'group', [(i, i ^ k) for i in range(8)])]
  transfers between devices with their start and end apart: 30 -> 24, of which waited for: 11 -> 8; matrix products, arithmetic and copies ran while one was open for 0% -> 0% of each run, Pallas kernels for 19% -> 14%
where the time goes in v1:
time: 162 us; the launch traced here: 161 us
  starting transfers between devices  64 us (40%)
  Pallas kernels  34.2 us (21%)
  waiting for transfers between devices  25.8 us (16%)
  blocking collectives  18.6 us (11%)
  local copies, waits for them, and re-layouts  17.7 us (11%)
    ppermute x14, starting transfers between devices, swap(): return lax.ppermute(x, 'group', [(i, i ^ k) for i in range(8)])  25.3 us
    ppermute x4, starting transfers between devices, left_of(): return lax.ppermute(x, 'dev', to_right)  21.2 us
    ppermute x14, waiting for transfers between devices, swap(): return lax.ppermute(x, 'group', [(i, i ^ k) for i in range(8)])  19.8 us
    all_to_all x1, blocking collectives, trade(): return lax.all_to_all(x, axis, split_axis=0, concat_axis=0, tiled=True)  18.6 us
    unnamed x24, local copies, waits for them, and re-layouts  17.7 us
    pallas_call x1, Pallas kernels, band_first(): pl.pallas_call(body, out_shape=(vmem_bf16(nt, 2 * n, TILE), f32(16, n), f...  13.6 us
    all_to_all x2, starting transfers between devices, trade(): return lax.all_to_all(x, axis, split_axis=0, concat_axis=0, tiled=True)  12.4 us
    pallas_call x1, Pallas kernels, local_first(): pl.pallas_call(body, out_shape=(vmem_bf16(nt, n, TILE), f32(16, n)), in_s...  5.81 us
  transfers between devices with their start and end apart: 24, of which 8 were waited for; matrix products, arithmetic and copies ran while one was open for 0% of the time, Pallas kernels for 14%

profile of v1, /device:TPU:0, one launch (start us, length us, event | category | flops | bytes accessed | tf_op | source)
XLA Modules:
  0.0 161.2 jit_solution(12268692055351467072)
XLA Ops:
  0.6 2.6 %prep.1 = (s32[32]{0:T(128)S(1)}, bf16[6,264,512]{2,1,0:T(8,128)(2,1)S(1)}, bf16[2,264,512]{2,1,0:T(8,128)(2,1)S(1)}, bf16[2,264,512]{2,1,0:T(8,128)(2,1)S(1)}, ...) custom-call(s32[8,8,2,16]{3,2,1,0:T(2,128)} %bitcast.3, ...), custom_call_target="tpu_custom_call" | custom-call | tf_op jit(solution)/shard_map/prep/pallas_call | solution.py:111
  3.2 1.3 collective-permute-start.1
  4.5 4.6 %collective-permute-start = (bf16[6,264,512]{2,1,0:T(8,128)(2,1)S(1)}, bf16[6,264,512]{2,1,0:T(8,128)(2,1)S(1)}, u32[]{:S(2)}, u32[]{:S(2)}) collective-permute-start(bf16[6,264,512]{2,1,0:T(8,128)(2,1)S(1)} %get-tuple-element.47.a_ref), channel_id=1, source_target_pairs={{0,1},{1,2},{2,3},{3,4},{4,5},{5,6},{6,7},{7,8},{8,9},{9,10},{10,1... | collective-permute-start | bytes 4866056 | tf_op jit(solution)/shard_map/ppermute | solution.py:527
  9.1 2.1 %collective-permute-start.2 = (bf16[2,264,512]{2,1,0:T(8,128)(2,1)S(1)}, bf16[2,264,512]{2,1,0:T(8,128)(2,1)S(1)}, u32[]{:S(2)}, u32[]{:S(2)}) collective-permute-start(bf16[2,264,512]{2,1,0:T(8,128)(2,1)S(1)} %get-tuple-element.49), channel_id=1, source_target_pairs={{0,32},{16,48},{32,0},{48,16},{64,96},{80,112},{96,64},{112,80},{1... | collective-permute-start | bytes 1622024 | tf_op jit(solution)/shard_map/ppermute | solution.py:530
  11.3 2.5 %collective-permute-start.3 = (bf16[2,264,512]{2,1,0:T(8,128)(2,1)S(1)}, bf16[2,264,512]{2,1,0:T(8,128)(2,1)S(1)}, u32[]{:S(2)}, u32[]{:S(2)}) collective-permute-start(bf16[2,264,512]{2,1,0:T(8,128)(2,1)S(1)} %get-tuple-element.50), channel_id=1, source_target_pairs={{0,96},{16,112},{32,64},{48,80},{64,32},{80,48},{96,0},{112,16},{1... | collective-permute-start | bytes 1622024 | tf_op jit(solution)/shard_map/ppermute | solution.py:530
  13.8 9.2 %collective-permute-done.2.refs_0_ = bf16[2,264,512]{2,1,0:T(8,128)(2,1)S(1)} collective-permute-done((bf16[2,264,512]{2,1,0:T(8,128)(2,1)S(1)}, bf16[2,264,512]{2,1,0:T(8,128)(2,1)S(1)}, u32[]{:S(2)}, u32[]{:S(2)}) %collective-permute-start.2) | collective-permute-done | bytes 540704 | tf_op jit(solution)/shard_map/ppermute | solution.py:530
  23.0 2.7 %collective-permute-done.3.refs_1_ = bf16[2,264,512]{2,1,0:T(8,128)(2,1)S(1)} collective-permute-done((bf16[2,264,512]{2,1,0:T(8,128)(2,1)S(1)}, bf16[2,264,512]{2,1,0:T(8,128)(2,1)S(1)}, u32[]{:S(2)}, u32[]{:S(2)}) %collective-permute-start.3) | collective-permute-done | bytes 540704 | tf_op jit(solution)/shard_map/ppermute | solution.py:530
  25.6 1.3 collective-permute-start.6
  27.0 5.8 %local_first.1 = (bf16[6,1536,256]{2,1,0:T(8,128)(2,1)S(1)}, f32[16,1536]{1,0:T(8,128)S(1)}) custom-call(bf16[6,264,512]{2,1,0:T(8,128)(2,1)S(1)} %get-tuple-element.47.a_ref), custom_call_target="tpu_custom_call" | custom-call | tf_op jit(solution)/shard_map/local_first/pallas_call | solution.py:167
  32.8 2.2 %copy-done.3 = bf16[6,1536,256]{2,1,0:T(8,128)(2,1)} copy-done((bf16[6,1536,256]{2,1,0:T(8,128)(2,1)}, bf16[6,1536,256]{2,1,0:T(8,128)(2,1)S(1)}, u32[]{:S(2)}) %copy-start.3) | copy-done | bytes 4718616
  34.9 1.0 shard_map.50
  36.0 2.2 %copy-done.2 = bf16[6,1536,256]{2,1,0:T(8,128)(2,1)} copy-done((bf16[6,1536,256]{2,1,0:T(8,128)(2,1)}, bf16[6,1536,256]{2,1,0:T(8,128)(2,1)S(1)}, u32[]{:S(2)}) %copy-start.2) | copy-done | bytes 4718616
  38.2 3.1 %collective-permute-done.6.refs_1_.refs_4_ = bf16[2,264,512]{2,1,0:T(8,128)(2,1)S(1)} collective-permute-done((bf16[2,264,512]{2,1,0:T(8,128)(2,1)S(1)}, bf16[2,264,512]{2,1,0:T(8,128)(2,1)S(1)}, u32[]{:S(2)}, u32[]{:S(2)}) %collective-permute-start.6) | collective-permute-done | bytes 540704 | tf_op jit(solution)/shard_map/ppermute | solution.py:530
  41.3 0.7 collective-permute-start.9
  42.0 5.2 %collective-permute-start.10 = (bf16[2,264,512]{2,1,0:T(8,128)(2,1)S(1)}, bf16[2,264,512]{2,1,0:T(8,128)(2,1)S(1)}, u32[]{:S(2)}, u32[]{:S(2)}) collective-permute-start(bf16[2,264,512]{2,1,0:T(8,128)(2,1)S(1)} %get-tuple-element.65), channel_id=1, source_target_pairs={{0,80},{16,64},{32,112},{48,96},{64,16},{80,0},{96,48},{112,32},{1... | collective-permute-start | bytes 1622024 | tf_op jit(solution)/shard_map/ppermute | solution.py:530
  47.3 1.0 shard_map.51
  48.3 1.7 %copy-done.5 = bf16[4,1536,256]{2,1,0:T(8,128)(2,1)} copy-done((bf16[4,1536,256]{2,1,0:T(8,128)(2,1)}, bf16[4,1536,256]{2,1,0:T(8,128)(2,1)S(1)}, u32[]{:S(2)}) %copy-start.5) | copy-done | bytes 3145752
  50.0 2.2 %collective-permute-start.11 = (f32[2,16,256]{2,1,0:T(8,128)S(1)}, f32[2,16,256]{2,1,0:T(8,128)S(1)}, u32[]{:S(2)}, u32[]{:S(2)}) collective-permute-start(f32[2,16,256]{2,1,0:T(8,128)S(1)} %get-tuple-element.67), channel_id=1, source_target_pairs={{0,32},{16,48},{32,0},{48,16},{64,96},{80,112},{96,64},{112,80},{1... | collective-permute-start | bytes 98312 | tf_op jit(solution)/shard_map/ppermute | solution.py:530
  52.2 13.6 %band_first.1 = (bf16[6,3072,256]{2,1,0:T(8,128)(2,1)S(1)}, f32[16,1536]{1,0:T(8,128)S(1)}, f32[16,1536]{1,0:T(8,128)S(1)}, f32[16,1536]{1,0:T(8,128)S(1)}) custom-call(bf16[6,264,512]{2,1,0:T(8,128)(2,1)S(1)} %collective-permute-done.l_ref, bf16[6,264,512]{2,1,0:T(8,128)(2,1)S(1)} %get-tuple-element.47.a_ref, ...), custom_call_target="tpu_custom_call" | custom-call | tf_op jit(solution)/shard_map/band_first/pallas_call | solution.py:216
  65.9 3.7 %copy-done = bf16[6,3072,256]{2,1,0:T(8,128)(2,1)} copy-done((bf16[6,3072,256]{2,1,0:T(8,128)(2,1)}, bf16[6,3072,256]{2,1,0:T(8,128)(2,1)S(1)}, u32[]{:S(2)}) %copy-start) | copy-done | bytes 9437208
  69.5 6.7 %collective-permute-start.7 = (f32[16,1536]{1,0:T(8,128)S(1)}, f32[16,1536]{1,0:T(8,128)S(1)}, u32[]{:S(2)}, u32[]{:S(2)}) collective-permute-start(f32[16,1536]{1,0:T(8,128)S(1)} %get-tuple-element.60), channel_id=1, source_target_pairs={{0,1},{1,2},{2,3},{3,4},{4,5},{5,6},{6,7},{7,8},{8,9},{9,10},{10,1... | collective-permute-start | bytes 294920 | tf_op jit(solution)/shard_map/ppermute | solution.py:527
  76.3 1.3 collective-permute-start.8
  77.6 2.4 %collective-permute-start.12 = (f32[2,16,256]{2,1,0:T(8,128)S(1)}, f32[2,16,256]{2,1,0:T(8,128)S(1)}, u32[]{:S(2)}, u32[]{:S(2)}) collective-permute-start(f32[2,16,256]{2,1,0:T(8,128)S(1)} %get-tuple-element.68), channel_id=1, source_target_pairs={{0,96},{16,112},{32,64},{48,80},{64,32},{80,48},{96,0},{112,16},{1... | collective-permute-start | bytes 98312 | tf_op jit(solution)/shard_map/ppermute | solution.py:530
  80.0 1.5 collective-permute-start.14
  81.5 1.0 shard_map.52
  82.5 1.7 %copy-done.7 = bf16[4,1536,256]{2,1,0:T(8,128)(2,1)} copy-done((bf16[4,1536,256]{2,1,0:T(8,128)(2,1)}, bf16[4,1536,256]{2,1,0:T(8,128)(2,1)S(1)}, u32[]{:S(2)}) %copy-start.7) | copy-done | bytes 3145752
  84.2 2.8 %collective-permute-start.15 = (f32[2,16,256]{2,1,0:T(8,128)S(1)}, f32[2,16,256]{2,1,0:T(8,128)S(1)}, u32[]{:S(2)}, u32[]{:S(2)}) collective-permute-start(f32[2,16,256]{2,1,0:T(8,128)S(1)} %get-tuple-element.71), channel_id=1, source_target_pairs={{0,112},{16,96},{32,80},{48,64},{64,48},{80,32},{96,16},{112,0},{1... | collective-permute-start | bytes 98312 | tf_op jit(solution)/shard_map/ppermute | solution.py:530
  87.1 4.4 %collective-permute-start.16 = (f32[2,16,256]{2,1,0:T(8,128)S(1)}, f32[2,16,256]{2,1,0:T(8,128)S(1)}, u32[]{:S(2)}, u32[]{:S(2)}) collective-permute-start(f32[2,16,256]{2,1,0:T(8,128)S(1)} %get-tuple-element.72), channel_id=1, source_target_pairs={{0,64},{16,80},{32,96},{48,112},{64,0},{80,16},{96,32},{112,48},{1... | collective-permute-start | bytes 98312 | tf_op jit(solution)/shard_map/ppermute | solution.py:530
  91.5 1.9 %collective-permute-done.16.refs_12_ = f32[2,16,256]{2,1,0:T(8,128)S(1)} collective-permute-done((f32[2,16,256]{2,1,0:T(8,128)S(1)}, f32[2,16,256]{2,1,0:T(8,128)S(1)}, u32[]{:S(2)}, u32[]{:S(2)}) %collective-permute-start.16) | collective-permute-done | bytes 32800 | tf_op jit(solution)/shard_map/ppermute | solution.py:530
  93.3 3.0 %collective-permute-done.17.refs_13_ = f32[2,16,256]{2,1,0:T(8,128)S(1)} collective-permute-done((f32[2,16,256]{2,1,0:T(8,128)S(1)}, f32[2,16,256]{2,1,0:T(8,128)S(1)}, u32[]{:S(2)}, u32[]{:S(2)}) %collective-permute-start.17) | collective-permute-done | bytes 32800 | tf_op jit(solution)/shard_map/ppermute | solution.py:530
  96.3 1.4 combine.1
  97.7 3.4 %all-to-all-start = ((f32[8,16,256]{2,1,0:T(8,128)}), f32[8,16,256]{2,1,0:T(8,128)S(1)}, u32[]{:S(2)}, u32[]{:S(2)}) async-start(f32[8,16,256]{2,1,0:T(8,128)} %get-tuple-element.77), calls=%async_computation | async-start | bytes 262144 | tf_op jit(solution)/shard_map/all_to_all | solution.py:533
  101.1 1.3 collective-permute-start.19
  102.4 4.5 %collective-permute-start.18 = (f32[8,1536]{1,0:T(8,128)S(1)}, f32[8,1536]{1,0:T(8,128)S(1)}, u32[]{:S(2)}, u32[]{:S(2)}) collective-permute-start(f32[8,1536]{1,0:T(8,128)S(1)} %get-tuple-element.74.w_ref), channel_id=1, source_target_pairs={{0,1},{1,2},{2,3},{3,4},{4,5},{5,6},{6,7},{7,8},{8,9},{9,10},{10,1... | collective-permute-start | bytes 147464 | tf_op jit(solution)/shard_map/ppermute | solution.py:527
  107.0 0.2 all-to-all-done._.refs_0_
  107.1 2.3 %copy-done.4 = bf16[6,1536,256]{2,1,0:T(8,128)(2,1)S(1)} copy-done((bf16[6,1536,256]{2,1,0:T(8,128)(2,1)S(1)}, bf16[6,1536,256]{2,1,0:T(8,128)(2,1)}, u32[]{:S(2)}) %copy-start.4) | copy-done | bytes 4718616
  109.5 0.7 local_second.1._.loc_ref.refs_0_
  110.2 3.9 %copy-done.1 = bf16[6,3072,256]{2,1,0:T(8,128)(2,1)S(1)} copy-done((bf16[6,3072,256]{2,1,0:T(8,128)(2,1)S(1)}, bf16[6,3072,256]{2,1,0:T(8,128)(2,1)}, u32[]{:S(2)}) %copy-start.1) | copy-done | bytes 9437208
  114.1 3.8 %band_second.1 = (f32[8,1536]{1,0:T(8,128)S(1)}, f32[8,1536]{1,0:T(8,128)S(1)}, f32[8,1536]{1,0:T(8,128)S(1)}) custom-call(bf16[6,3072,256]{2,1,0:T(8,128)(2,1)S(1)} %copy-done.1, f32[8,1536]{1,0:T(8,128)S(1)} %collective-permute-done.18.wl_ref, f32[8,1536]{1,0:T(8,128)S(1)} %get-tuple-element.74.w_ref, f32[8,1536]{1,0:T(8,128)S(1)} %collective-permute-done.19.wb_ref, ...), custom_call_target="tpu_custom_call" | custom-call | tf_op jit(solution)/shard_map/band_second/pallas_call | solution.py:382
  117.9 1.4 cross_second.1
  119.3 9.0 %all-to-all-start.1 = ((f32[8,24,256]{2,1,0:T(8,128)}), f32[8,24,256]{2,1,0:T(8,128)S(1)}, u32[]{:S(2)}, u32[]{:S(2)}) async-start(f32[8,24,256]{2,1,0:T(8,128)} %get-tuple-element.87), calls=%async_computation.1 | async-start | bytes 393216 | tf_op jit(solution)/shard_map/all_to_all | solution.py:533
  128.3 5.3 %collective-permute-start.20 = (f32[8,1536]{1,0:T(8,128)S(1)}, f32[8,1536]{1,0:T(8,128)S(1)}, u32[]{:S(2)}, u32[]{:S(2)}) collective-permute-start(f32[8,1536]{1,0:T(8,128)S(1)} %get-tuple-element.86), channel_id=1, source_target_pairs={{0,1},{1,2},{2,3},{3,4},{4,5},{5,6},{6,7},{7,8},{8,9},{9,10},{10,1... | collective-permute-start | bytes 147464 | tf_op jit(solution)/shard_map/ppermute | solution.py:527
  133.6 1.3 collective-permute-start.21
  134.9 0.4 collective-permute-done.20.refs_3_
  135.4 5.4 %collective-permute-done.21.refs_4_ = f32[8,1536]{1,0:T(8,128)S(1)} collective-permute-done((f32[8,1536]{1,0:T(8,128)S(1)}, f32[8,1536]{1,0:T(8,128)S(1)}, u32[]{:S(2)}, u32[]{:S(2)}) %collective-permute-start.21) | collective-permute-done | bytes 49184 | tf_op jit(solution)/shard_map/ppermute | solution.py:524
  140.8 0.7 group_sum.1
  141.5 18.6 %all_to_all.15.g_ref = f32[16,8,128]{2,1,0:T(8,128)S(1)} all-to-all(f32[16,8,128]{2,1,0:T(8,128)S(1)} %get-tuple-element.88), channel_id=1, replica_groups=mesh['group'=8,'dev'=16] {'dev'}, dimensions={0} | all-to-all | bytes 131072 | tf_op jit(solution)/shard_map/all_to_all | solution.py:533
  160.1 1.1 finish.1
  (39 shorter events, 0.1 us)
Async XLA Ops:
  3.2 49.0 %collective-permute-start.1 = (bf16[6,264,512]{2,1,0:T(8,128)(2,1)S(1)}, bf16[6,264,512]{2,1,0:T(8,128)(2,1)S(1)}, u32[]{:S(2)}, u32[]{:S(2)}) collective-permute-start(bf16[6,264,512]{2,1,0:T(8,128)(2,1)S(1)} %get-tuple-element.47.a_ref), channel_id=1, source_target_pairs={{1,0},{2,1},{3,2},{4,3},{5,4},{6,5},{7,6},{8,7},{9,8},{10,9},{11,1... | collective-permute-start | bytes 4866056 | tf_op jit(solution)/shard_map/ppermute | solution.py:524
  4.5 47.7 %collective-permute-start = (bf16[6,264,512]{2,1,0:T(8,128)(2,1)S(1)}, bf16[6,264,512]{2,1,0:T(8,128)(2,1)S(1)}, u32[]{:S(2)}, u32[]{:S(2)}) collective-permute-start(bf16[6,264,512]{2,1,0:T(8,128)(2,1)S(1)} %get-tuple-element.47.a_ref), channel_id=1, source_target_pairs={{0,1},{1,2},{2,3},{3,4},{4,5},{5,6},{6,7},{7,8},{8,9},{9,10},{10,1... | collective-permute-start | bytes 4866056 | tf_op jit(solution)/shard_map/ppermute | solution.py:527
  9.1 13.8 %collective-permute-start.2 = (bf16[2,264,512]{2,1,0:T(8,128)(2,1)S(1)}, bf16[2,264,512]{2,1,0:T(8,128)(2,1)S(1)}, u32[]{:S(2)}, u32[]{:S(2)}) collective-permute-start(bf16[2,264,512]{2,1,0:T(8,128)(2,1)S(1)} %get-tuple-element.49), channel_id=1, source_target_pairs={{0,32},{16,48},{32,0},{48,16},{64,96},{80,112},{96,64},{112,80},{1... | collective-permute-start | bytes 1622024 | tf_op jit(solution)/shard_map/ppermute | solution.py:530
  11.3 14.4 %collective-permute-start.3 = (bf16[2,264,512]{2,1,0:T(8,128)(2,1)S(1)}, bf16[2,264,512]{2,1,0:T(8,128)(2,1)S(1)}, u32[]{:S(2)}, u32[]{:S(2)}) collective-permute-start(bf16[2,264,512]{2,1,0:T(8,128)(2,1)S(1)} %get-tuple-element.50), channel_id=1, source_target_pairs={{0,96},{16,112},{32,64},{48,80},{64,32},{80,48},{96,0},{112,16},{1... | collective-permute-start | bytes 1622024 | tf_op jit(solution)/shard_map/ppermute | solution.py:530
  13.8 21.2 %collective-permute-start.4 = (bf16[2,264,512]{2,1,0:T(8,128)(2,1)S(1)}, bf16[2,264,512]{2,1,0:T(8,128)(2,1)S(1)}, u32[]{:S(2)}, u32[]{:S(2)}) collective-permute-start(bf16[2,264,512]{2,1,0:T(8,128)(2,1)S(1)} %get-tuple-element.51), channel_id=1, source_target_pairs={{0,16},{16,0},{32,48},{48,32},{64,80},{80,64},{96,112},{112,96},{1... | collective-permute-start | bytes 1622024 | tf_op jit(solution)/shard_map/ppermute | solution.py:530
  23.0 15.3 %collective-permute-start.5 = (bf16[2,264,512]{2,1,0:T(8,128)(2,1)S(1)}, bf16[2,264,512]{2,1,0:T(8,128)(2,1)S(1)}, u32[]{:S(2)}, u32[]{:S(2)}) collective-permute-start(bf16[2,264,512]{2,1,0:T(8,128)(2,1)S(1)} %get-tuple-element.53), channel_id=1, source_target_pairs={{0,48},{16,32},{32,16},{48,0},{64,112},{80,96},{96,80},{112,64},{1... | collective-permute-start | bytes 1622024 | tf_op jit(solution)/shard_map/ppermute | solution.py:530
  25.6 15.7 %collective-permute-start.6 = (bf16[2,264,512]{2,1,0:T(8,128)(2,1)S(1)}, bf16[2,264,512]{2,1,0:T(8,128)(2,1)S(1)}, u32[]{:S(2)}, u32[]{:S(2)}) collective-permute-start(bf16[2,264,512]{2,1,0:T(8,128)(2,1)S(1)} %get-tuple-element.54), channel_id=1, source_target_pairs={{0,112},{16,96},{32,80},{48,64},{64,48},{80,32},{96,16},{112,0},{1... | collective-permute-start | bytes 1622024 | tf_op jit(solution)/shard_map/ppermute | solution.py:530
  32.8 2.2 %copy-start.3 = (bf16[6,1536,256]{2,1,0:T(8,128)(2,1)}, bf16[6,1536,256]{2,1,0:T(8,128)(2,1)S(1)}, u32[]{:S(2)}) copy-start(bf16[6,1536,256]{2,1,0:T(8,128)(2,1)S(1)} %get-tuple-element.76.k_ref) | copy-start | bytes 14155780
  36.0 2.2 %copy-start.2 = (bf16[6,1536,256]{2,1,0:T(8,128)(2,1)}, bf16[6,1536,256]{2,1,0:T(8,128)(2,1)S(1)}, u32[]{:S(2)}) copy-start(bf16[6,1536,256]{2,1,0:T(8,128)(2,1)S(1)} %get-tuple-element.80.ka_ref) | copy-start | bytes 14155780
  41.3 38.7 %collective-permute-start.9 = (bf16[2,264,512]{2,1,0:T(8,128)(2,1)S(1)}, bf16[2,264,512]{2,1,0:T(8,128)(2,1)S(1)}, u32[]{:S(2)}, u32[]{:S(2)}) collective-permute-start(bf16[2,264,512]{2,1,0:T(8,128)(2,1)S(1)} %get-tuple-element.64), channel_id=1, source_target_pairs={{0,64},{16,80},{32,96},{48,112},{64,0},{80,16},{96,32},{112,48},{1... | collective-permute-start | bytes 1622024 | tf_op jit(solution)/shard_map/ppermute | solution.py:530
  42.0 38.0 %collective-permute-start.10 = (bf16[2,264,512]{2,1,0:T(8,128)(2,1)S(1)}, bf16[2,264,512]{2,1,0:T(8,128)(2,1)S(1)}, u32[]{:S(2)}, u32[]{:S(2)}) collective-permute-start(bf16[2,264,512]{2,1,0:T(8,128)(2,1)S(1)} %get-tuple-element.65), channel_id=1, source_target_pairs={{0,80},{16,64},{32,112},{48,96},{64,16},{80,0},{96,48},{112,32},{1... | collective-permute-start | bytes 1622024 | tf_op jit(solution)/shard_map/ppermute | solution.py:530
  48.3 1.7 %copy-start.5 = (bf16[4,1536,256]{2,1,0:T(8,128)(2,1)}, bf16[4,1536,256]{2,1,0:T(8,128)(2,1)S(1)}, u32[]{:S(2)}) copy-start(bf16[4,1536,256]{2,1,0:T(8,128)(2,1)S(1)} %get-tuple-element.81.kb_ref) | copy-start | bytes 9437188
  50.0 27.6 %collective-permute-start.11 = (f32[2,16,256]{2,1,0:T(8,128)S(1)}, f32[2,16,256]{2,1,0:T(8,128)S(1)}, u32[]{:S(2)}, u32[]{:S(2)}) collective-permute-start(f32[2,16,256]{2,1,0:T(8,128)S(1)} %get-tuple-element.67), channel_id=1, source_target_pairs={{0,32},{16,48},{32,0},{48,16},{64,96},{80,112},{96,64},{112,80},{1... | collective-permute-start | bytes 98312 | tf_op jit(solution)/shard_map/ppermute | solution.py:530
  52.2 44.1 %copy-start.9 = (f32[8,1536]{1,0:T(8,128)S(1)}, f32[8,1536]{1,0:T(8,128)}, u32[]{:S(2)}) copy-start(f32[8,1536]{1,0:T(8,128)} %r_ref.3) | copy-start | bytes 147460
  65.9 3.7 %copy-start = (bf16[6,3072,256]{2,1,0:T(8,128)(2,1)}, bf16[6,3072,256]{2,1,0:T(8,128)(2,1)S(1)}, u32[]{:S(2)}) copy-start(bf16[6,3072,256]{2,1,0:T(8,128)(2,1)S(1)} %get-tuple-element.78.k_ref) | copy-start | bytes 28311556
  69.5 26.8 %collective-permute-start.7 = (f32[16,1536]{1,0:T(8,128)S(1)}, f32[16,1536]{1,0:T(8,128)S(1)}, u32[]{:S(2)}, u32[]{:S(2)}) collective-permute-start(f32[16,1536]{1,0:T(8,128)S(1)} %get-tuple-element.60), channel_id=1, source_target_pairs={{0,1},{1,2},{2,3},{3,4},{4,5},{5,6},{6,7},{7,8},{8,9},{9,10},{10,1... | collective-permute-start | bytes 294920 | tf_op jit(solution)/shard_map/ppermute | solution.py:527
  76.3 20.0 %collective-permute-start.8 = (f32[16,1536]{1,0:T(8,128)S(1)}, f32[16,1536]{1,0:T(8,128)S(1)}, u32[]{:S(2)}, u32[]{:S(2)}) collective-permute-start(f32[16,1536]{1,0:T(8,128)S(1)} %get-tuple-element.61), channel_id=1, source_target_pairs={{1,0},{2,1},{3,2},{4,3},{5,4},{6,5},{7,6},{8,7},{9,8},{10,9},{11,1... | collective-permute-start | bytes 294920 | tf_op jit(solution)/shard_map/ppermute | solution.py:524
  77.6 6.6 %collective-permute-start.12 = (f32[2,16,256]{2,1,0:T(8,128)S(1)}, f32[2,16,256]{2,1,0:T(8,128)S(1)}, u32[]{:S(2)}, u32[]{:S(2)}) collective-permute-start(f32[2,16,256]{2,1,0:T(8,128)S(1)} %get-tuple-element.68), channel_id=1, source_target_pairs={{0,96},{16,112},{32,64},{48,80},{64,32},{80,48},{96,0},{112,16},{1... | collective-permute-start | bytes 98312 | tf_op jit(solution)/shard_map/ppermute | solution.py:530
  80.0 7.1 %collective-permute-start.13 = (f32[2,16,256]{2,1,0:T(8,128)S(1)}, f32[2,16,256]{2,1,0:T(8,128)S(1)}, u32[]{:S(2)}, u32[]{:S(2)}) collective-permute-start(f32[2,16,256]{2,1,0:T(8,128)S(1)} %get-tuple-element.69), channel_id=1, source_target_pairs={{0,16},{16,0},{32,48},{48,32},{64,80},{80,64},{96,112},{112,96},{1... | collective-permute-start | bytes 98312 | tf_op jit(solution)/shard_map/ppermute | solution.py:530
  80.0 11.5 %collective-permute-start.14 = (f32[2,16,256]{2,1,0:T(8,128)S(1)}, f32[2,16,256]{2,1,0:T(8,128)S(1)}, u32[]{:S(2)}, u32[]{:S(2)}) collective-permute-start(f32[2,16,256]{2,1,0:T(8,128)S(1)} %get-tuple-element.70), channel_id=1, source_target_pairs={{0,48},{16,32},{32,16},{48,0},{64,112},{80,96},{96,80},{112,64},{1... | collective-permute-start | bytes 98312 | tf_op jit(solution)/shard_map/ppermute | solution.py:530
  82.5 1.7 %copy-start.7 = (bf16[4,1536,256]{2,1,0:T(8,128)(2,1)}, bf16[4,1536,256]{2,1,0:T(8,128)(2,1)S(1)}, u32[]{:S(2)}) copy-start(bf16[4,1536,256]{2,1,0:T(8,128)(2,1)S(1)} %get-tuple-element.82.kc_ref) | copy-start | bytes 9437188
  84.2 7.2 %collective-permute-start.15 = (f32[2,16,256]{2,1,0:T(8,128)S(1)}, f32[2,16,256]{2,1,0:T(8,128)S(1)}, u32[]{:S(2)}, u32[]{:S(2)}) collective-permute-start(f32[2,16,256]{2,1,0:T(8,128)S(1)} %get-tuple-element.71), channel_id=1, source_target_pairs={{0,112},{16,96},{32,80},{48,64},{64,48},{80,32},{96,16},{112,0},{1... | collective-permute-start | bytes 98312 | tf_op jit(solution)/shard_map/ppermute | solution.py:530
  87.1 6.3 %collective-permute-start.16 = (f32[2,16,256]{2,1,0:T(8,128)S(1)}, f32[2,16,256]{2,1,0:T(8,128)S(1)}, u32[]{:S(2)}, u32[]{:S(2)}) collective-permute-start(f32[2,16,256]{2,1,0:T(8,128)S(1)} %get-tuple-element.72), channel_id=1, source_target_pairs={{0,64},{16,80},{32,96},{48,112},{64,0},{80,16},{96,32},{112,48},{1... | collective-permute-start | bytes 98312 | tf_op jit(solution)/shard_map/ppermute | solution.py:530
  91.4 4.8 %collective-permute-start.17 = (f32[2,16,256]{2,1,0:T(8,128)S(1)}, f32[2,16,256]{2,1,0:T(8,128)S(1)}, u32[]{:S(2)}, u32[]{:S(2)}) collective-permute-start(f32[2,16,256]{2,1,0:T(8,128)S(1)} %get-tuple-element.73), channel_id=1, source_target_pairs={{0,80},{16,64},{32,112},{48,96},{64,16},{80,0},{96,48},{112,32},{1... | collective-permute-start | bytes 98312 | tf_op jit(solution)/shard_map/ppermute | solution.py:530
  97.7 9.4 %all-to-all-start = ((f32[8,16,256]{2,1,0:T(8,128)}), f32[8,16,256]{2,1,0:T(8,128)S(1)}, u32[]{:S(2)}, u32[]{:S(2)}) async-start(f32[8,16,256]{2,1,0:T(8,128)} %get-tuple-element.77), calls=%async_computation | async-start | bytes 262144 | tf_op jit(solution)/shard_map/all_to_all | solution.py:533
  101.1 9.1 %collective-permute-start.19 = (f32[8,1536]{1,0:T(8,128)S(1)}, f32[8,1536]{1,0:T(8,128)S(1)}, u32[]{:S(2)}, u32[]{:S(2)}) collective-permute-start(f32[8,1536]{1,0:T(8,128)S(1)} %get-tuple-element.74.w_ref), channel_id=1, source_target_pairs={{1,0},{2,1},{3,2},{4,3},{5,4},{6,5},{7,6},{8,7},{9,8},{10,9},{11,1... | collective-permute-start | bytes 147464 | tf_op jit(solution)/shard_map/ppermute | solution.py:524
  102.4 7.8 %collective-permute-start.18 = (f32[8,1536]{1,0:T(8,128)S(1)}, f32[8,1536]{1,0:T(8,128)S(1)}, u32[]{:S(2)}, u32[]{:S(2)}) collective-permute-start(f32[8,1536]{1,0:T(8,128)S(1)} %get-tuple-element.74.w_ref), channel_id=1, source_target_pairs={{0,1},{1,2},{2,3},{3,4},{4,5},{5,6},{6,7},{7,8},{8,9},{9,10},{10,1... | collective-permute-start | bytes 147464 | tf_op jit(solution)/shard_map/ppermute | solution.py:527
  107.0 10.9 %slice-start = ((s8[4718592]{0:T(1024)(128)(4,1)}), s8[524288]{0:T(1024)(128)(4,1)S(1)}, s32[]{:S(2)}) async-start(s8[4718592]{0:T(1024)(128)(4,1)} %bitcast.1), calls=%async_computation.3 | async-start | bytes 1048576
  107.1 2.3 %copy-start.4 = (bf16[6,1536,256]{2,1,0:T(8,128)(2,1)S(1)}, bf16[6,1536,256]{2,1,0:T(8,128)(2,1)}, u32[]{:S(2)}) copy-start(bf16[6,1536,256]{2,1,0:T(8,128)(2,1)} %copy-done.3) | copy-start | bytes 14155780
  109.5 8.4 %copy-start.8 = (bf16[4,1536,256]{2,1,0:T(8,128)(2,1)S(1)}, bf16[4,1536,256]{2,1,0:T(8,128)(2,1)}, u32[]{:S(2)}) copy-start(bf16[4,1536,256]{2,1,0:T(8,128)(2,1)} %copy-done.7) | copy-start | bytes 9437188
  110.2 3.9 %copy-start.1 = (bf16[6,3072,256]{2,1,0:T(8,128)(2,1)S(1)}, bf16[6,3072,256]{2,1,0:T(8,128)(2,1)}, u32[]{:S(2)}) copy-start(bf16[6,3072,256]{2,1,0:T(8,128)(2,1)} %copy-done) | copy-start | bytes 28311556
  114.1 3.8 %slice-start.1 = ((s8[4718592]{0:T(1024)(128)(4,1)}), s8[4194304]{0:T(1024)(128)(4,1)S(1)}, s32[]{:S(2)}) async-start(s8[4718592]{0:T(1024)(128)(4,1)} %bitcast.1), calls=%async_computation.4 | async-start | bytes 8388608
  114.1 3.8 %copy-start.6 = (bf16[4,1536,256]{2,1,0:T(8,128)(2,1)S(1)}, bf16[4,1536,256]{2,1,0:T(8,128)(2,1)}, u32[]{:S(2)}) copy-start(bf16[4,1536,256]{2,1,0:T(8,128)(2,1)} %copy-done.5) | copy-start | bytes 9437188
  119.3 21.4 %all-to-all-start.1 = ((f32[8,24,256]{2,1,0:T(8,128)}), f32[8,24,256]{2,1,0:T(8,128)S(1)}, u32[]{:S(2)}, u32[]{:S(2)}) async-start(f32[8,24,256]{2,1,0:T(8,128)} %get-tuple-element.87), calls=%async_computation.1 | async-start | bytes 393216 | tf_op jit(solution)/shard_map/all_to_all | solution.py:533
  128.3 7.0 %collective-permute-start.20 = (f32[8,1536]{1,0:T(8,128)S(1)}, f32[8,1536]{1,0:T(8,128)S(1)}, u32[]{:S(2)}, u32[]{:S(2)}) collective-permute-start(f32[8,1536]{1,0:T(8,128)S(1)} %get-tuple-element.86), channel_id=1, source_target_pairs={{0,1},{1,2},{2,3},{3,4},{4,5},{5,6},{6,7},{7,8},{8,9},{9,10},{10,1... | collective-permute-start | bytes 147464 | tf_op jit(solution)/shard_map/ppermute | solution.py:527
  133.6 7.1 %collective-permute-start.21 = (f32[8,1536]{1,0:T(8,128)S(1)}, f32[8,1536]{1,0:T(8,128)S(1)}, u32[]{:S(2)}, u32[]{:S(2)}) collective-permute-start(f32[8,1536]{1,0:T(8,128)S(1)} %get-tuple-element.84.rl_ref), channel_id=1, source_target_pairs={{1,0},{2,1},{3,2},{4,3},{5,4},{6,5},{7,6},{8,7},{9,8},{10,9},{11,1... | collective-permute-start | bytes 147464 | tf_op jit(solution)/shard_map/ppermute | solution.py:524

commit v2 on v0

--- a/solution.py
+++ b/solution.py
@@ -162,7 +162,7 @@
             acc_ref[:, s] = fold_ones(mm(va[...], k_ref[t], NN))
             return carry
 
-        lax.fori_loop(0, nt, step, 0)
+        lax.fori_loop(0, nt, step, 0, unroll=2)
 
     return pl.pallas_call(
         body,
@@ -208,7 +208,7 @@
             acc[...] += mm(vb[:, s], k, NT)
             return carry
 
-        lax.fori_loop(0, nt, step, 0)
+        lax.fori_loop(0, nt, step, 0, unroll=2)
         rows = fold_ones(acc[...])
         rowl_ref[...] = rows[:, 0:n]
         rowo_ref[...] = rows[:, n:]
@@ -304,7 +304,7 @@
 
     def body(q_ref, r_ref, *refs):
         part_refs, (*x_refs, w_ref, deg_ref, sum_ref, acc) = refs[:m], refs[m:]
-        x_refs, out_refs = x_refs[:7], x_refs[7:]
+        x_refs, (own_ref, relay_ref) = x_refs[:7], x_refs[7:]
         g = lax.axis_index("group")
         total = part_refs[0][...]
         for p in part_refs[1:]:
@@ -323,10 +323,11 @@
         w = 0.5 * (deg * rv - acc[0:8, :])
         w_ref[...] = w
         deg_ref[...] = deg
-        for k, out in zip(SWAPS, out_refs):
-            for c in range(2):
-                t = jnp.maximum(q_ref[(g ^ k) * 2 + c], 0)
-                out[c * 8 : c * 8 + 8, :] = w_ref[:, span(t)]
+        for j in range(4):
+            for out, k in ((own_ref, 2 * j), (relay_ref, 2 * j + 1)):
+                for c in range(2):
+                    t = jnp.maximum(q_ref[(g ^ k) * 2 + c], 0)
+                    out[j, c * 8 : c * 8 + 8, :] = w_ref[:, span(t)]
         lane = lax.broadcasted_iota(jnp.int32, (8, 128), 1)
         sums = jnp.zeros((8, 128), F32)
         for k, v in enumerate((rv * rv, rv * w, w * w, 0.5 * deg * w * w)):
@@ -335,13 +336,29 @@
 
     return pl.pallas_call(
         body,
-        out_shape=[f32(16, TILE)] * 7 + [f32(8, n), f32(8, n), f32(8, 128)],
+        out_shape=[f32(4, 16, TILE), f32(4, 16, TILE), f32(8, n), f32(8, n), f32(8, 128)],
         in_specs=[SMEM] + [VM] * (m + 8),
-        out_specs=[VM] * 10,
+        out_specs=[VM] * 5,
         scratch_shapes=[pltpu.VMEM((16, n), F32)],
         compiler_params=params(),
         name="combine",
     )(table, r, *parts, *ret)
+
+
+def relay(own, partner):
+    def body(own_ref, partner_ref, *outs):
+        for j, out in enumerate(outs):
+            out[0] = own_ref[j + 1]
+            out[1] = partner_ref[j + 1]
+
+    return pl.pallas_call(
+        body,
+        out_shape=[f32(2, 16, TILE)] * 3,
+        in_specs=[VM, VM],
+        out_specs=[VM] * 3,
+        compiler_params=params(4),
+        name="relay",
+    )(own, partner)
 
 
 def local_second(k_local, w):
@@ -396,10 +413,12 @@
     def body(
         q_ref, ka_ref, kb_ref, kc_ref, w_ref, sum_ref, loc_ref, rl_ref, ro_ref, wl_ref, *refs
     ):
-        xw_refs, (col_ref, row_ref, va, acc, jobs, xw_ref) = refs[:7], refs[7:]
+        near_ref, *chip_refs, col_ref, row_ref, va, acc, jobs, xw_ref = refs
         g = lax.axis_index("group")
-        for k, x in zip(SWAPS, xw_refs):
-            xw_ref[g ^ k] = x[...]
+        xw_ref[g ^ 1] = near_ref[0]
+        for j, x in enumerate(chip_refs):
+            for i in range(2):
+                xw_ref[g ^ (2 * j + 2 + i)] = x[i]
         va[...] = split(w_ref[...])
         acc[...] = jnp.zeros_like(acc)
         for ks, k_ref in zip(STAGES, (ka_ref, kb_ref, kc_ref)):
@@ -436,7 +455,7 @@
     return pl.pallas_call(
         body,
         out_shape=(f32(8, 24, TILE), f32(8, n)),
-        in_specs=[SMEM] + [VM] * 16,
+        in_specs=[SMEM] + [VM] * 13,
         out_specs=(VM, VM),
         scratch_shapes=[
             pltpu.VMEM((16, n), BF16),
@@ -557,15 +576,16 @@
     from_left, from_right = left_of(to_r), right_of(to_l)
     k_c, row_c, *col_c = cross(STAGES[2], acc_band)
     ret = ret_near[2:] + ret_near[:2] + [swap(x, k) for x, k in zip(col_c, STAGES[2])]
-    *xw_out, w, deg, sums = combine(
+    w_own, w_relay, w, deg, sums = combine(
         table, targets, (acc_local, acc_band, from_left, from_right, row_a, row_b, row_c), ret
     )
-    w_left, w_right = left_of(w), right_of(w)
-    xw = [swap(x, k) for x, k in zip(xw_out, SWAPS)]
+    w_left = left_of(w)
+    w_right = right_of(w)
+    partner = swap(w_relay, 1)
+    xw = [partner] + [swap(x, 2 * j + 2) for j, x in enumerate(relay(w_own, partner))]
     loc2 = local_second(k_local, w)
     col_r, rowl_b, rowo_b = band_second(k_band, w_left, w, w_right, loc2)
-    from_left2 = left_of(col_r)
-    from_right2 = right_of(rowl_b)
+    from_left2, from_right2 = left_of(col_r), right_of(rowl_b)
     col_x, row_x = cross_second(table, (k_a, k_b, k_c), w, xw, sums, loc2, rowl_b, rowo_b, w_left)
     w2, column = group_sum(table, w, deg, (loc2, rowo_b, row_x, from_left2, from_right2), trade(col_x))
     return finish(trade(column, "dev"), targets, w, w2)

time: 150 us -> 144 us (0.960)
  starting transfers between devices: 64.3 us -> 60.5 us
  Pallas kernels: 35.7 us -> 33.8 us
    ppermute x21 -> x18, starting transfers between devices: 30 us -> 25 us  [swap(): return lax.ppermute(x, 'group', [(i, i ^ k) for i in range(8)])]
    ppermute x4, starting transfers between devices: 22.3 us -> 24.4 us  [left_of(): return lax.ppermute(x, 'dev', to_right)]
    ppermute x21 -> x18, waiting for transfers between devices: 25.7 us -> 24.8 us  [swap(): return lax.ppermute(x, 'group', [(i, i ^ k) for i in range(8)])]
  transfers between devices with their start and end apart: 30 -> 27, of which waited for: 11 -> 9; matrix products, arithmetic and copies ran while one was open for 0% -> 0% of each run, Pallas kernels for 19% -> 19%
where the time goes in v2:
time: 144 us; the launch traced here: 143 us
  starting transfers between devices  60.5 us (42%)
  Pallas kernels  33.8 us (23%)
  waiting for transfers between devices  29.5 us (20%)
  blocking collectives  18.7 us (13%)
    ppermute x18, starting transfers between devices, swap(): return lax.ppermute(x, 'group', [(i, i ^ k) for i in range(8)])  25 us
    ppermute x18, waiting for transfers between devices, swap(): return lax.ppermute(x, 'group', [(i, i ^ k) for i in range(8)])  24.8 us
    ppermute x4, starting transfers between devices, left_of(): return lax.ppermute(x, 'dev', to_right)  24.4 us
    all_to_all x1, blocking collectives, trade(): return lax.all_to_all(x, axis, split_axis=0, concat_axis=0, tiled=True)  18.7 us
    pallas_call x1, Pallas kernels, band_first(): pl.pallas_call(body, out_shape=(vmem_bf16(nt, 2 * n, TILE), f32(16, n), f...  13.8 us
    all_to_all x1, starting transfers between devices, trade(): return lax.all_to_all(x, axis, split_axis=0, concat_axis=0, tiled=True)  5.91 us
    pallas_call x1, Pallas kernels, local_first(): pl.pallas_call(body, out_shape=(vmem_bf16(nt, n, TILE), f32(16, n)), in_s...  5.86 us
    ppermute x4, starting transfers between devices, right_of(): return lax.ppermute(x, 'dev', to_left)  5.17 us
  transfers between devices with their start and end apart: 27, of which 9 were waited for; matrix products, arithmetic and copies ran while one was open for 0% of the time, Pallas kernels for 19%

profile of v2, /device:TPU:0, one launch (start us, length us, event | category | flops | bytes accessed | tf_op | source)
XLA Modules:
  0.0 143.3 jit_solution(4627545636727019016)
XLA Ops:
  0.6 2.6 %prep.1 = (s32[32]{0:T(128)S(1)}, bf16[6,264,512]{2,1,0:T(8,128)(2,1)S(1)}, bf16[2,264,512]{2,1,0:T(8,128)(2,1)S(1)}, bf16[2,264,512]{2,1,0:T(8,128)(2,1)S(1)}, ...) custom-call(s32[8,8,2,16]{3,2,1,0:T(2,128)} %bitcast.1, ...), custom_call_target="tpu_custom_call" | custom-call | tf_op jit(solution)/shard_map/prep/pallas_call | solution.py:111
  3.2 1.3 collective-permute-start.1
  4.5 4.6 %collective-permute-start = (bf16[6,264,512]{2,1,0:T(8,128)(2,1)S(1)}, bf16[6,264,512]{2,1,0:T(8,128)(2,1)S(1)}, u32[]{:S(2)}, u32[]{:S(2)}) collective-permute-start(bf16[6,264,512]{2,1,0:T(8,128)(2,1)S(1)} %get-tuple-element.51.a_ref), channel_id=1, source_target_pairs={{0,1},{1,2},{2,3},{3,4},{4,5},{5,6},{6,7},{7,8},{8,9},{9,10},{10,1... | collective-permute-start | bytes 4866056 | tf_op jit(solution)/shard_map/ppermute | solution.py:549
  9.1 2.1 %collective-permute-start.2 = (bf16[2,264,512]{2,1,0:T(8,128)(2,1)S(1)}, bf16[2,264,512]{2,1,0:T(8,128)(2,1)S(1)}, u32[]{:S(2)}, u32[]{:S(2)}) collective-permute-start(bf16[2,264,512]{2,1,0:T(8,128)(2,1)S(1)} %get-tuple-element.53), channel_id=1, source_target_pairs={{0,32},{16,48},{32,0},{48,16},{64,96},{80,112},{96,64},{112,80},{1... | collective-permute-start | bytes 1622024 | tf_op jit(solution)/shard_map/ppermute | solution.py:552
  11.3 2.5 %collective-permute-start.3 = (bf16[2,264,512]{2,1,0:T(8,128)(2,1)S(1)}, bf16[2,264,512]{2,1,0:T(8,128)(2,1)S(1)}, u32[]{:S(2)}, u32[]{:S(2)}) collective-permute-start(bf16[2,264,512]{2,1,0:T(8,128)(2,1)S(1)} %get-tuple-element.54), channel_id=1, source_target_pairs={{0,96},{16,112},{32,64},{48,80},{64,32},{80,48},{96,0},{112,16},{1... | collective-permute-start | bytes 1622024 | tf_op jit(solution)/shard_map/ppermute | solution.py:552
  13.8 9.2 %collective-permute-done.2.refs_0_ = bf16[2,264,512]{2,1,0:T(8,128)(2,1)S(1)} collective-permute-done((bf16[2,264,512]{2,1,0:T(8,128)(2,1)S(1)}, bf16[2,264,512]{2,1,0:T(8,128)(2,1)S(1)}, u32[]{:S(2)}, u32[]{:S(2)}) %collective-permute-start.2) | collective-permute-done | bytes 540704 | tf_op jit(solution)/shard_map/ppermute | solution.py:552
  23.0 2.7 %collective-permute-done.3.refs_1_ = bf16[2,264,512]{2,1,0:T(8,128)(2,1)S(1)} collective-permute-done((bf16[2,264,512]{2,1,0:T(8,128)(2,1)S(1)}, bf16[2,264,512]{2,1,0:T(8,128)(2,1)S(1)}, u32[]{:S(2)}, u32[]{:S(2)}) %collective-permute-start.3) | collective-permute-done | bytes 540704 | tf_op jit(solution)/shard_map/ppermute | solution.py:552
  25.6 1.3 collective-permute-start.6
  27.0 5.9 %local_first.1 = (bf16[6,1536,256]{2,1,0:T(8,128)(2,1)S(1)}, f32[16,1536]{1,0:T(8,128)S(1)}) custom-call(bf16[6,264,512]{2,1,0:T(8,128)(2,1)S(1)} %get-tuple-element.51.a_ref), custom_call_target="tpu_custom_call" | custom-call | tf_op jit(solution)/shard_map/local_first/pallas_call | solution.py:167
  32.8 1.1 shard_map.50
  33.9 3.3 %collective-permute-done.5.refs_0_.refs_3_ = bf16[2,264,512]{2,1,0:T(8,128)(2,1)S(1)} collective-permute-done((bf16[2,264,512]{2,1,0:T(8,128)(2,1)S(1)}, bf16[2,264,512]{2,1,0:T(8,128)(2,1)S(1)}, u32[]{:S(2)}, u32[]{:S(2)}) %collective-permute-start.5) | collective-permute-done | bytes 540704 | tf_op jit(solution)/shard_map/ppermute | solution.py:552
  37.3 4.0 %collective-permute-done.6.refs_1_.refs_4_ = bf16[2,264,512]{2,1,0:T(8,128)(2,1)S(1)} collective-permute-done((bf16[2,264,512]{2,1,0:T(8,128)(2,1)S(1)}, bf16[2,264,512]{2,1,0:T(8,128)(2,1)S(1)}, u32[]{:S(2)}, u32[]{:S(2)}) %collective-permute-start.6) | collective-permute-done | bytes 540704 | tf_op jit(solution)/shard_map/ppermute | solution.py:552
  41.3 0.7 collective-permute-start.9
  42.0 2.1 %collective-permute-start.10 = (bf16[2,264,512]{2,1,0:T(8,128)(2,1)S(1)}, bf16[2,264,512]{2,1,0:T(8,128)(2,1)S(1)}, u32[]{:S(2)}, u32[]{:S(2)}) collective-permute-start(bf16[2,264,512]{2,1,0:T(8,128)(2,1)S(1)} %get-tuple-element.69), channel_id=1, source_target_pairs={{0,80},{16,64},{32,112},{48,96},{64,16},{80,0},{96,48},{112,32},{1... | collective-permute-start | bytes 1622024 | tf_op jit(solution)/shard_map/ppermute | solution.py:552
  44.1 1.0 shard_map.51
  45.1 1.3 collective-permute-start.11
  46.4 13.8 %band_first.1 = (bf16[6,3072,256]{2,1,0:T(8,128)(2,1)S(1)}, f32[16,1536]{1,0:T(8,128)S(1)}, f32[16,1536]{1,0:T(8,128)S(1)}, f32[16,1536]{1,0:T(8,128)S(1)}) custom-call(bf16[6,264,512]{2,1,0:T(8,128)(2,1)S(1)} %collective-permute-done.l_ref, bf16[6,264,512]{2,1,0:T(8,128)(2,1)S(1)} %get-tuple-element.51.a_ref, ...), custom_call_target="tpu_custom_call" | custom-call | tf_op jit(solution)/shard_map/band_first/pallas_call | solution.py:216
  60.2 7.1 %collective-permute-start.7 = (f32[16,1536]{1,0:T(8,128)S(1)}, f32[16,1536]{1,0:T(8,128)S(1)}, u32[]{:S(2)}, u32[]{:S(2)}) collective-permute-start(f32[16,1536]{1,0:T(8,128)S(1)} %get-tuple-element.64), channel_id=1, source_target_pairs={{0,1},{1,2},{2,3},{3,4},{4,5},{5,6},{6,7},{7,8},{8,9},{9,10},{10,1... | collective-permute-start | bytes 294920 | tf_op jit(solution)/shard_map/ppermute | solution.py:549
  67.4 1.3 collective-permute-start.8
  68.7 2.0 %collective-permute-start.12 = (f32[2,16,256]{2,1,0:T(8,128)S(1)}, f32[2,16,256]{2,1,0:T(8,128)S(1)}, u32[]{:S(2)}, u32[]{:S(2)}) collective-permute-start(f32[2,16,256]{2,1,0:T(8,128)S(1)} %get-tuple-element.72), channel_id=1, source_target_pairs={{0,96},{16,112},{32,64},{48,80},{64,32},{80,48},{96,0},{112,16},{1... | collective-permute-start | bytes 98312 | tf_op jit(solution)/shard_map/ppermute | solution.py:552
  70.7 1.5 %collective-permute-start.14 = (f32[2,16,256]{2,1,0:T(8,128)S(1)}, f32[2,16,256]{2,1,0:T(8,128)S(1)}, u32[]{:S(2)}, u32[]{:S(2)}) collective-permute-start(f32[2,16,256]{2,1,0:T(8,128)S(1)} %get-tuple-element.74), channel_id=1, source_target_pairs={{0,48},{16,32},{32,16},{48,0},{64,112},{80,96},{96,80},{112,64},{1... | collective-permute-start | bytes 98312 | tf_op jit(solution)/shard_map/ppermute | solution.py:552
  72.2 1.0 shard_map.52
  73.2 0.7 collective-permute-done.12.refs_8_
  73.9 2.8 %collective-permute-start.15 = (f32[2,16,256]{2,1,0:T(8,128)S(1)}, f32[2,16,256]{2,1,0:T(8,128)S(1)}, u32[]{:S(2)}, u32[]{:S(2)}) collective-permute-start(f32[2,16,256]{2,1,0:T(8,128)S(1)} %get-tuple-element.75), channel_id=1, source_target_pairs={{0,112},{16,96},{32,80},{48,64},{64,48},{80,32},{96,16},{112,0},{1... | collective-permute-start | bytes 98312 | tf_op jit(solution)/shard_map/ppermute | solution.py:552
  76.6 3.8 %collective-permute-start.16 = (f32[2,16,256]{2,1,0:T(8,128)S(1)}, f32[2,16,256]{2,1,0:T(8,128)S(1)}, u32[]{:S(2)}, u32[]{:S(2)}) collective-permute-start(f32[2,16,256]{2,1,0:T(8,128)S(1)} %get-tuple-element.76), channel_id=1, source_target_pairs={{0,64},{16,80},{32,96},{48,112},{64,0},{80,16},{96,32},{112,48},{1... | collective-permute-start | bytes 98312 | tf_op jit(solution)/shard_map/ppermute | solution.py:552
  80.5 1.9 %collective-permute-done.16.refs_12_ = f32[2,16,256]{2,1,0:T(8,128)S(1)} collective-permute-done((f32[2,16,256]{2,1,0:T(8,128)S(1)}, f32[2,16,256]{2,1,0:T(8,128)S(1)}, u32[]{:S(2)}, u32[]{:S(2)}) %collective-permute-start.16) | collective-permute-done | bytes 32800 | tf_op jit(solution)/shard_map/ppermute | solution.py:552
  82.3 3.0 %collective-permute-done.17.refs_13_ = f32[2,16,256]{2,1,0:T(8,128)S(1)} collective-permute-done((f32[2,16,256]{2,1,0:T(8,128)S(1)}, f32[2,16,256]{2,1,0:T(8,128)S(1)}, u32[]{:S(2)}, u32[]{:S(2)}) %collective-permute-start.17) | collective-permute-done | bytes 32800 | tf_op jit(solution)/shard_map/ppermute | solution.py:552
  85.3 0.8 combine.1
  86.1 0.0 collective-permute-start.20
  86.2 1.3 collective-permute-start.19
  87.5 5.3 %collective-permute-start.18 = (f32[8,1536]{1,0:T(8,128)S(1)}, f32[8,1536]{1,0:T(8,128)S(1)}, u32[]{:S(2)}, u32[]{:S(2)}) collective-permute-start(f32[8,1536]{1,0:T(8,128)S(1)} %get-tuple-element.78.w_ref), channel_id=1, source_target_pairs={{0,1},{1,2},{2,3},{3,4},{4,5},{5,6},{6,7},{7,8},{8,9},{9,10},{10,1... | collective-permute-start | bytes 147464 | tf_op jit(solution)/shard_map/ppermute | solution.py:549
  92.8 1.5 %collective-permute-start.21 = (f32[2,16,256]{2,1,0:T(8,128)S(1)}, f32[2,16,256]{2,1,0:T(8,128)S(1)}, u32[]{:S(2)}, u32[]{:S(2)}) collective-permute-start(f32[2,16,256]{2,1,0:T(8,128)S(1)} %get-tuple-element.90), channel_id=1, source_target_pairs={{0,32},{16,48},{32,0},{48,16},{64,96},{80,112},{96,64},{112,80},{1... | collective-permute-start | bytes 98312 | tf_op jit(solution)/shard_map/ppermute | solution.py:552
  94.3 1.2 collective-permute-start.22
  95.5 2.1 %collective-permute-start.23 = (f32[2,16,256]{2,1,0:T(8,128)S(1)}, f32[2,16,256]{2,1,0:T(8,128)S(1)}, u32[]{:S(2)}, u32[]{:S(2)}) collective-permute-start(f32[2,16,256]{2,1,0:T(8,128)S(1)} %get-tuple-element.92), channel_id=1, source_target_pairs={{0,96},{16,112},{32,64},{48,80},{64,32},{80,48},{96,0},{112,16},{1... | collective-permute-start | bytes 98312 | tf_op jit(solution)/shard_map/ppermute | solution.py:552
  97.6 0.7 local_second.1._.loc_ref.refs_0_
  98.3 0.0 collective-permute-done.18.wl_ref
  98.3 3.8 %band_second.1 = (f32[8,1536]{1,0:T(8,128)S(1)}, f32[8,1536]{1,0:T(8,128)S(1)}, f32[8,1536]{1,0:T(8,128)S(1)}) custom-call(bf16[6,3072,256]{2,1,0:T(8,128)(2,1)S(1)} %get-tuple-element.81.k_ref, f32[8,1536]{1,0:T(8,128)S(1)} %collective-permute-done.18.wl_ref, f32[8,1536]{1,0:T(8,128)S(1)} %get-tuple-element.78.w_ref, ...), custom_call_target="tpu_custom_call" | custom-call | tf_op jit(solution)/shard_map/band_second/pallas_call | solution.py:399
  102.1 0.0 collective-permute-done.21.refs_1_
  102.1 0.0 collective-permute-done.22.refs_2_
  102.1 1.4 cross_second.1
  103.5 5.9 %all-to-all-start = ((f32[8,24,256]{2,1,0:T(8,128)}), f32[8,24,256]{2,1,0:T(8,128)S(1)}, u32[]{:S(2)}, u32[]{:S(2)}) async-start(f32[8,24,256]{2,1,0:T(8,128)} %get-tuple-element.95), calls=%async_computation | async-start | bytes 393216 | tf_op jit(solution)/shard_map/all_to_all | solution.py:555
  109.4 7.4 %collective-permute-start.24 = (f32[8,1536]{1,0:T(8,128)S(1)}, f32[8,1536]{1,0:T(8,128)S(1)}, u32[]{:S(2)}, u32[]{:S(2)}) collective-permute-start(f32[8,1536]{1,0:T(8,128)S(1)} %get-tuple-element.94), channel_id=1, source_target_pairs={{0,1},{1,2},{2,3},{3,4},{4,5},{5,6},{6,7},{7,8},{8,9},{9,10},{10,1... | collective-permute-start | bytes 147464 | tf_op jit(solution)/shard_map/ppermute | solution.py:549
  116.8 1.3 collective-permute-start.25
  118.1 0.4 collective-permute-done.24.refs_3_
  118.5 4.3 %collective-permute-done.25.refs_4_ = f32[8,1536]{1,0:T(8,128)S(1)} collective-permute-done((f32[8,1536]{1,0:T(8,128)S(1)}, f32[8,1536]{1,0:T(8,128)S(1)}, u32[]{:S(2)}, u32[]{:S(2)}) %collective-permute-start.25) | collective-permute-done | bytes 49184 | tf_op jit(solution)/shard_map/ppermute | solution.py:546
  122.8 0.7 group_sum.1
  123.5 18.7 %all_to_all.10.g_ref = f32[16,8,128]{2,1,0:T(8,128)S(1)} all-to-all(f32[16,8,128]{2,1,0:T(8,128)S(1)} %get-tuple-element.96), channel_id=1, replica_groups=mesh['group'=8,'dev'=16] {'dev'}, dimensions={0} | all-to-all | bytes 131072 | tf_op jit(solution)/shard_map/all_to_all | solution.py:555
  142.2 1.1 finish.1
  (23 shorter events, 0.1 us)
Async XLA Ops:
  3.2 43.2 %collective-permute-start.1 = (bf16[6,264,512]{2,1,0:T(8,128)(2,1)S(1)}, bf16[6,264,512]{2,1,0:T(8,128)(2,1)S(1)}, u32[]{:S(2)}, u32[]{:S(2)}) collective-permute-start(bf16[6,264,512]{2,1,0:T(8,128)(2,1)S(1)} %get-tuple-element.51.a_ref), channel_id=1, source_target_pairs={{1,0},{2,1},{3,2},{4,3},{5,4},{6,5},{7,6},{8,7},{9,8},{10,9},{11,1... | collective-permute-start | bytes 4866056 | tf_op jit(solution)/shard_map/ppermute | solution.py:546
  4.5 42.0 %collective-permute-start = (bf16[6,264,512]{2,1,0:T(8,128)(2,1)S(1)}, bf16[6,264,512]{2,1,0:T(8,128)(2,1)S(1)}, u32[]{:S(2)}, u32[]{:S(2)}) collective-permute-start(bf16[6,264,512]{2,1,0:T(8,128)(2,1)S(1)} %get-tuple-element.51.a_ref), channel_id=1, source_target_pairs={{0,1},{1,2},{2,3},{3,4},{4,5},{5,6},{6,7},{7,8},{8,9},{9,10},{10,1... | collective-permute-start | bytes 4866056 | tf_op jit(solution)/shard_map/ppermute | solution.py:549
  9.1 13.8 %collective-permute-start.2 = (bf16[2,264,512]{2,1,0:T(8,128)(2,1)S(1)}, bf16[2,264,512]{2,1,0:T(8,128)(2,1)S(1)}, u32[]{:S(2)}, u32[]{:S(2)}) collective-permute-start(bf16[2,264,512]{2,1,0:T(8,128)(2,1)S(1)} %get-tuple-element.53), channel_id=1, source_target_pairs={{0,32},{16,48},{32,0},{48,16},{64,96},{80,112},{96,64},{112,80},{1... | collective-permute-start | bytes 1622024 | tf_op jit(solution)/shard_map/ppermute | solution.py:552
  11.3 14.4 %collective-permute-start.3 = (bf16[2,264,512]{2,1,0:T(8,128)(2,1)S(1)}, bf16[2,264,512]{2,1,0:T(8,128)(2,1)S(1)}, u32[]{:S(2)}, u32[]{:S(2)}) collective-permute-start(bf16[2,264,512]{2,1,0:T(8,128)(2,1)S(1)} %get-tuple-element.54), channel_id=1, source_target_pairs={{0,96},{16,112},{32,64},{48,80},{64,32},{80,48},{96,0},{112,16},{1... | collective-permute-start | bytes 1622024 | tf_op jit(solution)/shard_map/ppermute | solution.py:552
  13.8 19.0 %collective-permute-start.4 = (bf16[2,264,512]{2,1,0:T(8,128)(2,1)S(1)}, bf16[2,264,512]{2,1,0:T(8,128)(2,1)S(1)}, u32[]{:S(2)}, u32[]{:S(2)}) collective-permute-start(bf16[2,264,512]{2,1,0:T(8,128)(2,1)S(1)} %get-tuple-element.55), channel_id=1, source_target_pairs={{0,16},{16,0},{32,48},{48,32},{64,80},{80,64},{96,112},{112,96},{1... | collective-permute-start | bytes 1622024 | tf_op jit(solution)/shard_map/ppermute | solution.py:552
  23.0 14.3 %collective-permute-start.5 = (bf16[2,264,512]{2,1,0:T(8,128)(2,1)S(1)}, bf16[2,264,512]{2,1,0:T(8,128)(2,1)S(1)}, u32[]{:S(2)}, u32[]{:S(2)}) collective-permute-start(bf16[2,264,512]{2,1,0:T(8,128)(2,1)S(1)} %get-tuple-element.57), channel_id=1, source_target_pairs={{0,48},{16,32},{32,16},{48,0},{64,112},{80,96},{96,80},{112,64},{1... | collective-permute-start | bytes 1622024 | tf_op jit(solution)/shard_map/ppermute | solution.py:552
  25.6 15.7 %collective-permute-start.6 = (bf16[2,264,512]{2,1,0:T(8,128)(2,1)S(1)}, bf16[2,264,512]{2,1,0:T(8,128)(2,1)S(1)}, u32[]{:S(2)}, u32[]{:S(2)}) collective-permute-start(bf16[2,264,512]{2,1,0:T(8,128)(2,1)S(1)} %get-tuple-element.58), channel_id=1, source_target_pairs={{0,112},{16,96},{32,80},{48,64},{64,48},{80,32},{96,16},{112,0},{1... | collective-permute-start | bytes 1622024 | tf_op jit(solution)/shard_map/ppermute | solution.py:552
  41.3 29.4 %collective-permute-start.9 = (bf16[2,264,512]{2,1,0:T(8,128)(2,1)S(1)}, bf16[2,264,512]{2,1,0:T(8,128)(2,1)S(1)}, u32[]{:S(2)}, u32[]{:S(2)}) collective-permute-start(bf16[2,264,512]{2,1,0:T(8,128)(2,1)S(1)} %get-tuple-element.68), channel_id=1, source_target_pairs={{0,64},{16,80},{32,96},{48,112},{64,0},{80,16},{96,32},{112,48},{1... | collective-permute-start | bytes 1622024 | tf_op jit(solution)/shard_map/ppermute | solution.py:552
  42.0 28.7 %collective-permute-start.10 = (bf16[2,264,512]{2,1,0:T(8,128)(2,1)S(1)}, bf16[2,264,512]{2,1,0:T(8,128)(2,1)S(1)}, u32[]{:S(2)}, u32[]{:S(2)}) collective-permute-start(bf16[2,264,512]{2,1,0:T(8,128)(2,1)S(1)} %get-tuple-element.69), channel_id=1, source_target_pairs={{0,80},{16,64},{32,112},{48,96},{64,16},{80,0},{96,48},{112,32},{1... | collective-permute-start | bytes 1622024 | tf_op jit(solution)/shard_map/ppermute | solution.py:552
  45.1 23.5 %collective-permute-start.11 = (f32[2,16,256]{2,1,0:T(8,128)S(1)}, f32[2,16,256]{2,1,0:T(8,128)S(1)}, u32[]{:S(2)}, u32[]{:S(2)}) collective-permute-start(f32[2,16,256]{2,1,0:T(8,128)S(1)} %get-tuple-element.71), channel_id=1, source_target_pairs={{0,32},{16,48},{32,0},{48,16},{64,96},{80,112},{96,64},{112,80},{1... | collective-permute-start | bytes 98312 | tf_op jit(solution)/shard_map/ppermute | solution.py:552
  46.4 38.9 %copy-start = (f32[8,1536]{1,0:T(8,128)S(1)}, f32[8,1536]{1,0:T(8,128)}, u32[]{:S(2)}) copy-start(f32[8,1536]{1,0:T(8,128)} %r_ref.3) | copy-start | bytes 147460
  60.2 25.0 %collective-permute-start.7 = (f32[16,1536]{1,0:T(8,128)S(1)}, f32[16,1536]{1,0:T(8,128)S(1)}, u32[]{:S(2)}, u32[]{:S(2)}) collective-permute-start(f32[16,1536]{1,0:T(8,128)S(1)} %get-tuple-element.64), channel_id=1, source_target_pairs={{0,1},{1,2},{2,3},{3,4},{4,5},{5,6},{6,7},{7,8},{8,9},{9,10},{10,1... | collective-permute-start | bytes 294920 | tf_op jit(solution)/shard_map/ppermute | solution.py:549
  67.4 17.9 %collective-permute-start.8 = (f32[16,1536]{1,0:T(8,128)S(1)}, f32[16,1536]{1,0:T(8,128)S(1)}, u32[]{:S(2)}, u32[]{:S(2)}) collective-permute-start(f32[16,1536]{1,0:T(8,128)S(1)} %get-tuple-element.65), channel_id=1, source_target_pairs={{1,0},{2,1},{3,2},{4,3},{5,4},{6,5},{7,6},{8,7},{9,8},{10,9},{11,1... | collective-permute-start | bytes 294920 | tf_op jit(solution)/shard_map/ppermute | solution.py:546
  68.7 5.2 %collective-permute-start.12 = (f32[2,16,256]{2,1,0:T(8,128)S(1)}, f32[2,16,256]{2,1,0:T(8,128)S(1)}, u32[]{:S(2)}, u32[]{:S(2)}) collective-permute-start(f32[2,16,256]{2,1,0:T(8,128)S(1)} %get-tuple-element.72), channel_id=1, source_target_pairs={{0,96},{16,112},{32,64},{48,80},{64,32},{80,48},{96,0},{112,16},{1... | collective-permute-start | bytes 98312 | tf_op jit(solution)/shard_map/ppermute | solution.py:552
  70.7 6.0 %collective-permute-start.13 = (f32[2,16,256]{2,1,0:T(8,128)S(1)}, f32[2,16,256]{2,1,0:T(8,128)S(1)}, u32[]{:S(2)}, u32[]{:S(2)}) collective-permute-start(f32[2,16,256]{2,1,0:T(8,128)S(1)} %get-tuple-element.73), channel_id=1, source_target_pairs={{0,16},{16,0},{32,48},{48,32},{64,80},{80,64},{96,112},{112,96},{1... | collective-permute-start | bytes 98312 | tf_op jit(solution)/shard_map/ppermute | solution.py:552
  70.7 9.8 %collective-permute-start.14 = (f32[2,16,256]{2,1,0:T(8,128)S(1)}, f32[2,16,256]{2,1,0:T(8,128)S(1)}, u32[]{:S(2)}, u32[]{:S(2)}) collective-permute-start(f32[2,16,256]{2,1,0:T(8,128)S(1)} %get-tuple-element.74), channel_id=1, source_target_pairs={{0,48},{16,32},{32,16},{48,0},{64,112},{80,96},{96,80},{112,64},{1... | collective-permute-start | bytes 98312 | tf_op jit(solution)/shard_map/ppermute | solution.py:552
  73.9 6.6 %collective-permute-start.15 = (f32[2,16,256]{2,1,0:T(8,128)S(1)}, f32[2,16,256]{2,1,0:T(8,128)S(1)}, u32[]{:S(2)}, u32[]{:S(2)}) collective-permute-start(f32[2,16,256]{2,1,0:T(8,128)S(1)} %get-tuple-element.75), channel_id=1, source_target_pairs={{0,112},{16,96},{32,80},{48,64},{64,48},{80,32},{96,16},{112,0},{1... | collective-permute-start | bytes 98312 | tf_op jit(solution)/shard_map/ppermute | solution.py:552
  76.6 5.7 %collective-permute-start.16 = (f32[2,16,256]{2,1,0:T(8,128)S(1)}, f32[2,16,256]{2,1,0:T(8,128)S(1)}, u32[]{:S(2)}, u32[]{:S(2)}) collective-permute-start(f32[2,16,256]{2,1,0:T(8,128)S(1)} %get-tuple-element.76), channel_id=1, source_target_pairs={{0,64},{16,80},{32,96},{48,112},{64,0},{80,16},{96,32},{112,48},{1... | collective-permute-start | bytes 98312 | tf_op jit(solution)/shard_map/ppermute | solution.py:552
  80.4 4.8 %collective-permute-start.17 = (f32[2,16,256]{2,1,0:T(8,128)S(1)}, f32[2,16,256]{2,1,0:T(8,128)S(1)}, u32[]{:S(2)}, u32[]{:S(2)}) collective-permute-start(f32[2,16,256]{2,1,0:T(8,128)S(1)} %get-tuple-element.77), channel_id=1, source_target_pairs={{0,80},{16,64},{32,112},{48,96},{64,16},{80,0},{96,48},{112,32},{1... | collective-permute-start | bytes 98312 | tf_op jit(solution)/shard_map/ppermute | solution.py:552
  86.1 6.6 %collective-permute-start.20 = (f32[4,16,256]{2,1,0:T(8,128)S(1)}, f32[4,16,256]{2,1,0:T(8,128)S(1)}, u32[]{:S(2)}, u32[]{:S(2)}) collective-permute-start(f32[4,16,256]{2,1,0:T(8,128)S(1)} %get-tuple-element.88), channel_id=1, source_target_pairs={{0,16},{16,0},{32,48},{48,32},{64,80},{80,64},{96,112},{112,96},{1... | collective-permute-start | bytes 196616 | tf_op jit(solution)/shard_map/ppermute | solution.py:552
  86.2 12.1 %collective-permute-start.19 = (f32[8,1536]{1,0:T(8,128)S(1)}, f32[8,1536]{1,0:T(8,128)S(1)}, u32[]{:S(2)}, u32[]{:S(2)}) collective-permute-start(f32[8,1536]{1,0:T(8,128)S(1)} %get-tuple-element.78.w_ref), channel_id=1, source_target_pairs={{1,0},{2,1},{3,2},{4,3},{5,4},{6,5},{7,6},{8,7},{9,8},{10,9},{11,1... | collective-permute-start | bytes 147464 | tf_op jit(solution)/shard_map/ppermute | solution.py:546
  87.5 10.8 %collective-permute-start.18 = (f32[8,1536]{1,0:T(8,128)S(1)}, f32[8,1536]{1,0:T(8,128)S(1)}, u32[]{:S(2)}, u32[]{:S(2)}) collective-permute-start(f32[8,1536]{1,0:T(8,128)S(1)} %get-tuple-element.78.w_ref), channel_id=1, source_target_pairs={{0,1},{1,2},{2,3},{3,4},{4,5},{5,6},{6,7},{7,8},{8,9},{9,10},{10,1... | collective-permute-start | bytes 147464 | tf_op jit(solution)/shard_map/ppermute | solution.py:549
  92.8 9.3 %collective-permute-start.21 = (f32[2,16,256]{2,1,0:T(8,128)S(1)}, f32[2,16,256]{2,1,0:T(8,128)S(1)}, u32[]{:S(2)}, u32[]{:S(2)}) collective-permute-start(f32[2,16,256]{2,1,0:T(8,128)S(1)} %get-tuple-element.90), channel_id=1, source_target_pairs={{0,32},{16,48},{32,0},{48,16},{64,96},{80,112},{96,64},{112,80},{1... | collective-permute-start | bytes 98312 | tf_op jit(solution)/shard_map/ppermute | solution.py:552
  94.3 7.9 %collective-permute-start.22 = (f32[2,16,256]{2,1,0:T(8,128)S(1)}, f32[2,16,256]{2,1,0:T(8,128)S(1)}, u32[]{:S(2)}, u32[]{:S(2)}) collective-permute-start(f32[2,16,256]{2,1,0:T(8,128)S(1)} %get-tuple-element.91), channel_id=1, source_target_pairs={{0,64},{16,80},{32,96},{48,112},{64,0},{80,16},{96,32},{112,48},{1... | collective-permute-start | bytes 98312 | tf_op jit(solution)/shard_map/ppermute | solution.py:552
  95.5 6.7 %collective-permute-start.23 = (f32[2,16,256]{2,1,0:T(8,128)S(1)}, f32[2,16,256]{2,1,0:T(8,128)S(1)}, u32[]{:S(2)}, u32[]{:S(2)}) collective-permute-start(f32[2,16,256]{2,1,0:T(8,128)S(1)} %get-tuple-element.92), channel_id=1, source_target_pairs={{0,96},{16,112},{32,64},{48,80},{64,32},{80,48},{96,0},{112,16},{1... | collective-permute-start | bytes 98312 | tf_op jit(solution)/shard_map/ppermute | solution.py:552
  103.5 19.3 %all-to-all-start = ((f32[8,24,256]{2,1,0:T(8,128)}), f32[8,24,256]{2,1,0:T(8,128)S(1)}, u32[]{:S(2)}, u32[]{:S(2)}) async-start(f32[8,24,256]{2,1,0:T(8,128)} %get-tuple-element.95), calls=%async_computation | async-start | bytes 393216 | tf_op jit(solution)/shard_map/all_to_all | solution.py:555
  109.4 9.1 %collective-permute-start.24 = (f32[8,1536]{1,0:T(8,128)S(1)}, f32[8,1536]{1,0:T(8,128)S(1)}, u32[]{:S(2)}, u32[]{:S(2)}) collective-permute-start(f32[8,1536]{1,0:T(8,128)S(1)} %get-tuple-element.94), channel_id=1, source_target_pairs={{0,1},{1,2},{2,3},{3,4},{4,5},{5,6},{6,7},{7,8},{8,9},{9,10},{10,1... | collective-permute-start | bytes 147464 | tf_op jit(solution)/shard_map/ppermute | solution.py:549
  116.8 6.0 %collective-permute-start.25 = (f32[8,1536]{1,0:T(8,128)S(1)}, f32[8,1536]{1,0:T(8,128)S(1)}, u32[]{:S(2)}, u32[]{:S(2)}) collective-permute-start(f32[8,1536]{1,0:T(8,128)S(1)} %get-tuple-element.87.rl_ref), channel_id=1, source_target_pairs={{1,0},{2,1},{3,2},{4,3},{5,4},{6,5},{7,6},{8,7},{9,8},{10,9},{11,1... | collective-permute-start | bytes 147464 | tf_op jit(solution)/shard_map/ppermute | solution.py:546

commit v3 on v2

--- a/solution.py
+++ b/solution.py
@@ -141,11 +141,11 @@
     )(*held, *arrived)
 
 
-def local_first(own):
+def local_first(own, after):
     nt, _, _ = own.shape
     n = nt * TILE
 
-    def body(a_ref, k_ref, acc_ref, na, nb, va):
+    def body(a_ref, _, k_ref, acc_ref, na, nb, va):
         for i in range(nt):
             s = slice(i * TILE, (i + 1) * TILE)
             x = col_norms(a_ref[i, 0:TILE, :])
@@ -167,12 +167,12 @@
     return pl.pallas_call(
         body,
         out_shape=(vmem_bf16(nt, n, TILE), f32(16, n)),
-        in_specs=[VM],
+        in_specs=[VM, ANY],
         out_specs=(VM, VM),
         scratch_shapes=[pltpu.VMEM((n, 128), F32), pltpu.VMEM((8, n), F32), pltpu.VMEM((32, n), BF16)],
         compiler_params=params(),
         name="local_first",
-    )(own)
+    )(own, after)
 
 
 def band_first(left, own, right, after):
@@ -230,17 +230,16 @@
     )(left, own, right, *after)
 
 
-def cross_first(ks, table, own, tiles, after, held=()):
+def cross_first(ks, table, own, tiles, after):
     nt, _, d = own.shape
     n = nt * TILE
     m = len(ks)
     slots = 2 * m
-    p = len(held)
 
     def body(q_ref, a_ref, _, *refs):
         tile_refs = refs[:m]
-        k_ref, row_ref, *cols = refs[m + p : 2 * m + p + 2]
-        buf, jobs, sems, na, va, acc, nb, col = refs[2 * m + 2 * p + 2 :]
+        k_ref, row_ref, *cols = refs[m : 2 * m + 2]
+        buf, jobs, sems, na, va, acc, nb, col = refs[2 * m + 2 :]
         g = lax.axis_index("group")
         count = jnp.int32(0)
         for i, k in enumerate(ks):
@@ -280,10 +279,9 @@
 
     return pl.pallas_call(
         body,
-        out_shape=[vmem_bf16(slots, n, TILE), f32(16, n)] + [f32(2, 16, TILE)] * (m + p),
-        in_specs=[SMEM, VM, ANY] + [ANY] * m + [VM] * p,
-        out_specs=[VM] * (2 + m + p),
-        input_output_aliases={3 + m + i: 2 + m + i for i in range(p)},
+        out_shape=[vmem_bf16(slots, n, TILE), f32(16, n)] + [f32(2, 16, TILE)] * m,
+        in_specs=[SMEM, VM, ANY] + [ANY] * m,
+        out_specs=[VM] * (2 + m),
         scratch_shapes=[
             pltpu.VMEM((slots, TILE + EXTRA, d), BF16),
             pltpu.SMEM((slots,), jnp.int32),
@@ -295,7 +293,7 @@
             pltpu.VMEM((slots, 16, TILE), F32),
         ],
         compiler_params=params(),
-    )(table, own, after, *tiles, *held)
+    )(table, own, after, *tiles)
 
 
 def combine(table, r, parts, ret):
@@ -346,14 +344,18 @@
 
 
 def relay(own, partner):
+    summed = own.shape[0] == 5
+
     def body(own_ref, partner_ref, *outs):
         for j, out in enumerate(outs):
             out[0] = own_ref[j + 1]
             out[1] = partner_ref[j + 1]
-
-    return pl.pallas_call(
-        body,
-        out_shape=[f32(2, 16, TILE)] * 3,
+            if summed:
+                out[2] = own_ref[4] + partner_ref[4]
+
+    return pl.pallas_call(
+        body,
+        out_shape=[f32(2 + summed, 16, TILE)] * 3,
         in_specs=[VM, VM],
         out_specs=[VM] * 3,
         compiler_params=params(4),
@@ -413,7 +415,7 @@
     def body(
         q_ref, ka_ref, kb_ref, kc_ref, w_ref, sum_ref, loc_ref, rl_ref, ro_ref, wl_ref, *refs
     ):
-        near_ref, *chip_refs, col_ref, row_ref, va, acc, jobs, xw_ref = refs
+        near_ref, *chip_refs, own_ref, relay_ref, row_ref, va, acc, jobs, xw_ref, col_ref = refs
         g = lax.axis_index("group")
         xw_ref[g ^ 1] = near_ref[0]
         for j, x in enumerate(chip_refs):
@@ -448,60 +450,66 @@
         pairs = w_ref[...] * (0.5 * loc_ref[...] + ro_ref[...] + row) + wl_ref[...] * rl_ref[...]
         lane = lax.broadcasted_iota(jnp.int32, (8, 128), 1)
         pay = jnp.where(lane == 3, sum_ref[...] - jnp.sum(pairs, axis=1, keepdims=True), sum_ref[...])
-        for h in range(8):
-            col_ref[h, 16:24, 0:128] = pay
-            col_ref[h, 16:24, 128:] = jnp.zeros((8, 128), F32)
-
-    return pl.pallas_call(
-        body,
-        out_shape=(f32(8, 24, TILE), f32(8, n)),
+        for j in range(4):
+            own_ref[j] = col_ref[g ^ (2 * j)]
+            relay_ref[j] = col_ref[g ^ (2 * j + 1)]
+        for out in (own_ref, relay_ref):
+            out[4] = jnp.zeros((16, TILE), F32)
+            out[4, 0:8, 0:128] = pay
+
+    return pl.pallas_call(
+        body,
+        out_shape=(f32(5, 16, TILE), f32(5, 16, TILE), f32(8, n)),
         in_specs=[SMEM] + [VM] * 13,
-        out_specs=(VM, VM),
+        out_specs=(VM, VM, VM),
         scratch_shapes=[
             pltpu.VMEM((16, n), BF16),
             pltpu.VMEM((16, n), F32),
             pltpu.SMEM((16,), jnp.int32),
             pltpu.VMEM((8, 16, TILE), F32),
+            pltpu.VMEM((8, 16, TILE), F32),
         ],
         compiler_params=params(),
         name="cross_second",
     )(table, *k_caches, w, sums, loc, row_left, row_own, w_left, *xw)
 
 
-def group_sum(table, w, deg, parts, ret):
+def group_sum(table, w, deg, parts, own, partner, chips):
     n = w.shape[1]
     m = len(parts)
 
     def body(q_ref, w_ref, deg_ref, *refs):
-        part_refs, (x_ref, w2_ref, out_ref, acc) = refs[:m], refs[m:]
+        part_refs, (own_ref, partner_ref, *chip_refs, w2_ref, out_ref, acc) = refs[:m], refs[m:]
+        g = lax.axis_index("group")
         total = part_refs[0][...]
         for p in part_refs[1:]:
             total = total + p[...]
         acc[...] = total
-        for h in range(8):
+        for k in range(1, 8):
             for c in range(2):
-                t = q_ref[h * 2 + c]
+                t = q_ref[(g ^ k) * 2 + c]
 
                 @pl.when(t >= 0)
-                def _(h=h, c=c, t=t):
-                    acc[:, span(t)] = acc[:, span(t)] + x_ref[h, c * 8 : c * 8 + 8, :]
+                def _(k=k, c=c, t=t):
+                    x = partner_ref.at[0] if k == 1 else chip_refs[k // 2 - 1].at[k % 2]
+                    acc[:, span(t)] = acc[:, span(t)] + x[c * 8 : c * 8 + 8, :]
 
         w2_ref[...] = 0.5 * (deg_ref[...] * w_ref[...] - acc[...])
-        sums = x_ref[0, 16:24, 0:128]
-        for h in range(1, 8):
-            sums = sums + x_ref[h, 16:24, 0:128]
+        sums = own_ref[4, 0:8, 0:128] + partner_ref[4, 0:8, 0:128]
+        for x in chip_refs:
+            sums = sums + x[2, 0:8, 0:128]
         for v in range(16):
             out_ref[v] = sums
 
     return pl.pallas_call(
         body,
         out_shape=(f32(8, n), f32(16, 8, 128)),
-        in_specs=[SMEM] + [VM] * (3 + m),
+        in_specs=[SMEM] + [VM] * (2 + m + 5),
         out_specs=(VM, VM),
         scratch_shapes=[pltpu.VMEM((8, n), F32)],
         compiler_params=params(),
         name="group_sum",
-    )(table, w, deg, *parts, ret)
+    )(table, w, deg, *parts, own, partner, *chips)
 
 
 def finish(gathered, r, w, w2):
@@ -560,24 +568,29 @@
         arrived[k] = swap(x, k)
     left = left_of(own)
     right = right_of(own)
-    k_local, acc_local = local_first(own)
-
-    def cross(stage, after, held=()):
-        return cross_first(stage, table, own, [arrived[k] for k in stage], after, held)
-
-    k_a, row_a, *col_a = cross(STAGES[0], acc_local)
+
+    def cross(stage, after):
+        return cross_first(stage, table, own, [arrived[k] for k in stage], after)
+
+    ret = {}
+
+    def give_back(cols, stage):
+        for x, k in zip(cols, stage):
+            ret[k] = swap(x, k)
+
+    k_a, row_a, *col_a = cross(STAGES[0], table)
+    give_back(col_a, STAGES[0])
     for x, k in zip(gate(outgoing[5:], [row_a, arrived[3], arrived[7]]), STAGES[2]):
         arrived[k] = swap(x, k)
-    k_b, row_b, *col_b = cross(STAGES[1], row_a, col_a)
-    ret_near = []
-    for x, k in zip(col_b, STAGES[1] + STAGES[0]):
-        ret_near.append(swap(x, k))
+    k_b, row_b, *col_b = cross(STAGES[1], row_a)
+    give_back(col_b, STAGES[1])
     k_band, to_r, to_l, acc_band = band_first(left, own, right, [row_b])
     from_left, from_right = left_of(to_r), right_of(to_l)
     k_c, row_c, *col_c = cross(STAGES[2], acc_band)
-    ret = ret_near[2:] + ret_near[:2] + [swap(x, k) for x, k in zip(col_c, STAGES[2])]
+    give_back(col_c, STAGES[2])
+    k_local, acc_local = local_first(own, row_c)
     w_own, w_relay, w, deg, sums = combine(
-        table, targets, (acc_local, acc_band, from_left, from_right, row_a, row_b, row_c), ret
+        table, targets, (acc_local, acc_band, from_left, from_right, row_a, row_b, row_c), [ret[k] for k in SWAPS]
     )
     w_left = left_of(w)
     w_right = right_of(w)
@@ -585,9 +598,13 @@
     xw = [partner] + [swap(x, 2 * j + 2) for j, x in enumerate(relay(w_own, partner))]
     loc2 = local_second(k_local, w)
     col_r, rowl_b, rowo_b = band_second(k_band, w_left, w, w_right, loc2)
-    from_left2, from_right2 = left_of(col_r), right_of(rowl_b)
-    col_x, row_x = cross_second(table, (k_a, k_b, k_c), w, xw, sums, loc2, rowl_b, rowo_b, w_left)
-    w2, column = group_sum(table, w, deg, (loc2, rowo_b, row_x, from_left2, from_right2), trade(col_x))
+    from_left2 = left_of(col_r)
+    from_right2 = right_of(rowl_b)
+    x_own, x_relay, row_x = cross_second(table, (k_a, k_b, k_c), w, xw, sums, loc2, rowl_b, rowo_b, w_left)
+    x_partner = swap(x_relay, 1)
+    chips = [swap(x, 2 * j + 2) for j, x in enumerate(relay(x_own, x_partner))]
+    parts = (loc2, rowo_b, row_x, from_left2, from_right2)
+    w2, column = group_sum(table, w, deg, parts, x_own, x_partner, chips)
     return finish(trade(column, "dev"), targets, w, w2)
 
 

time: 144 us -> 148 us (1.028)
  starting transfers between devices: 60.5 us -> 63.8 us
  blocking collectives: 18.7 us -> 20.7 us
    ppermute x18 -> x22, starting transfers between devices: 25 us -> 31.2 us  [swap(): return lax.ppermute(x, 'group', [(i, i ^ k) for i in range(8)])]
    all_to_all x1 -> x0, starting transfers between devices: 5.91 us -> none  [trade(): return lax.all_to_all(x, axis, split_axis=0, concat_axis=0, tiled=True)]
    ppermute x4, waiting for transfers between devices: 4.26 us -> 0.01 us  [right_of(): return lax.ppermute(x, 'dev', to_left)]
    ppermute x18 -> x22, waiting for transfers between devices: 24.8 us -> 29 us  [swap(): return lax.ppermute(x, 'group', [(i, i ^ k) for i in range(8)])]
    ppermute x4, starting transfers between devices: 24.4 us -> 27.4 us  [left_of(): return lax.ppermute(x, 'dev', to_right)]
    all_to_all x1, blocking collectives: 18.7 us -> 20.7 us  [trade(): return lax.all_to_all(x, axis, split_axis=0, concat_axis=0, tiled=True)]
  transfers between devices with their start and end apart: 27 -> 30, of which waited for: 9 -> 7; matrix products, arithmetic and copies ran while one was open for 0% -> 0% of each run, Pallas kernels for 19% -> 18%
where the time goes in v3:
time: 148 us
  starting transfers between devices  63.8 us (43%)
  Pallas kernels  33.1 us (22%)
  waiting for transfers between devices  29.1 us (20%)
  blocking collectives  20.7 us (14%)
    ppermute x22, starting transfers between devices, swap(): return lax.ppermute(x, 'group', [(i, i ^ k) for i in range(8)])  31.2 us
    ppermute x22, waiting for transfers between devices, swap(): return lax.ppermute(x, 'group', [(i, i ^ k) for i in range(8)])  29 us
    ppermute x4, starting transfers between devices, left_of(): return lax.ppermute(x, 'dev', to_right)  27.4 us
    all_to_all x1, blocking collectives, trade(): return lax.all_to_all(x, axis, split_axis=0, concat_axis=0, tiled=True)  20.7 us
    pallas_call x1, Pallas kernels, band_first(): pl.pallas_call(body, out_shape=(vmem_bf16(nt, 2 * n, TILE), f32(16, n), f...  13.7 us
    pallas_call x1, Pallas kernels, local_first(): pl.pallas_call(body, out_shape=(vmem_bf16(nt, n, TILE), f32(16, n)), in_s...  5.81 us
    ppermute x4, starting transfers between devices, right_of(): return lax.ppermute(x, 'dev', to_left)  5.14 us
    pallas_call x1, Pallas kernels, band_second(): pl.pallas_call(body, out_shape=(f32(8, n), f32(8, n), f32(8, n)), in_spec...  3.76 us
  transfers between devices with their start and end apart: 30, of which 7 were waited for; matrix products, arithmetic and copies ran while one was open for 0% of the time, Pallas kernels for 18%

profile of v3, /device:TPU:0, one launch (start us, length us, event | category | flops | bytes accessed | tf_op | source)
XLA Modules:
  0.0 147.6 jit_solution(17537321255801829651)
XLA Ops:
  0.6 2.6 %prep.1 = (s32[32]{0:T(128)S(1)}, bf16[6,264,512]{2,1,0:T(8,128)(2,1)S(1)}, bf16[2,264,512]{2,1,0:T(8,128)(2,1)S(1)}, bf16[2,264,512]{2,1,0:T(8,128)(2,1)S(1)}, ...) custom-call(s32[8,8,2,16]{3,2,1,0:T(2,128)} %bitcast.1, ...), custom_call_target="tpu_custom_call" | custom-call | tf_op jit(solution)/shard_map/prep/pallas_call | solution.py:111
  3.2 1.3 collective-permute-start.1
  4.5 4.6 %collective-permute-start = (bf16[6,264,512]{2,1,0:T(8,128)(2,1)S(1)}, bf16[6,264,512]{2,1,0:T(8,128)(2,1)S(1)}, u32[]{:S(2)}, u32[]{:S(2)}) collective-permute-start(bf16[6,264,512]{2,1,0:T(8,128)(2,1)S(1)} %get-tuple-element.52.a_ref), channel_id=1, source_target_pairs={{0,1},{1,2},{2,3},{3,4},{4,5},{5,6},{6,7},{7,8},{8,9},{9,10},{10,1... | collective-permute-start | bytes 4866056 | tf_op jit(solution)/shard_map/ppermute | solution.py:557
  9.1 2.1 %collective-permute-start.2 = (bf16[2,264,512]{2,1,0:T(8,128)(2,1)S(1)}, bf16[2,264,512]{2,1,0:T(8,128)(2,1)S(1)}, u32[]{:S(2)}, u32[]{:S(2)}) collective-permute-start(bf16[2,264,512]{2,1,0:T(8,128)(2,1)S(1)} %get-tuple-element.53), channel_id=1, source_target_pairs={{0,32},{16,48},{32,0},{48,16},{64,96},{80,112},{96,64},{112,80},{1... | collective-permute-start | bytes 1622024 | tf_op jit(solution)/shard_map/ppermute | solution.py:560
  11.3 2.5 %collective-permute-start.3 = (bf16[2,264,512]{2,1,0:T(8,128)(2,1)S(1)}, bf16[2,264,512]{2,1,0:T(8,128)(2,1)S(1)}, u32[]{:S(2)}, u32[]{:S(2)}) collective-permute-start(bf16[2,264,512]{2,1,0:T(8,128)(2,1)S(1)} %get-tuple-element.54), channel_id=1, source_target_pairs={{0,96},{16,112},{32,64},{48,80},{64,32},{80,48},{96,0},{112,16},{1... | collective-permute-start | bytes 1622024 | tf_op jit(solution)/shard_map/ppermute | solution.py:560
  13.8 9.2 %collective-permute-done.2.refs_0_ = bf16[2,264,512]{2,1,0:T(8,128)(2,1)S(1)} collective-permute-done((bf16[2,264,512]{2,1,0:T(8,128)(2,1)S(1)}, bf16[2,264,512]{2,1,0:T(8,128)(2,1)S(1)}, u32[]{:S(2)}, u32[]{:S(2)}) %collective-permute-start.2) | collective-permute-done | bytes 540704 | tf_op jit(solution)/shard_map/ppermute | solution.py:560
  23.0 2.7 %collective-permute-done.3.refs_1_ = bf16[2,264,512]{2,1,0:T(8,128)(2,1)S(1)} collective-permute-done((bf16[2,264,512]{2,1,0:T(8,128)(2,1)S(1)}, bf16[2,264,512]{2,1,0:T(8,128)(2,1)S(1)}, u32[]{:S(2)}, u32[]{:S(2)}) %collective-permute-start.3) | collective-permute-done | bytes 540704 | tf_op jit(solution)/shard_map/ppermute | solution.py:560
  25.6 1.3 collective-permute-start.6
  27.0 1.0 shard_map.50
  28.0 9.2 %collective-permute-done.5.refs_0_.refs_3_ = bf16[2,264,512]{2,1,0:T(8,128)(2,1)S(1)} collective-permute-done((bf16[2,264,512]{2,1,0:T(8,128)(2,1)S(1)}, bf16[2,264,512]{2,1,0:T(8,128)(2,1)S(1)}, u32[]{:S(2)}, u32[]{:S(2)}) %collective-permute-start.5) | collective-permute-done | bytes 540704 | tf_op jit(solution)/shard_map/ppermute | solution.py:560
  37.3 4.0 %collective-permute-done.6.refs_1_.refs_4_ = bf16[2,264,512]{2,1,0:T(8,128)(2,1)S(1)} collective-permute-done((bf16[2,264,512]{2,1,0:T(8,128)(2,1)S(1)}, bf16[2,264,512]{2,1,0:T(8,128)(2,1)S(1)}, u32[]{:S(2)}, u32[]{:S(2)}) %collective-permute-start.6) | collective-permute-done | bytes 540704 | tf_op jit(solution)/shard_map/ppermute | solution.py:560
  41.3 0.7 collective-permute-start.7
  42.0 2.1 %collective-permute-start.8 = (bf16[2,264,512]{2,1,0:T(8,128)(2,1)S(1)}, bf16[2,264,512]{2,1,0:T(8,128)(2,1)S(1)}, u32[]{:S(2)}, u32[]{:S(2)}) collective-permute-start(bf16[2,264,512]{2,1,0:T(8,128)(2,1)S(1)} %get-tuple-element.64), channel_id=1, source_target_pairs={{0,80},{16,64},{32,112},{48,96},{64,16},{80,0},{96,48},{112,32},{1... | collective-permute-start | bytes 1622024 | tf_op jit(solution)/shard_map/ppermute | solution.py:560
  44.1 0.1 collective-permute-start.11
  44.2 1.0 shard_map.51
  45.2 13.7 %band_first.1 = (bf16[6,3072,256]{2,1,0:T(8,128)(2,1)S(1)}, f32[16,1536]{1,0:T(8,128)S(1)}, f32[16,1536]{1,0:T(8,128)S(1)}, f32[16,1536]{1,0:T(8,128)S(1)}) custom-call(bf16[6,264,512]{2,1,0:T(8,128)(2,1)S(1)} %collective-permute-done.l_ref, bf16[6,264,512]{2,1,0:T(8,128)(2,1)S(1)} %get-tuple-element.52.a_ref, ...), custom_call_target="tpu_custom_call" | custom-call | tf_op jit(solution)/shard_map/band_first/pallas_call | solution.py:216
  58.9 8.2 %collective-permute-start.9 = (f32[16,1536]{1,0:T(8,128)S(1)}, f32[16,1536]{1,0:T(8,128)S(1)}, u32[]{:S(2)}, u32[]{:S(2)}) collective-permute-start(f32[16,1536]{1,0:T(8,128)S(1)} %get-tuple-element.67), channel_id=1, source_target_pairs={{0,1},{1,2},{2,3},{3,4},{4,5},{5,6},{6,7},{7,8},{8,9},{9,10},{10,1... | collective-permute-start | bytes 294920 | tf_op jit(solution)/shard_map/ppermute | solution.py:557
  67.1 1.3 collective-permute-start.10
  68.4 2.0 %collective-permute-start.12 = (f32[2,16,256]{2,1,0:T(8,128)S(1)}, f32[2,16,256]{2,1,0:T(8,128)S(1)}, u32[]{:S(2)}, u32[]{:S(2)}) collective-permute-start(f32[2,16,256]{2,1,0:T(8,128)S(1)} %get-tuple-element.70), channel_id=1, source_target_pairs={{0,96},{16,112},{32,64},{48,80},{64,32},{80,48},{96,0},{112,16},{1... | collective-permute-start | bytes 98312 | tf_op jit(solution)/shard_map/ppermute | solution.py:560
  70.5 0.2 collective-permute-start.14
  70.7 1.2 shard_map.52
  71.9 1.8 %collective-permute-done.12.refs_8_ = f32[2,16,256]{2,1,0:T(8,128)S(1)} collective-permute-done((f32[2,16,256]{2,1,0:T(8,128)S(1)}, f32[2,16,256]{2,1,0:T(8,128)S(1)}, u32[]{:S(2)}, u32[]{:S(2)}) %collective-permute-start.12) | collective-permute-done | bytes 32800 | tf_op jit(solution)/shard_map/ppermute | solution.py:560
  73.6 2.9 %collective-permute-start.15 = (f32[2,16,256]{2,1,0:T(8,128)S(1)}, f32[2,16,256]{2,1,0:T(8,128)S(1)}, u32[]{:S(2)}, u32[]{:S(2)}) collective-permute-start(f32[2,16,256]{2,1,0:T(8,128)S(1)} %get-tuple-element.73), channel_id=1, source_target_pairs={{0,112},{16,96},{32,80},{48,64},{64,48},{80,32},{96,16},{112,0},{1... | collective-permute-start | bytes 98312 | tf_op jit(solution)/shard_map/ppermute | solution.py:560
  76.6 3.8 %collective-permute-start.16 = (f32[2,16,256]{2,1,0:T(8,128)S(1)}, f32[2,16,256]{2,1,0:T(8,128)S(1)}, u32[]{:S(2)}, u32[]{:S(2)}) collective-permute-start(f32[2,16,256]{2,1,0:T(8,128)S(1)} %get-tuple-element.74), channel_id=1, source_target_pairs={{0,64},{16,80},{32,96},{48,112},{64,0},{80,16},{96,32},{112,48},{1... | collective-permute-start | bytes 98312 | tf_op jit(solution)/shard_map/ppermute | solution.py:560
  80.4 5.8 %local_first.1 = (bf16[6,1536,256]{2,1,0:T(8,128)(2,1)S(1)}, f32[16,1536]{1,0:T(8,128)S(1)}) custom-call(bf16[6,264,512]{2,1,0:T(8,128)(2,1)S(1)} %get-tuple-element.52.a_ref, f32[16,1536]{1,0:T(8,128)S(1)} %get-tuple-element.65._.refs_6_), custom_call_target="tpu_custom_call" | custom-call | tf_op jit(solution)/shard_map/local_first/pallas_call | solution.py:167
  86.2 0.0 collective-permute-done.16.refs_12_
  86.3 0.8 combine.1
  87.2 0.2 collective-permute-start.20
  87.4 1.3 collective-permute-start.19
  88.7 5.1 %collective-permute-start.18 = (f32[8,1536]{1,0:T(8,128)S(1)}, f32[8,1536]{1,0:T(8,128)S(1)}, u32[]{:S(2)}, u32[]{:S(2)}) collective-permute-start(f32[8,1536]{1,0:T(8,128)S(1)} %get-tuple-element.76.w_ref), channel_id=1, source_target_pairs={{0,1},{1,2},{2,3},{3,4},{4,5},{5,6},{6,7},{7,8},{8,9},{9,10},{10,1... | collective-permute-start | bytes 147464 | tf_op jit(solution)/shard_map/ppermute | solution.py:557
  93.8 1.9 %collective-permute-start.21 = (f32[2,16,256]{2,1,0:T(8,128)S(1)}, f32[2,16,256]{2,1,0:T(8,128)S(1)}, u32[]{:S(2)}, u32[]{:S(2)}) collective-permute-start(f32[2,16,256]{2,1,0:T(8,128)S(1)} %get-tuple-element.88), channel_id=1, source_target_pairs={{0,32},{16,48},{32,0},{48,16},{64,96},{80,112},{96,64},{112,80},{1... | collective-permute-start | bytes 98312 | tf_op jit(solution)/shard_map/ppermute | solution.py:560
  95.7 2.1 %collective-permute-start.22 = (f32[2,16,256]{2,1,0:T(8,128)S(1)}, f32[2,16,256]{2,1,0:T(8,128)S(1)}, u32[]{:S(2)}, u32[]{:S(2)}) collective-permute-start(f32[2,16,256]{2,1,0:T(8,128)S(1)} %get-tuple-element.89), channel_id=1, source_target_pairs={{0,64},{16,80},{32,96},{48,112},{64,0},{80,16},{96,32},{112,48},{1... | collective-permute-start | bytes 98312 | tf_op jit(solution)/shard_map/ppermute | solution.py:560
  97.8 0.8 collective-permute-start.23
  98.6 0.7 local_second.1._.loc_ref.refs_0_
  99.3 0.0 collective-permute-done.18.wl_ref
  99.3 3.8 %band_second.1 = (f32[8,1536]{1,0:T(8,128)S(1)}, f32[8,1536]{1,0:T(8,128)S(1)}, f32[8,1536]{1,0:T(8,128)S(1)}) custom-call(bf16[6,3072,256]{2,1,0:T(8,128)(2,1)S(1)} %get-tuple-element.79.k_ref, f32[8,1536]{1,0:T(8,128)S(1)} %collective-permute-done.18.wl_ref, f32[8,1536]{1,0:T(8,128)S(1)} %get-tuple-element.76.w_ref, ...), custom_call_target="tpu_custom_call" | custom-call | tf_op jit(solution)/shard_map/band_second/pallas_call | solution.py:401
  103.2 0.7 cross_second.1
  103.9 3.6 %collective-permute-start.26 = (f32[5,16,256]{2,1,0:T(8,128)S(1)}, f32[5,16,256]{2,1,0:T(8,128)S(1)}, u32[]{:S(2)}, u32[]{:S(2)}) collective-permute-start(f32[5,16,256]{2,1,0:T(8,128)S(1)} %get-tuple-element.94), channel_id=1, source_target_pairs={{0,16},{16,0},{32,48},{48,32},{64,80},{80,64},{96,112},{112,96},{1... | collective-permute-start | bytes 245768 | tf_op jit(solution)/shard_map/ppermute | solution.py:560
  107.5 1.3 collective-permute-start.25
  108.8 9.4 %collective-permute-start.24 = (f32[8,1536]{1,0:T(8,128)S(1)}, f32[8,1536]{1,0:T(8,128)S(1)}, u32[]{:S(2)}, u32[]{:S(2)}) collective-permute-start(f32[8,1536]{1,0:T(8,128)S(1)} %get-tuple-element.92), channel_id=1, source_target_pairs={{0,1},{1,2},{2,3},{3,4},{4,5},{5,6},{6,7},{7,8},{8,9},{9,10},{10,1... | collective-permute-start | bytes 147464 | tf_op jit(solution)/shard_map/ppermute | solution.py:557
  118.2 0.1 collective-permute-start.27
  118.3 0.1 collective-permute-start.28
  118.4 4.6 %collective-permute-start.29 = (f32[3,16,256]{2,1,0:T(8,128)S(1)}, f32[3,16,256]{2,1,0:T(8,128)S(1)}, u32[]{:S(2)}, u32[]{:S(2)}) collective-permute-start(f32[3,16,256]{2,1,0:T(8,128)S(1)} %get-tuple-element.97), channel_id=1, source_target_pairs={{0,96},{16,112},{32,64},{48,80},{64,32},{80,48},{96,0},{112,16},{1... | collective-permute-start | bytes 147464 | tf_op jit(solution)/shard_map/ppermute | solution.py:560
  123.0 1.0 collective-permute-done.28.refs_8_
  124.1 1.0 collective-permute-done.29.refs_9_
  125.1 0.7 group_sum.1
  125.8 20.7 %all_to_all.5.g_ref = f32[16,8,128]{2,1,0:T(8,128)S(1)} all-to-all(f32[16,8,128]{2,1,0:T(8,128)S(1)} %get-tuple-element.98), channel_id=1, replica_groups=mesh['group'=8,'dev'=16] {'dev'}, dimensions={0} | all-to-all | bytes 131072 | tf_op jit(solution)/shard_map/all_to_all | solution.py:563
  146.5 1.1 finish.1
  (30 shorter events, 0.1 us)
Async XLA Ops:
  3.2 42.0 %collective-permute-start.1 = (bf16[6,264,512]{2,1,0:T(8,128)(2,1)S(1)}, bf16[6,264,512]{2,1,0:T(8,128)(2,1)S(1)}, u32[]{:S(2)}, u32[]{:S(2)}) collective-permute-start(bf16[6,264,512]{2,1,0:T(8,128)(2,1)S(1)} %get-tuple-element.52.a_ref), channel_id=1, source_target_pairs={{1,0},{2,1},{3,2},{4,3},{5,4},{6,5},{7,6},{8,7},{9,8},{10,9},{11,1... | collective-permute-start | bytes 4866056 | tf_op jit(solution)/shard_map/ppermute | solution.py:554
  4.5 40.7 %collective-permute-start = (bf16[6,264,512]{2,1,0:T(8,128)(2,1)S(1)}, bf16[6,264,512]{2,1,0:T(8,128)(2,1)S(1)}, u32[]{:S(2)}, u32[]{:S(2)}) collective-permute-start(bf16[6,264,512]{2,1,0:T(8,128)(2,1)S(1)} %get-tuple-element.52.a_ref), channel_id=1, source_target_pairs={{0,1},{1,2},{2,3},{3,4},{4,5},{5,6},{6,7},{7,8},{8,9},{9,10},{10,1... | collective-permute-start | bytes 4866056 | tf_op jit(solution)/shard_map/ppermute | solution.py:557
  9.1 13.8 %collective-permute-start.2 = (bf16[2,264,512]{2,1,0:T(8,128)(2,1)S(1)}, bf16[2,264,512]{2,1,0:T(8,128)(2,1)S(1)}, u32[]{:S(2)}, u32[]{:S(2)}) collective-permute-start(bf16[2,264,512]{2,1,0:T(8,128)(2,1)S(1)} %get-tuple-element.53), channel_id=1, source_target_pairs={{0,32},{16,48},{32,0},{48,16},{64,96},{80,112},{96,64},{112,80},{1... | collective-permute-start | bytes 1622024 | tf_op jit(solution)/shard_map/ppermute | solution.py:560
  11.3 14.4 %collective-permute-start.3 = (bf16[2,264,512]{2,1,0:T(8,128)(2,1)S(1)}, bf16[2,264,512]{2,1,0:T(8,128)(2,1)S(1)}, u32[]{:S(2)}, u32[]{:S(2)}) collective-permute-start(bf16[2,264,512]{2,1,0:T(8,128)(2,1)S(1)} %get-tuple-element.54), channel_id=1, source_target_pairs={{0,96},{16,112},{32,64},{48,80},{64,32},{80,48},{96,0},{112,16},{1... | collective-permute-start | bytes 1622024 | tf_op jit(solution)/shard_map/ppermute | solution.py:560
  13.8 13.2 %collective-permute-start.4 = (bf16[2,264,512]{2,1,0:T(8,128)(2,1)S(1)}, bf16[2,264,512]{2,1,0:T(8,128)(2,1)S(1)}, u32[]{:S(2)}, u32[]{:S(2)}) collective-permute-start(bf16[2,264,512]{2,1,0:T(8,128)(2,1)S(1)} %get-tuple-element.55), channel_id=1, source_target_pairs={{0,16},{16,0},{32,48},{48,32},{64,80},{80,64},{96,112},{112,96},{1... | collective-permute-start | bytes 1622024 | tf_op jit(solution)/shard_map/ppermute | solution.py:560
  23.0 14.3 %collective-permute-start.5 = (bf16[2,264,512]{2,1,0:T(8,128)(2,1)S(1)}, bf16[2,264,512]{2,1,0:T(8,128)(2,1)S(1)}, u32[]{:S(2)}, u32[]{:S(2)}) collective-permute-start(bf16[2,264,512]{2,1,0:T(8,128)(2,1)S(1)} %get-tuple-element.57), channel_id=1, source_target_pairs={{0,48},{16,32},{32,16},{48,0},{64,112},{80,96},{96,80},{112,64},{1... | collective-permute-start | bytes 1622024 | tf_op jit(solution)/shard_map/ppermute | solution.py:560
  25.6 15.7 %collective-permute-start.6 = (bf16[2,264,512]{2,1,0:T(8,128)(2,1)S(1)}, bf16[2,264,512]{2,1,0:T(8,128)(2,1)S(1)}, u32[]{:S(2)}, u32[]{:S(2)}) collective-permute-start(bf16[2,264,512]{2,1,0:T(8,128)(2,1)S(1)} %get-tuple-element.58), channel_id=1, source_target_pairs={{0,112},{16,96},{32,80},{48,64},{64,48},{80,32},{96,16},{112,0},{1... | collective-permute-start | bytes 1622024 | tf_op jit(solution)/shard_map/ppermute | solution.py:560
  41.3 29.2 %collective-permute-start.7 = (bf16[2,264,512]{2,1,0:T(8,128)(2,1)S(1)}, bf16[2,264,512]{2,1,0:T(8,128)(2,1)S(1)}, u32[]{:S(2)}, u32[]{:S(2)}) collective-permute-start(bf16[2,264,512]{2,1,0:T(8,128)(2,1)S(1)} %get-tuple-element.63), channel_id=1, source_target_pairs={{0,64},{16,80},{32,96},{48,112},{64,0},{80,16},{96,32},{112,48},{1... | collective-permute-start | bytes 1622024 | tf_op jit(solution)/shard_map/ppermute | solution.py:560
  42.0 28.4 %collective-permute-start.8 = (bf16[2,264,512]{2,1,0:T(8,128)(2,1)S(1)}, bf16[2,264,512]{2,1,0:T(8,128)(2,1)S(1)}, u32[]{:S(2)}, u32[]{:S(2)}) collective-permute-start(bf16[2,264,512]{2,1,0:T(8,128)(2,1)S(1)} %get-tuple-element.64), channel_id=1, source_target_pairs={{0,80},{16,64},{32,112},{48,96},{64,16},{80,0},{96,48},{112,32},{1... | collective-permute-start | bytes 1622024 | tf_op jit(solution)/shard_map/ppermute | solution.py:560
  44.1 24.3 %collective-permute-start.11 = (f32[2,16,256]{2,1,0:T(8,128)S(1)}, f32[2,16,256]{2,1,0:T(8,128)S(1)}, u32[]{:S(2)}, u32[]{:S(2)}) collective-permute-start(f32[2,16,256]{2,1,0:T(8,128)S(1)} %get-tuple-element.69), channel_id=1, source_target_pairs={{0,32},{16,48},{32,0},{48,16},{64,96},{80,112},{96,64},{112,80},{1... | collective-permute-start | bytes 98312 | tf_op jit(solution)/shard_map/ppermute | solution.py:560
  58.9 27.4 %copy-start = (f32[8,1536]{1,0:T(8,128)S(1)}, f32[8,1536]{1,0:T(8,128)}, u32[]{:S(2)}) copy-start(f32[8,1536]{1,0:T(8,128)} %r_ref.3) | copy-start | bytes 147460
  58.9 27.4 %collective-permute-start.9 = (f32[16,1536]{1,0:T(8,128)S(1)}, f32[16,1536]{1,0:T(8,128)S(1)}, u32[]{:S(2)}, u32[]{:S(2)}) collective-permute-start(f32[16,1536]{1,0:T(8,128)S(1)} %get-tuple-element.67), channel_id=1, source_target_pairs={{0,1},{1,2},{2,3},{3,4},{4,5},{5,6},{6,7},{7,8},{8,9},{9,10},{10,1... | collective-permute-start | bytes 294920 | tf_op jit(solution)/shard_map/ppermute | solution.py:557
  67.1 19.2 %collective-permute-start.10 = (f32[16,1536]{1,0:T(8,128)S(1)}, f32[16,1536]{1,0:T(8,128)S(1)}, u32[]{:S(2)}, u32[]{:S(2)}) collective-permute-start(f32[16,1536]{1,0:T(8,128)S(1)} %get-tuple-element.68), channel_id=1, source_target_pairs={{1,0},{2,1},{3,2},{4,3},{5,4},{6,5},{7,6},{8,7},{9,8},{10,9},{11,1... | collective-permute-start | bytes 294920 | tf_op jit(solution)/shard_map/ppermute | solution.py:554
  68.4 5.2 %collective-permute-start.12 = (f32[2,16,256]{2,1,0:T(8,128)S(1)}, f32[2,16,256]{2,1,0:T(8,128)S(1)}, u32[]{:S(2)}, u32[]{:S(2)}) collective-permute-start(f32[2,16,256]{2,1,0:T(8,128)S(1)} %get-tuple-element.70), channel_id=1, source_target_pairs={{0,96},{16,112},{32,64},{48,80},{64,32},{80,48},{96,0},{112,16},{1... | collective-permute-start | bytes 98312 | tf_op jit(solution)/shard_map/ppermute | solution.py:560
  70.4 6.1 %collective-permute-start.13 = (f32[2,16,256]{2,1,0:T(8,128)S(1)}, f32[2,16,256]{2,1,0:T(8,128)S(1)}, u32[]{:S(2)}, u32[]{:S(2)}) collective-permute-start(f32[2,16,256]{2,1,0:T(8,128)S(1)} %get-tuple-element.71), channel_id=1, source_target_pairs={{0,16},{16,0},{32,48},{48,32},{64,80},{80,64},{96,112},{112,96},{1... | collective-permute-start | bytes 98312 | tf_op jit(solution)/shard_map/ppermute | solution.py:560
  70.5 10.0 %collective-permute-start.14 = (f32[2,16,256]{2,1,0:T(8,128)S(1)}, f32[2,16,256]{2,1,0:T(8,128)S(1)}, u32[]{:S(2)}, u32[]{:S(2)}) collective-permute-start(f32[2,16,256]{2,1,0:T(8,128)S(1)} %get-tuple-element.72), channel_id=1, source_target_pairs={{0,48},{16,32},{32,16},{48,0},{64,112},{80,96},{96,80},{112,64},{1... | collective-permute-start | bytes 98312 | tf_op jit(solution)/shard_map/ppermute | solution.py:560
  73.6 12.6 %collective-permute-start.15 = (f32[2,16,256]{2,1,0:T(8,128)S(1)}, f32[2,16,256]{2,1,0:T(8,128)S(1)}, u32[]{:S(2)}, u32[]{:S(2)}) collective-permute-start(f32[2,16,256]{2,1,0:T(8,128)S(1)} %get-tuple-element.73), channel_id=1, source_target_pairs={{0,112},{16,96},{32,80},{48,64},{64,48},{80,32},{96,16},{112,0},{1... | collective-permute-start | bytes 98312 | tf_op jit(solution)/shard_map/ppermute | solution.py:560
  76.6 9.7 %collective-permute-start.16 = (f32[2,16,256]{2,1,0:T(8,128)S(1)}, f32[2,16,256]{2,1,0:T(8,128)S(1)}, u32[]{:S(2)}, u32[]{:S(2)}) collective-permute-start(f32[2,16,256]{2,1,0:T(8,128)S(1)} %get-tuple-element.74), channel_id=1, source_target_pairs={{0,64},{16,80},{32,96},{48,112},{64,0},{80,16},{96,32},{112,48},{1... | collective-permute-start | bytes 98312 | tf_op jit(solution)/shard_map/ppermute | solution.py:560
  80.4 5.9 %collective-permute-start.17 = (f32[2,16,256]{2,1,0:T(8,128)S(1)}, f32[2,16,256]{2,1,0:T(8,128)S(1)}, u32[]{:S(2)}, u32[]{:S(2)}) collective-permute-start(f32[2,16,256]{2,1,0:T(8,128)S(1)} %get-tuple-element.75), channel_id=1, source_target_pairs={{0,80},{16,64},{32,112},{48,96},{64,16},{80,0},{96,48},{112,32},{1... | collective-permute-start | bytes 98312 | tf_op jit(solution)/shard_map/ppermute | solution.py:560
  87.2 6.6 %collective-permute-start.20 = (f32[4,16,256]{2,1,0:T(8,128)S(1)}, f32[4,16,256]{2,1,0:T(8,128)S(1)}, u32[]{:S(2)}, u32[]{:S(2)}) collective-permute-start(f32[4,16,256]{2,1,0:T(8,128)S(1)} %get-tuple-element.86), channel_id=1, source_target_pairs={{0,16},{16,0},{32,48},{48,32},{64,80},{80,64},{96,112},{112,96},{1... | collective-permute-start | bytes 196616 | tf_op jit(solution)/shard_map/ppermute | solution.py:560
  87.4 12.0 %collective-permute-start.19 = (f32[8,1536]{1,0:T(8,128)S(1)}, f32[8,1536]{1,0:T(8,128)S(1)}, u32[]{:S(2)}, u32[]{:S(2)}) collective-permute-start(f32[8,1536]{1,0:T(8,128)S(1)} %get-tuple-element.76.w_ref), channel_id=1, source_target_pairs={{1,0},{2,1},{3,2},{4,3},{5,4},{6,5},{7,6},{8,7},{9,8},{10,9},{11,1... | collective-permute-start | bytes 147464 | tf_op jit(solution)/shard_map/ppermute | solution.py:554
  88.7 10.7 %collective-permute-start.18 = (f32[8,1536]{1,0:T(8,128)S(1)}, f32[8,1536]{1,0:T(8,128)S(1)}, u32[]{:S(2)}, u32[]{:S(2)}) collective-permute-start(f32[8,1536]{1,0:T(8,128)S(1)} %get-tuple-element.76.w_ref), channel_id=1, source_target_pairs={{0,1},{1,2},{2,3},{3,4},{4,5},{5,6},{6,7},{7,8},{8,9},{9,10},{10,1... | collective-permute-start | bytes 147464 | tf_op jit(solution)/shard_map/ppermute | solution.py:557
  93.8 9.3 %collective-permute-start.21 = (f32[2,16,256]{2,1,0:T(8,128)S(1)}, f32[2,16,256]{2,1,0:T(8,128)S(1)}, u32[]{:S(2)}, u32[]{:S(2)}) collective-permute-start(f32[2,16,256]{2,1,0:T(8,128)S(1)} %get-tuple-element.88), channel_id=1, source_target_pairs={{0,32},{16,48},{32,0},{48,16},{64,96},{80,112},{96,64},{112,80},{1... | collective-permute-start | bytes 98312 | tf_op jit(solution)/shard_map/ppermute | solution.py:560
  95.7 7.4 %collective-permute-start.22 = (f32[2,16,256]{2,1,0:T(8,128)S(1)}, f32[2,16,256]{2,1,0:T(8,128)S(1)}, u32[]{:S(2)}, u32[]{:S(2)}) collective-permute-start(f32[2,16,256]{2,1,0:T(8,128)S(1)} %get-tuple-element.89), channel_id=1, source_target_pairs={{0,64},{16,80},{32,96},{48,112},{64,0},{80,16},{96,32},{112,48},{1... | collective-permute-start | bytes 98312 | tf_op jit(solution)/shard_map/ppermute | solution.py:560
  97.8 5.4 %collective-permute-start.23 = (f32[2,16,256]{2,1,0:T(8,128)S(1)}, f32[2,16,256]{2,1,0:T(8,128)S(1)}, u32[]{:S(2)}, u32[]{:S(2)}) collective-permute-start(f32[2,16,256]{2,1,0:T(8,128)S(1)} %get-tuple-element.90), channel_id=1, source_target_pairs={{0,96},{16,112},{32,64},{48,80},{64,32},{80,48},{96,0},{112,16},{1... | collective-permute-start | bytes 98312 | tf_op jit(solution)/shard_map/ppermute | solution.py:560
  103.9 14.3 %collective-permute-start.26 = (f32[5,16,256]{2,1,0:T(8,128)S(1)}, f32[5,16,256]{2,1,0:T(8,128)S(1)}, u32[]{:S(2)}, u32[]{:S(2)}) collective-permute-start(f32[5,16,256]{2,1,0:T(8,128)S(1)} %get-tuple-element.94), channel_id=1, source_target_pairs={{0,16},{16,0},{32,48},{48,32},{64,80},{80,64},{96,112},{112,96},{1... | collective-permute-start | bytes 245768 | tf_op jit(solution)/shard_map/ppermute | solution.py:560
  107.5 15.6 %collective-permute-start.25 = (f32[8,1536]{1,0:T(8,128)S(1)}, f32[8,1536]{1,0:T(8,128)S(1)}, u32[]{:S(2)}, u32[]{:S(2)}) collective-permute-start(f32[8,1536]{1,0:T(8,128)S(1)} %get-tuple-element.85.rl_ref), channel_id=1, source_target_pairs={{1,0},{2,1},{3,2},{4,3},{5,4},{6,5},{7,6},{8,7},{9,8},{10,9},{11,1... | collective-permute-start | bytes 147464 | tf_op jit(solution)/shard_map/ppermute | solution.py:554
  108.8 14.3 %collective-permute-start.24 = (f32[8,1536]{1,0:T(8,128)S(1)}, f32[8,1536]{1,0:T(8,128)S(1)}, u32[]{:S(2)}, u32[]{:S(2)}) collective-permute-start(f32[8,1536]{1,0:T(8,128)S(1)} %get-tuple-element.92), channel_id=1, source_target_pairs={{0,1},{1,2},{2,3},{3,4},{4,5},{5,6},{6,7},{7,8},{8,9},{9,10},{10,1... | collective-permute-start | bytes 147464 | tf_op jit(solution)/shard_map/ppermute | solution.py:557
  118.2 4.8 %collective-permute-start.27 = (f32[3,16,256]{2,1,0:T(8,128)S(1)}, f32[3,16,256]{2,1,0:T(8,128)S(1)}, u32[]{:S(2)}, u32[]{:S(2)}) collective-permute-start(f32[3,16,256]{2,1,0:T(8,128)S(1)} %get-tuple-element.95), channel_id=1, source_target_pairs={{0,32},{16,48},{32,0},{48,16},{64,96},{80,112},{96,64},{112,80},{1... | collective-permute-start | bytes 147464 | tf_op jit(solution)/shard_map/ppermute | solution.py:560
  118.3 5.7 %collective-permute-start.28 = (f32[3,16,256]{2,1,0:T(8,128)S(1)}, f32[3,16,256]{2,1,0:T(8,128)S(1)}, u32[]{:S(2)}, u32[]{:S(2)}) collective-permute-start(f32[3,16,256]{2,1,0:T(8,128)S(1)} %get-tuple-element.96), channel_id=1, source_target_pairs={{0,64},{16,80},{32,96},{48,112},{64,0},{80,16},{96,32},{112,48},{1... | collective-permute-start | bytes 147464 | tf_op jit(solution)/shard_map/ppermute | solution.py:560
  118.4 6.7 %collective-permute-start.29 = (f32[3,16,256]{2,1,0:T(8,128)S(1)}, f32[3,16,256]{2,1,0:T(8,128)S(1)}, u32[]{:S(2)}, u32[]{:S(2)}) collective-permute-start(f32[3,16,256]{2,1,0:T(8,128)S(1)} %get-tuple-element.97), channel_id=1, source_target_pairs={{0,96},{16,112},{32,64},{48,80},{64,32},{80,48},{96,0},{112,16},{1... | collective-permute-start | bytes 147464 | tf_op jit(solution)/shard_map/ppermute | solution.py:560

commit v4 on v2

--- a/solution.py
+++ b/solution.py
@@ -230,17 +230,16 @@
     )(left, own, right, *after)
 
 
-def cross_first(ks, table, own, tiles, after, held=()):
+def cross_first(ks, table, own, tiles, after):
     nt, _, d = own.shape
     n = nt * TILE
     m = len(ks)
     slots = 2 * m
-    p = len(held)
 
     def body(q_ref, a_ref, _, *refs):
         tile_refs = refs[:m]
-        k_ref, row_ref, *cols = refs[m + p : 2 * m + p + 2]
-        buf, jobs, sems, na, va, acc, nb, col = refs[2 * m + 2 * p + 2 :]
+        k_ref, row_ref, *cols = refs[m : 2 * m + 2]
+        buf, jobs, sems, na, va, acc, nb, col = refs[2 * m + 2 :]
         g = lax.axis_index("group")
         count = jnp.int32(0)
         for i, k in enumerate(ks):
@@ -259,31 +258,38 @@
             va[:, s] = rhs_ones(a_ref[i, TILE:, :], 1.0)
         acc[...] = jnp.zeros_like(acc)
 
-        def step(j, carry):
+        def arrive(j, carry):
             pltpu.make_async_copy(tile_refs[0].at[0], buf.at[j], sems.at[j]).wait()
-            b = buf[j, 0:TILE, :]
-            nb[...] = col_norms(b).T[0:8]
-            b = b * jnp.asarray(-2.0, BF16)
-            vb = rhs_ones(buf[j, TILE:, :], 1.0)
-            for i in range(nt):
-                c = slice(i * TILE, (i + 1) * TILE)
-                k_ref[j, c, :] = kernel_tile(a_ref[i, 0:TILE, :], b, na[c, :], nb[0:1, :])
-            k = k_ref[j]
-            col[jobs[j]] = fold_ones(mm(va[...], k, NN))
-            acc[...] += mm(vb, k, NT)
             return carry
 
-        lax.fori_loop(0, count, step, 0)
+        lax.fori_loop(0, count, arrive, 0)
+
+        def step(pair, carry):
+            for u in range(2):
+                j = jnp.minimum(2 * pair + u, count - 1)
+                live = (2 * pair + u < count).astype(F32)
+                b = buf[j, 0:TILE, :]
+                nb[u] = col_norms(b).T[0:8]
+                b = b * jnp.asarray(-2.0, BF16)
+                vb = rhs_ones(buf[j, TILE:, :].astype(F32) * live, live)
+                for i in range(nt):
+                    c = slice(i * TILE, (i + 1) * TILE)
+                    k_ref[j, c, :] = kernel_tile(a_ref[i, 0:TILE, :], b, na[c, :], nb[u, 0:1, :])
+                k = k_ref[j]
+                col[jobs[j]] = fold_ones(mm(va[...], k, NN))
+                acc[...] += mm(vb, k, NT)
+            return carry
+
+        lax.fori_loop(0, (count + 1) // 2, step, 0)
         row_ref[...] = fold_ones(acc[...])
         for i, out in enumerate(cols):
             out[...] = col[2 * i : 2 * i + 2]
 
     return pl.pallas_call(
         body,
-        out_shape=[vmem_bf16(slots, n, TILE), f32(16, n)] + [f32(2, 16, TILE)] * (m + p),
-        in_specs=[SMEM, VM, ANY] + [ANY] * m + [VM] * p,
-        out_specs=[VM] * (2 + m + p),
-        input_output_aliases={3 + m + i: 2 + m + i for i in range(p)},
+        out_shape=[vmem_bf16(slots, n, TILE), f32(16, n)] + [f32(2, 16, TILE)] * m,
+        in_specs=[SMEM, VM, ANY] + [ANY] * m,
+        out_specs=[VM] * (2 + m),
         scratch_shapes=[
             pltpu.VMEM((slots, TILE + EXTRA, d), BF16),
             pltpu.SMEM((slots,), jnp.int32),
@@ -291,11 +297,11 @@
             pltpu.VMEM((n, 128), F32),
             pltpu.VMEM((32, n), BF16),
             pltpu.VMEM((32, n), F32),
-            pltpu.VMEM((8, TILE), F32),
+            pltpu.VMEM((2, 8, TILE), F32),
             pltpu.VMEM((slots, 16, TILE), F32),
         ],
         compiler_params=params(),
-    )(table, own, after, *tiles, *held)
+    )(table, own, after, *tiles)
 
 
 def combine(table, r, parts, ret):
@@ -433,16 +439,19 @@
 
                     count = count + live.astype(jnp.int32)
 
-            def step(j, carry, k_ref=k_ref):
-                slot = jobs[j]
-                h, c = slot >> 1, slot & 1
-                rows = pl.ds(pl.multiple_of(c * 8, 8), 8)
-                k = k_ref[j]
-                col_ref[h, rows, :] = fold(mm(va[...], k, NN))
-                acc[...] += mm(split(xw_ref[h, rows, :]), k, NT)
+            def step(pair, carry, k_ref=k_ref, count=count):
+                for u in range(2):
+                    j = jnp.minimum(2 * pair + u, count - 1)
+                    live = (2 * pair + u < count).astype(F32)
+                    slot = jobs[j]
+                    h, c = slot >> 1, slot & 1
+                    rows = pl.ds(pl.multiple_of(c * 8, 8), 8)
+                    k = k_ref[j]
+                    col_ref[h, rows, :] = fold(mm(va[...], k, NN))
+                    acc[...] += mm(split(xw_ref[h, rows, :] * live), k, NT)
                 return carry
 
-            lax.fori_loop(0, count, step, 0)
+            lax.fori_loop(0, (count + 1) // 2, step, 0)
         row = fold(acc[...])
         row_ref[...] = row
         pairs = w_ref[...] * (0.5 * loc_ref[...] + ro_ref[...] + row) + wl_ref[...] * rl_ref[...]
@@ -562,22 +571,27 @@
     right = right_of(own)
     k_local, acc_local = local_first(own)
 
-    def cross(stage, after, held=()):
-        return cross_first(stage, table, own, [arrived[k] for k in stage], after, held)
+    def cross(stage, after):
+        return cross_first(stage, table, own, [arrived[k] for k in stage], after)
+
+    ret = {}
+
+    def give_back(cols, stage):
+        for x, k in zip(cols, stage):
+            ret[k] = swap(x, k)
 
     k_a, row_a, *col_a = cross(STAGES[0], acc_local)
+    give_back(col_a, STAGES[0])
     for x, k in zip(gate(outgoing[5:], [row_a, arrived[3], arrived[7]]), STAGES[2]):
         arrived[k] = swap(x, k)
-    k_b, row_b, *col_b = cross(STAGES[1], row_a, col_a)
-    ret_near = []
-    for x, k in zip(col_b, STAGES[1] + STAGES[0]):
-        ret_near.append(swap(x, k))
+    k_b, row_b, *col_b = cross(STAGES[1], row_a)
+    give_back(col_b, STAGES[1])
     k_band, to_r, to_l, acc_band = band_first(left, own, right, [row_b])
     from_left, from_right = left_of(to_r), right_of(to_l)
     k_c, row_c, *col_c = cross(STAGES[2], acc_band)
-    ret = ret_near[2:] + ret_near[:2] + [swap(x, k) for x, k in zip(col_c, STAGES[2])]
+    give_back(col_c, STAGES[2])
     w_own, w_relay, w, deg, sums = combine(
-        table, targets, (acc_local, acc_band, from_left, from_right, row_a, row_b, row_c), ret
+        table, targets, (acc_local, acc_band, from_left, from_right, row_a, row_b, row_c), [ret[k] for k in SWAPS]
     )
     w_left = left_of(w)
     w_right = right_of(w)
@@ -585,7 +599,8 @@
     xw = [partner] + [swap(x, 2 * j + 2) for j, x in enumerate(relay(w_own, partner))]
     loc2 = local_second(k_local, w)
     col_r, rowl_b, rowo_b = band_second(k_band, w_left, w, w_right, loc2)
-    from_left2, from_right2 = left_of(col_r), right_of(rowl_b)
+    from_left2 = left_of(col_r)
+    from_right2 = right_of(rowl_b)
     col_x, row_x = cross_second(table, (k_a, k_b, k_c), w, xw, sums, loc2, rowl_b, rowo_b, w_left)
     w2, column = group_sum(table, w, deg, (loc2, rowo_b, row_x, from_left2, from_right2), trade(col_x))
     return finish(trade(column, "dev"), targets, w, w2)

time: 144 us -> 143 us (level)
  starting transfers between devices: 60.5 us -> 57.7 us
    ppermute x18, starting transfers between devices: 25 us -> 23 us  [swap(): return lax.ppermute(x, 'group', [(i, i ^ k) for i in range(8)])]
    all_to_all x1, starting transfers between devices: 5.91 us -> 4.33 us  [trade(): return lax.all_to_all(x, axis, split_axis=0, concat_axis=0, tiled=True)]
where the time goes in v4:
time: 143 us; the launch traced here: 142 us
  starting transfers between devices  57.7 us (40%)
  Pallas kernels  34 us (24%)
  waiting for transfers between devices  30.7 us (21%)
  blocking collectives  18.8 us (13%)
    ppermute x18, waiting for transfers between devices, swap(): return lax.ppermute(x, 'group', [(i, i ^ k) for i in range(8)])  26 us
    ppermute x4, starting transfers between devices, left_of(): return lax.ppermute(x, 'dev', to_right)  25.2 us
    ppermute x18, starting transfers between devices, swap(): return lax.ppermute(x, 'group', [(i, i ^ k) for i in range(8)])  23 us
    all_to_all x1, blocking collectives, trade(): return lax.all_to_all(x, axis, split_axis=0, concat_axis=0, tiled=True)  18.8 us
    pallas_call x1, Pallas kernels, band_first(): pl.pallas_call(body, out_shape=(vmem_bf16(nt, 2 * n, TILE), f32(16, n), f...  13.8 us
    pallas_call x1, Pallas kernels, local_first(): pl.pallas_call(body, out_shape=(vmem_bf16(nt, n, TILE), f32(16, n)), in_s...  5.86 us
    ppermute x4, starting transfers between devices, right_of(): return lax.ppermute(x, 'dev', to_left)  5.17 us
    all_to_all x1, starting transfers between devices, trade(): return lax.all_to_all(x, axis, split_axis=0, concat_axis=0, tiled=True)  4.33 us
  transfers between devices with their start and end apart: 27, of which 9 were waited for; matrix products, arithmetic and copies ran while one was open for 0% of the time, Pallas kernels for 19%

profile of v4, /device:TPU:0, one launch (start us, length us, event | category | flops | bytes accessed | tf_op | source)
XLA Modules:
  0.0 142.1 jit_solution(5474683199577301747)
XLA Ops:
  0.6 2.6 %prep.1 = (s32[32]{0:T(128)S(1)}, bf16[6,264,512]{2,1,0:T(8,128)(2,1)S(1)}, bf16[2,264,512]{2,1,0:T(8,128)(2,1)S(1)}, bf16[2,264,512]{2,1,0:T(8,128)(2,1)S(1)}, ...) custom-call(s32[8,8,2,16]{3,2,1,0:T(2,128)} %bitcast.1, ...), custom_call_target="tpu_custom_call" | custom-call | tf_op jit(solution)/shard_map/prep/pallas_call | solution.py:111
  3.2 1.3 collective-permute-start.1
  4.5 4.6 %collective-permute-start = (bf16[6,264,512]{2,1,0:T(8,128)(2,1)S(1)}, bf16[6,264,512]{2,1,0:T(8,128)(2,1)S(1)}, u32[]{:S(2)}, u32[]{:S(2)}) collective-permute-start(bf16[6,264,512]{2,1,0:T(8,128)(2,1)S(1)} %get-tuple-element.48.a_ref), channel_id=1, source_target_pairs={{0,1},{1,2},{2,3},{3,4},{4,5},{5,6},{6,7},{7,8},{8,9},{9,10},{10,1... | collective-permute-start | bytes 4866056 | tf_op jit(solution)/shard_map/ppermute | solution.py:558
  9.1 2.1 %collective-permute-start.2 = (bf16[2,264,512]{2,1,0:T(8,128)(2,1)S(1)}, bf16[2,264,512]{2,1,0:T(8,128)(2,1)S(1)}, u32[]{:S(2)}, u32[]{:S(2)}) collective-permute-start(bf16[2,264,512]{2,1,0:T(8,128)(2,1)S(1)} %get-tuple-element.50), channel_id=1, source_target_pairs={{0,32},{16,48},{32,0},{48,16},{64,96},{80,112},{96,64},{112,80},{1... | collective-permute-start | bytes 1622024 | tf_op jit(solution)/shard_map/ppermute | solution.py:561
  11.3 2.5 %collective-permute-start.3 = (bf16[2,264,512]{2,1,0:T(8,128)(2,1)S(1)}, bf16[2,264,512]{2,1,0:T(8,128)(2,1)S(1)}, u32[]{:S(2)}, u32[]{:S(2)}) collective-permute-start(bf16[2,264,512]{2,1,0:T(8,128)(2,1)S(1)} %get-tuple-element.51), channel_id=1, source_target_pairs={{0,96},{16,112},{32,64},{48,80},{64,32},{80,48},{96,0},{112,16},{1... | collective-permute-start | bytes 1622024 | tf_op jit(solution)/shard_map/ppermute | solution.py:561
  13.8 9.2 %collective-permute-done.2.refs_0_ = bf16[2,264,512]{2,1,0:T(8,128)(2,1)S(1)} collective-permute-done((bf16[2,264,512]{2,1,0:T(8,128)(2,1)S(1)}, bf16[2,264,512]{2,1,0:T(8,128)(2,1)S(1)}, u32[]{:S(2)}, u32[]{:S(2)}) %collective-permute-start.2) | collective-permute-done | bytes 540704 | tf_op jit(solution)/shard_map/ppermute | solution.py:561
  23.0 2.7 %collective-permute-done.3.refs_1_ = bf16[2,264,512]{2,1,0:T(8,128)(2,1)S(1)} collective-permute-done((bf16[2,264,512]{2,1,0:T(8,128)(2,1)S(1)}, bf16[2,264,512]{2,1,0:T(8,128)(2,1)S(1)}, u32[]{:S(2)}, u32[]{:S(2)}) %collective-permute-start.3) | collective-permute-done | bytes 540704 | tf_op jit(solution)/shard_map/ppermute | solution.py:561
  25.6 1.3 collective-permute-start.6
  27.0 5.9 %local_first.1 = (bf16[6,1536,256]{2,1,0:T(8,128)(2,1)S(1)}, f32[16,1536]{1,0:T(8,128)S(1)}) custom-call(bf16[6,264,512]{2,1,0:T(8,128)(2,1)S(1)} %get-tuple-element.48.a_ref), custom_call_target="tpu_custom_call" | custom-call | tf_op jit(solution)/shard_map/local_first/pallas_call | solution.py:167
  32.8 1.1 shard_map.50
  33.9 3.3 %collective-permute-done.5.refs_0_.refs_3_ = bf16[2,264,512]{2,1,0:T(8,128)(2,1)S(1)} collective-permute-done((bf16[2,264,512]{2,1,0:T(8,128)(2,1)S(1)}, bf16[2,264,512]{2,1,0:T(8,128)(2,1)S(1)}, u32[]{:S(2)}, u32[]{:S(2)}) %collective-permute-start.5) | collective-permute-done | bytes 540704 | tf_op jit(solution)/shard_map/ppermute | solution.py:561
  37.3 4.0 %collective-permute-done.6.refs_1_.refs_4_ = bf16[2,264,512]{2,1,0:T(8,128)(2,1)S(1)} collective-permute-done((bf16[2,264,512]{2,1,0:T(8,128)(2,1)S(1)}, bf16[2,264,512]{2,1,0:T(8,128)(2,1)S(1)}, u32[]{:S(2)}, u32[]{:S(2)}) %collective-permute-start.6) | collective-permute-done | bytes 540704 | tf_op jit(solution)/shard_map/ppermute | solution.py:561
  41.3 0.7 collective-permute-start.9
  42.0 2.1 %collective-permute-start.10 = (bf16[2,264,512]{2,1,0:T(8,128)(2,1)S(1)}, bf16[2,264,512]{2,1,0:T(8,128)(2,1)S(1)}, u32[]{:S(2)}, u32[]{:S(2)}) collective-permute-start(bf16[2,264,512]{2,1,0:T(8,128)(2,1)S(1)} %get-tuple-element.63), channel_id=1, source_target_pairs={{0,80},{16,64},{32,112},{48,96},{64,16},{80,0},{96,48},{112,32},{1... | collective-permute-start | bytes 1622024 | tf_op jit(solution)/shard_map/ppermute | solution.py:561
  44.1 0.8 collective-permute-start.11
  44.9 1.2 shard_map.51
  46.1 0.0 copy-start
  46.1 13.8 %band_first.1 = (bf16[6,3072,256]{2,1,0:T(8,128)(2,1)S(1)}, f32[16,1536]{1,0:T(8,128)S(1)}, f32[16,1536]{1,0:T(8,128)S(1)}, f32[16,1536]{1,0:T(8,128)S(1)}) custom-call(bf16[6,264,512]{2,1,0:T(8,128)(2,1)S(1)} %collective-permute-done.l_ref, bf16[6,264,512]{2,1,0:T(8,128)(2,1)S(1)} %get-tuple-element.48.a_ref, ...), custom_call_target="tpu_custom_call" | custom-call | tf_op jit(solution)/shard_map/band_first/pallas_call | solution.py:216
  59.9 7.1 %collective-permute-start.7 = (f32[16,1536]{1,0:T(8,128)S(1)}, f32[16,1536]{1,0:T(8,128)S(1)}, u32[]{:S(2)}, u32[]{:S(2)}) collective-permute-start(f32[16,1536]{1,0:T(8,128)S(1)} %get-tuple-element.58), channel_id=1, source_target_pairs={{0,1},{1,2},{2,3},{3,4},{4,5},{5,6},{6,7},{7,8},{8,9},{9,10},{10,1... | collective-permute-start | bytes 294920 | tf_op jit(solution)/shard_map/ppermute | solution.py:558
  67.1 1.3 collective-permute-start.8
  68.4 2.0 %collective-permute-start.12 = (f32[2,16,256]{2,1,0:T(8,128)S(1)}, f32[2,16,256]{2,1,0:T(8,128)S(1)}, u32[]{:S(2)}, u32[]{:S(2)}) collective-permute-start(f32[2,16,256]{2,1,0:T(8,128)S(1)} %get-tuple-element.66), channel_id=1, source_target_pairs={{0,96},{16,112},{32,64},{48,80},{64,32},{80,48},{96,0},{112,16},{1... | collective-permute-start | bytes 98312 | tf_op jit(solution)/shard_map/ppermute | solution.py:561
  70.4 0.2 collective-permute-start.14
  70.6 1.0 shard_map.52
  71.6 1.9 %collective-permute-done.12.refs_8_ = f32[2,16,256]{2,1,0:T(8,128)S(1)} collective-permute-done((f32[2,16,256]{2,1,0:T(8,128)S(1)}, f32[2,16,256]{2,1,0:T(8,128)S(1)}, u32[]{:S(2)}, u32[]{:S(2)}) %collective-permute-start.12) | collective-permute-done | bytes 32800 | tf_op jit(solution)/shard_map/ppermute | solution.py:561
  73.6 2.7 %collective-permute-start.15 = (f32[2,16,256]{2,1,0:T(8,128)S(1)}, f32[2,16,256]{2,1,0:T(8,128)S(1)}, u32[]{:S(2)}, u32[]{:S(2)}) collective-permute-start(f32[2,16,256]{2,1,0:T(8,128)S(1)} %get-tuple-element.69), channel_id=1, source_target_pairs={{0,112},{16,96},{32,80},{48,64},{64,48},{80,32},{96,16},{112,0},{1... | collective-permute-start | bytes 98312 | tf_op jit(solution)/shard_map/ppermute | solution.py:561
  76.3 3.7 %collective-permute-start.16 = (f32[2,16,256]{2,1,0:T(8,128)S(1)}, f32[2,16,256]{2,1,0:T(8,128)S(1)}, u32[]{:S(2)}, u32[]{:S(2)}) collective-permute-start(f32[2,16,256]{2,1,0:T(8,128)S(1)} %get-tuple-element.70), channel_id=1, source_target_pairs={{0,64},{16,80},{32,96},{48,112},{64,0},{80,16},{96,32},{112,48},{1... | collective-permute-start | bytes 98312 | tf_op jit(solution)/shard_map/ppermute | solution.py:561
  80.0 1.9 %collective-permute-done.16.refs_12_ = f32[2,16,256]{2,1,0:T(8,128)S(1)} collective-permute-done((f32[2,16,256]{2,1,0:T(8,128)S(1)}, f32[2,16,256]{2,1,0:T(8,128)S(1)}, u32[]{:S(2)}, u32[]{:S(2)}) %collective-permute-start.16) | collective-permute-done | bytes 32800 | tf_op jit(solution)/shard_map/ppermute | solution.py:561
  81.9 3.0 %collective-permute-done.17.refs_13_ = f32[2,16,256]{2,1,0:T(8,128)S(1)} collective-permute-done((f32[2,16,256]{2,1,0:T(8,128)S(1)}, f32[2,16,256]{2,1,0:T(8,128)S(1)}, u32[]{:S(2)}, u32[]{:S(2)}) %collective-permute-start.17) | collective-permute-done | bytes 32800 | tf_op jit(solution)/shard_map/ppermute | solution.py:561
  84.8 0.8 combine.1
  85.7 0.0 collective-permute-start.20
  85.7 1.3 collective-permute-start.19
  87.0 5.3 %collective-permute-start.18 = (f32[8,1536]{1,0:T(8,128)S(1)}, f32[8,1536]{1,0:T(8,128)S(1)}, u32[]{:S(2)}, u32[]{:S(2)}) collective-permute-start(f32[8,1536]{1,0:T(8,128)S(1)} %get-tuple-element.72.w_ref), channel_id=1, source_target_pairs={{0,1},{1,2},{2,3},{3,4},{4,5},{5,6},{6,7},{7,8},{8,9},{9,10},{10,1... | collective-permute-start | bytes 147464 | tf_op jit(solution)/shard_map/ppermute | solution.py:558
  92.3 0.2 collective-permute-start.21
  92.5 2.2 %collective-permute-start.22 = (f32[2,16,256]{2,1,0:T(8,128)S(1)}, f32[2,16,256]{2,1,0:T(8,128)S(1)}, u32[]{:S(2)}, u32[]{:S(2)}) collective-permute-start(f32[2,16,256]{2,1,0:T(8,128)S(1)} %get-tuple-element.85), channel_id=1, source_target_pairs={{0,64},{16,80},{32,96},{48,112},{64,0},{80,16},{96,32},{112,48},{1... | collective-permute-start | bytes 98312 | tf_op jit(solution)/shard_map/ppermute | solution.py:561
  94.8 2.3 %collective-permute-start.23 = (f32[2,16,256]{2,1,0:T(8,128)S(1)}, f32[2,16,256]{2,1,0:T(8,128)S(1)}, u32[]{:S(2)}, u32[]{:S(2)}) collective-permute-start(f32[2,16,256]{2,1,0:T(8,128)S(1)} %get-tuple-element.86), channel_id=1, source_target_pairs={{0,96},{16,112},{32,64},{48,80},{64,32},{80,48},{96,0},{112,16},{1... | collective-permute-start | bytes 98312 | tf_op jit(solution)/shard_map/ppermute | solution.py:561
  97.1 0.7 local_second.1._.loc_ref.refs_0_
  97.9 0.0 collective-permute-done.18.wl_ref
  97.9 3.8 %band_second.1 = (f32[8,1536]{1,0:T(8,128)S(1)}, f32[8,1536]{1,0:T(8,128)S(1)}, f32[8,1536]{1,0:T(8,128)S(1)}) custom-call(bf16[6,3072,256]{2,1,0:T(8,128)(2,1)S(1)} %get-tuple-element.75.k_ref, f32[8,1536]{1,0:T(8,128)S(1)} %collective-permute-done.18.wl_ref, f32[8,1536]{1,0:T(8,128)S(1)} %get-tuple-element.72.w_ref, ...), custom_call_target="tpu_custom_call" | custom-call | tf_op jit(solution)/shard_map/band_second/pallas_call | solution.py:405
  101.7 0.0 collective-permute-done.22.refs_2_
  101.7 1.4 cross_second.1
  103.1 4.3 %all-to-all-start = ((f32[8,24,256]{2,1,0:T(8,128)}), f32[8,24,256]{2,1,0:T(8,128)S(1)}, u32[]{:S(2)}, u32[]{:S(2)}) async-start(f32[8,24,256]{2,1,0:T(8,128)} %get-tuple-element.89), calls=%async_computation | async-start | bytes 393216 | tf_op jit(solution)/shard_map/all_to_all | solution.py:564
  107.4 8.1 %collective-permute-start.24 = (f32[8,1536]{1,0:T(8,128)S(1)}, f32[8,1536]{1,0:T(8,128)S(1)}, u32[]{:S(2)}, u32[]{:S(2)}) collective-permute-start(f32[8,1536]{1,0:T(8,128)S(1)} %get-tuple-element.88), channel_id=1, source_target_pairs={{0,1},{1,2},{2,3},{3,4},{4,5},{5,6},{6,7},{7,8},{8,9},{9,10},{10,1... | collective-permute-start | bytes 147464 | tf_op jit(solution)/shard_map/ppermute | solution.py:558
  115.5 1.3 collective-permute-start.25
  116.8 0.4 collective-permute-done.24.refs_3_
  117.2 4.3 %collective-permute-done.25.refs_4_ = f32[8,1536]{1,0:T(8,128)S(1)} collective-permute-done((f32[8,1536]{1,0:T(8,128)S(1)}, f32[8,1536]{1,0:T(8,128)S(1)}, u32[]{:S(2)}, u32[]{:S(2)}) %collective-permute-start.25) | collective-permute-done | bytes 49184 | tf_op jit(solution)/shard_map/ppermute | solution.py:555
  121.5 0.7 group_sum.1
  122.2 18.8 %all_to_all.10.g_ref = f32[16,8,128]{2,1,0:T(8,128)S(1)} all-to-all(f32[16,8,128]{2,1,0:T(8,128)S(1)} %get-tuple-element.90), channel_id=1, replica_groups=mesh['group'=8,'dev'=16] {'dev'}, dimensions={0} | all-to-all | bytes 131072 | tf_op jit(solution)/shard_map/all_to_all | solution.py:564
  141.0 1.1 finish.1
  (23 shorter events, 0.1 us)
Async XLA Ops:
  3.2 42.9 %collective-permute-start.1 = (bf16[6,264,512]{2,1,0:T(8,128)(2,1)S(1)}, bf16[6,264,512]{2,1,0:T(8,128)(2,1)S(1)}, u32[]{:S(2)}, u32[]{:S(2)}) collective-permute-start(bf16[6,264,512]{2,1,0:T(8,128)(2,1)S(1)} %get-tuple-element.48.a_ref), channel_id=1, source_target_pairs={{1,0},{2,1},{3,2},{4,3},{5,4},{6,5},{7,6},{8,7},{9,8},{10,9},{11,1... | collective-permute-start | bytes 4866056 | tf_op jit(solution)/shard_map/ppermute | solution.py:555
  4.5 41.6 %collective-permute-start = (bf16[6,264,512]{2,1,0:T(8,128)(2,1)S(1)}, bf16[6,264,512]{2,1,0:T(8,128)(2,1)S(1)}, u32[]{:S(2)}, u32[]{:S(2)}) collective-permute-start(bf16[6,264,512]{2,1,0:T(8,128)(2,1)S(1)} %get-tuple-element.48.a_ref), channel_id=1, source_target_pairs={{0,1},{1,2},{2,3},{3,4},{4,5},{5,6},{6,7},{7,8},{8,9},{9,10},{10,1... | collective-permute-start | bytes 4866056 | tf_op jit(solution)/shard_map/ppermute | solution.py:558
  9.1 13.8 %collective-permute-start.2 = (bf16[2,264,512]{2,1,0:T(8,128)(2,1)S(1)}, bf16[2,264,512]{2,1,0:T(8,128)(2,1)S(1)}, u32[]{:S(2)}, u32[]{:S(2)}) collective-permute-start(bf16[2,264,512]{2,1,0:T(8,128)(2,1)S(1)} %get-tuple-element.50), channel_id=1, source_target_pairs={{0,32},{16,48},{32,0},{48,16},{64,96},{80,112},{96,64},{112,80},{1... | collective-permute-start | bytes 1622024 | tf_op jit(solution)/shard_map/ppermute | solution.py:561
  11.3 14.4 %collective-permute-start.3 = (bf16[2,264,512]{2,1,0:T(8,128)(2,1)S(1)}, bf16[2,264,512]{2,1,0:T(8,128)(2,1)S(1)}, u32[]{:S(2)}, u32[]{:S(2)}) collective-permute-start(bf16[2,264,512]{2,1,0:T(8,128)(2,1)S(1)} %get-tuple-element.51), channel_id=1, source_target_pairs={{0,96},{16,112},{32,64},{48,80},{64,32},{80,48},{96,0},{112,16},{1... | collective-permute-start | bytes 1622024 | tf_op jit(solution)/shard_map/ppermute | solution.py:561
  13.8 19.0 %collective-permute-start.4 = (bf16[2,264,512]{2,1,0:T(8,128)(2,1)S(1)}, bf16[2,264,512]{2,1,0:T(8,128)(2,1)S(1)}, u32[]{:S(2)}, u32[]{:S(2)}) collective-permute-start(bf16[2,264,512]{2,1,0:T(8,128)(2,1)S(1)} %get-tuple-element.52), channel_id=1, source_target_pairs={{0,16},{16,0},{32,48},{48,32},{64,80},{80,64},{96,112},{112,96},{1... | collective-permute-start | bytes 1622024 | tf_op jit(solution)/shard_map/ppermute | solution.py:561
  23.0 14.3 %collective-permute-start.5 = (bf16[2,264,512]{2,1,0:T(8,128)(2,1)S(1)}, bf16[2,264,512]{2,1,0:T(8,128)(2,1)S(1)}, u32[]{:S(2)}, u32[]{:S(2)}) collective-permute-start(bf16[2,264,512]{2,1,0:T(8,128)(2,1)S(1)} %get-tuple-element.54), channel_id=1, source_target_pairs={{0,48},{16,32},{32,16},{48,0},{64,112},{80,96},{96,80},{112,64},{1... | collective-permute-start | bytes 1622024 | tf_op jit(solution)/shard_map/ppermute | solution.py:561
  25.6 15.7 %collective-permute-start.6 = (bf16[2,264,512]{2,1,0:T(8,128)(2,1)S(1)}, bf16[2,264,512]{2,1,0:T(8,128)(2,1)S(1)}, u32[]{:S(2)}, u32[]{:S(2)}) collective-permute-start(bf16[2,264,512]{2,1,0:T(8,128)(2,1)S(1)} %get-tuple-element.55), channel_id=1, source_target_pairs={{0,112},{16,96},{32,80},{48,64},{64,48},{80,32},{96,16},{112,0},{1... | collective-permute-start | bytes 1622024 | tf_op jit(solution)/shard_map/ppermute | solution.py:561
  41.3 29.1 %collective-permute-start.9 = (bf16[2,264,512]{2,1,0:T(8,128)(2,1)S(1)}, bf16[2,264,512]{2,1,0:T(8,128)(2,1)S(1)}, u32[]{:S(2)}, u32[]{:S(2)}) collective-permute-start(bf16[2,264,512]{2,1,0:T(8,128)(2,1)S(1)} %get-tuple-element.62), channel_id=1, source_target_pairs={{0,64},{16,80},{32,96},{48,112},{64,0},{80,16},{96,32},{112,48},{1... | collective-permute-start | bytes 1622024 | tf_op jit(solution)/shard_map/ppermute | solution.py:561
  42.0 28.4 %collective-permute-start.10 = (bf16[2,264,512]{2,1,0:T(8,128)(2,1)S(1)}, bf16[2,264,512]{2,1,0:T(8,128)(2,1)S(1)}, u32[]{:S(2)}, u32[]{:S(2)}) collective-permute-start(bf16[2,264,512]{2,1,0:T(8,128)(2,1)S(1)} %get-tuple-element.63), channel_id=1, source_target_pairs={{0,80},{16,64},{32,112},{48,96},{64,16},{80,0},{96,48},{112,32},{1... | collective-permute-start | bytes 1622024 | tf_op jit(solution)/shard_map/ppermute | solution.py:561
  44.1 24.2 %collective-permute-start.11 = (f32[2,16,256]{2,1,0:T(8,128)S(1)}, f32[2,16,256]{2,1,0:T(8,128)S(1)}, u32[]{:S(2)}, u32[]{:S(2)}) collective-permute-start(f32[2,16,256]{2,1,0:T(8,128)S(1)} %get-tuple-element.65), channel_id=1, source_target_pairs={{0,32},{16,48},{32,0},{48,16},{64,96},{80,112},{96,64},{112,80},{1... | collective-permute-start | bytes 98312 | tf_op jit(solution)/shard_map/ppermute | solution.py:561
  46.1 38.7 %copy-start = (f32[8,1536]{1,0:T(8,128)S(1)}, f32[8,1536]{1,0:T(8,128)}, u32[]{:S(2)}) copy-start(f32[8,1536]{1,0:T(8,128)} %r_ref.3) | copy-start | bytes 147460
  59.9 24.9 %collective-permute-start.7 = (f32[16,1536]{1,0:T(8,128)S(1)}, f32[16,1536]{1,0:T(8,128)S(1)}, u32[]{:S(2)}, u32[]{:S(2)}) collective-permute-start(f32[16,1536]{1,0:T(8,128)S(1)} %get-tuple-element.58), channel_id=1, source_target_pairs={{0,1},{1,2},{2,3},{3,4},{4,5},{5,6},{6,7},{7,8},{8,9},{9,10},{10,1... | collective-permute-start | bytes 294920 | tf_op jit(solution)/shard_map/ppermute | solution.py:558
  67.1 17.8 %collective-permute-start.8 = (f32[16,1536]{1,0:T(8,128)S(1)}, f32[16,1536]{1,0:T(8,128)S(1)}, u32[]{:S(2)}, u32[]{:S(2)}) collective-permute-start(f32[16,1536]{1,0:T(8,128)S(1)} %get-tuple-element.59), channel_id=1, source_target_pairs={{1,0},{2,1},{3,2},{4,3},{5,4},{6,5},{7,6},{8,7},{9,8},{10,9},{11,1... | collective-permute-start | bytes 294920 | tf_op jit(solution)/shard_map/ppermute | solution.py:555
  68.4 5.2 %collective-permute-start.12 = (f32[2,16,256]{2,1,0:T(8,128)S(1)}, f32[2,16,256]{2,1,0:T(8,128)S(1)}, u32[]{:S(2)}, u32[]{:S(2)}) collective-permute-start(f32[2,16,256]{2,1,0:T(8,128)S(1)} %get-tuple-element.66), channel_id=1, source_target_pairs={{0,96},{16,112},{32,64},{48,80},{64,32},{80,48},{96,0},{112,16},{1... | collective-permute-start | bytes 98312 | tf_op jit(solution)/shard_map/ppermute | solution.py:561
  70.4 5.9 %collective-permute-start.13 = (f32[2,16,256]{2,1,0:T(8,128)S(1)}, f32[2,16,256]{2,1,0:T(8,128)S(1)}, u32[]{:S(2)}, u32[]{:S(2)}) collective-permute-start(f32[2,16,256]{2,1,0:T(8,128)S(1)} %get-tuple-element.67), channel_id=1, source_target_pairs={{0,16},{16,0},{32,48},{48,32},{64,80},{80,64},{96,112},{112,96},{1... | collective-permute-start | bytes 98312 | tf_op jit(solution)/shard_map/ppermute | solution.py:561
  70.4 9.6 %collective-permute-start.14 = (f32[2,16,256]{2,1,0:T(8,128)S(1)}, f32[2,16,256]{2,1,0:T(8,128)S(1)}, u32[]{:S(2)}, u32[]{:S(2)}) collective-permute-start(f32[2,16,256]{2,1,0:T(8,128)S(1)} %get-tuple-element.68), channel_id=1, source_target_pairs={{0,48},{16,32},{32,16},{48,0},{64,112},{80,96},{96,80},{112,64},{1... | collective-permute-start | bytes 98312 | tf_op jit(solution)/shard_map/ppermute | solution.py:561
  73.6 6.4 %collective-permute-start.15 = (f32[2,16,256]{2,1,0:T(8,128)S(1)}, f32[2,16,256]{2,1,0:T(8,128)S(1)}, u32[]{:S(2)}, u32[]{:S(2)}) collective-permute-start(f32[2,16,256]{2,1,0:T(8,128)S(1)} %get-tuple-element.69), channel_id=1, source_target_pairs={{0,112},{16,96},{32,80},{48,64},{64,48},{80,32},{96,16},{112,0},{1... | collective-permute-start | bytes 98312 | tf_op jit(solution)/shard_map/ppermute | solution.py:561
  76.3 5.6 %collective-permute-start.16 = (f32[2,16,256]{2,1,0:T(8,128)S(1)}, f32[2,16,256]{2,1,0:T(8,128)S(1)}, u32[]{:S(2)}, u32[]{:S(2)}) collective-permute-start(f32[2,16,256]{2,1,0:T(8,128)S(1)} %get-tuple-element.70), channel_id=1, source_target_pairs={{0,64},{16,80},{32,96},{48,112},{64,0},{80,16},{96,32},{112,48},{1... | collective-permute-start | bytes 98312 | tf_op jit(solution)/shard_map/ppermute | solution.py:561
  80.0 4.8 %collective-permute-start.17 = (f32[2,16,256]{2,1,0:T(8,128)S(1)}, f32[2,16,256]{2,1,0:T(8,128)S(1)}, u32[]{:S(2)}, u32[]{:S(2)}) collective-permute-start(f32[2,16,256]{2,1,0:T(8,128)S(1)} %get-tuple-element.71), channel_id=1, source_target_pairs={{0,80},{16,64},{32,112},{48,96},{64,16},{80,0},{96,48},{112,32},{1... | collective-permute-start | bytes 98312 | tf_op jit(solution)/shard_map/ppermute | solution.py:561
  85.7 6.7 %collective-permute-start.20 = (f32[4,16,256]{2,1,0:T(8,128)S(1)}, f32[4,16,256]{2,1,0:T(8,128)S(1)}, u32[]{:S(2)}, u32[]{:S(2)}) collective-permute-start(f32[4,16,256]{2,1,0:T(8,128)S(1)} %get-tuple-element.82), channel_id=1, source_target_pairs={{0,16},{16,0},{32,48},{48,32},{64,80},{80,64},{96,112},{112,96},{1... | collective-permute-start | bytes 196616 | tf_op jit(solution)/shard_map/ppermute | solution.py:561
  85.7 12.2 %collective-permute-start.19 = (f32[8,1536]{1,0:T(8,128)S(1)}, f32[8,1536]{1,0:T(8,128)S(1)}, u32[]{:S(2)}, u32[]{:S(2)}) collective-permute-start(f32[8,1536]{1,0:T(8,128)S(1)} %get-tuple-element.72.w_ref), channel_id=1, source_target_pairs={{1,0},{2,1},{3,2},{4,3},{5,4},{6,5},{7,6},{8,7},{9,8},{10,9},{11,1... | collective-permute-start | bytes 147464 | tf_op jit(solution)/shard_map/ppermute | solution.py:555
  87.0 10.9 %collective-permute-start.18 = (f32[8,1536]{1,0:T(8,128)S(1)}, f32[8,1536]{1,0:T(8,128)S(1)}, u32[]{:S(2)}, u32[]{:S(2)}) collective-permute-start(f32[8,1536]{1,0:T(8,128)S(1)} %get-tuple-element.72.w_ref), channel_id=1, source_target_pairs={{0,1},{1,2},{2,3},{3,4},{4,5},{5,6},{6,7},{7,8},{8,9},{9,10},{10,1... | collective-permute-start | bytes 147464 | tf_op jit(solution)/shard_map/ppermute | solution.py:558
  92.3 9.3 %collective-permute-start.21 = (f32[2,16,256]{2,1,0:T(8,128)S(1)}, f32[2,16,256]{2,1,0:T(8,128)S(1)}, u32[]{:S(2)}, u32[]{:S(2)}) collective-permute-start(f32[2,16,256]{2,1,0:T(8,128)S(1)} %get-tuple-element.84), channel_id=1, source_target_pairs={{0,32},{16,48},{32,0},{48,16},{64,96},{80,112},{96,64},{112,80},{1... | collective-permute-start | bytes 98312 | tf_op jit(solution)/shard_map/ppermute | solution.py:561
  92.5 9.1 %collective-permute-start.22 = (f32[2,16,256]{2,1,0:T(8,128)S(1)}, f32[2,16,256]{2,1,0:T(8,128)S(1)}, u32[]{:S(2)}, u32[]{:S(2)}) collective-permute-start(f32[2,16,256]{2,1,0:T(8,128)S(1)} %get-tuple-element.85), channel_id=1, source_target_pairs={{0,64},{16,80},{32,96},{48,112},{64,0},{80,16},{96,32},{112,48},{1... | collective-permute-start | bytes 98312 | tf_op jit(solution)/shard_map/ppermute | solution.py:561
  94.8 6.9 %collective-permute-start.23 = (f32[2,16,256]{2,1,0:T(8,128)S(1)}, f32[2,16,256]{2,1,0:T(8,128)S(1)}, u32[]{:S(2)}, u32[]{:S(2)}) collective-permute-start(f32[2,16,256]{2,1,0:T(8,128)S(1)} %get-tuple-element.86), channel_id=1, source_target_pairs={{0,96},{16,112},{32,64},{48,80},{64,32},{80,48},{96,0},{112,16},{1... | collective-permute-start | bytes 98312 | tf_op jit(solution)/shard_map/ppermute | solution.py:561
  103.1 18.4 %all-to-all-start = ((f32[8,24,256]{2,1,0:T(8,128)}), f32[8,24,256]{2,1,0:T(8,128)S(1)}, u32[]{:S(2)}, u32[]{:S(2)}) async-start(f32[8,24,256]{2,1,0:T(8,128)} %get-tuple-element.89), calls=%async_computation | async-start | bytes 393216 | tf_op jit(solution)/shard_map/all_to_all | solution.py:564
  107.4 9.8 %collective-permute-start.24 = (f32[8,1536]{1,0:T(8,128)S(1)}, f32[8,1536]{1,0:T(8,128)S(1)}, u32[]{:S(2)}, u32[]{:S(2)}) collective-permute-start(f32[8,1536]{1,0:T(8,128)S(1)} %get-tuple-element.88), channel_id=1, source_target_pairs={{0,1},{1,2},{2,3},{3,4},{4,5},{5,6},{6,7},{7,8},{8,9},{9,10},{10,1... | collective-permute-start | bytes 147464 | tf_op jit(solution)/shard_map/ppermute | solution.py:558
  115.5 6.0 %collective-permute-start.25 = (f32[8,1536]{1,0:T(8,128)S(1)}, f32[8,1536]{1,0:T(8,128)S(1)}, u32[]{:S(2)}, u32[]{:S(2)}) collective-permute-start(f32[8,1536]{1,0:T(8,128)S(1)} %get-tuple-element.81.rl_ref), channel_id=1, source_target_pairs={{1,0},{2,1},{3,2},{4,3},{5,4},{6,5},{7,6},{8,7},{9,8},{10,9},{11,1... | collective-permute-start | bytes 147464 | tf_op jit(solution)/shard_map/ppermute | solution.py:555

commit v5 on v4

--- a/solution.py
+++ b/solution.py
@@ -175,59 +175,52 @@
     )(own)
 
 
-def band_first(left, own, right, after):
-    nt, _, _ = own.shape
+def band_first(rows, right, after, left_side):
+    nt, _, _ = rows.shape
     n = nt * TILE
-    m = len(after)
-
-    def body(l_ref, a_ref, b_ref, *refs):
-        k_ref, col_ref, rowl_ref, rowo_ref, na, nb, va, vb, acc = refs[m:]
+
+    def body(a_ref, b_ref, before_ref, k_ref, col_ref, row_ref, na, nb, va, vb, acc):
         v = lax.axis_index("dev")
-        has_left = (v > 0).astype(F32)
+        has_rows = (v > 0).astype(F32) if left_side else 1.0
         has_right = (v < lax.axis_size("dev") - 1).astype(F32)
         for i in range(nt):
             s = slice(i * TILE, (i + 1) * TILE)
-            e = slice(n + i * TILE, n + (i + 1) * TILE)
-            na[s, :] = col_norms(l_ref[i, 0:TILE, :])
-            na[e, :] = col_norms(a_ref[i, 0:TILE, :])
+            na[s, :] = col_norms(a_ref[i, 0:TILE, :])
             nb[:, s] = col_norms(b_ref[i, 0:TILE, :]).T[0:8]
-            va[:, s] = rhs_ones(l_ref[i, TILE:, :], has_left)
-            va[:, e] = rhs_ones(a_ref[i, TILE:, :], 1.0)
+            va[:, s] = rhs_ones(a_ref[i, TILE:, :], has_rows)
             vb[:, s] = rhs_ones(b_ref[i, TILE:, :], has_right)
         acc[...] = jnp.zeros_like(acc)
 
         def step(t, carry):
             s = span(t)
             b = b_ref[t, 0:TILE, :] * jnp.asarray(-2.0, BF16)
-            for j, x in enumerate((l_ref, a_ref)):
-                for i in range(nt):
-                    e = slice((j * nt + i) * TILE, (j * nt + i + 1) * TILE)
-                    k_ref[t, e, :] = kernel_tile(x[i, 0:TILE, :], b, na[e, :], nb[0:1, s])
+            for i in range(nt):
+                c = slice(i * TILE, (i + 1) * TILE)
+                k_ref[t, c, :] = kernel_tile(a_ref[i, 0:TILE, :], b, na[c, :], nb[0:1, s])
             k = k_ref[t]
-            col_ref[:, s] = fold_ones(mm(va[...], k, NN))
+            col = fold_ones(mm(va[...], k, NN))
+            col_ref[:, s] = before_ref[:, s] + col if left_side else col
             acc[...] += mm(vb[:, s], k, NT)
             return carry
 
         lax.fori_loop(0, nt, step, 0, unroll=2)
-        rows = fold_ones(acc[...])
-        rowl_ref[...] = rows[:, 0:n]
-        rowo_ref[...] = rows[:, n:]
-
-    return pl.pallas_call(
-        body,
-        out_shape=(vmem_bf16(nt, 2 * n, TILE), f32(16, n), f32(16, n), f32(16, n)),
-        in_specs=[VM] * 3 + [ANY] * m,
-        out_specs=(VM,) * 4,
+        row_ref[...] = fold_ones(acc[...])
+
+    return pl.pallas_call(
+        body,
+        out_shape=(vmem_bf16(nt, n, TILE), f32(16, n), f32(16, n)),
+        in_specs=[VM, VM, VM if left_side else ANY],
+        out_specs=(VM,) * 3,
         scratch_shapes=[
-            pltpu.VMEM((2 * n, 128), F32),
+            pltpu.VMEM((n, 128), F32),
             pltpu.VMEM((8, n), F32),
-            pltpu.VMEM((32, 2 * n), BF16),
             pltpu.VMEM((32, n), BF16),
-            pltpu.VMEM((32, 2 * n), F32),
+            pltpu.VMEM((32, n), BF16),
+            pltpu.VMEM((32, n), F32),
         ],
         compiler_params=params(),
-        name="band_first",
-    )(left, own, right, *after)
+        name="band_left" if left_side else "band_own",
+    )(rows, right, after)
 
 
 def cross_first(ks, table, own, tiles, after):
@@ -385,32 +378,31 @@
     )(k_local, w)
 
 
-def band_second(k_band, w_left, w, w_right, after):
-    nt, n2, _ = k_band.shape
-    n = n2 // 2
-
-    def body(k_ref, wl_ref, w_ref, wb_ref, _, col_ref, rowl_ref, rowo_ref, va, acc):
-        va[:, 0:n] = split(wl_ref[...])
-        va[:, n:] = split(w_ref[...])
+def band_second(k_left, k_own, w_left, w, w_right, after):
+    nt, n, _ = k_own.shape
+
+    def body(kl_ref, ko_ref, wl_ref, w_ref, wb_ref, _, col_ref, rowl_ref, rowo_ref, acc_l, acc_o):
+        va_l = split(wl_ref[...])
+        va_o = split(w_ref[...])
         vb = split(wb_ref[...])
         for t in range(nt):
             s = slice(t * TILE, (t + 1) * TILE)
-            col_ref[:, s] = fold(mm(va[...], k_ref[t], NN))
-            new = mm(vb[:, s], k_ref[t], NT)
-            acc[...] = new if t == 0 else acc[...] + new
-        rows = fold(acc[...])
-        rowl_ref[...] = rows[:, 0:n]
-        rowo_ref[...] = rows[:, n:]
+            col_ref[:, s] = fold(mm(va_l, kl_ref[t], NN) + mm(va_o, ko_ref[t], NN))
+            for acc, k_ref in ((acc_l, kl_ref), (acc_o, ko_ref)):
+                new = mm(vb[:, s], k_ref[t], NT)
+                acc[...] = new if t == 0 else acc[...] + new
+        rowl_ref[...] = fold(acc_l[...])
+        rowo_ref[...] = fold(acc_o[...])
 
     return pl.pallas_call(
         body,
         out_shape=(f32(8, n), f32(8, n), f32(8, n)),
-        in_specs=[VM] * 4 + [ANY],
+        in_specs=[VM] * 5 + [ANY],
         out_specs=(VM,) * 3,
-        scratch_shapes=[pltpu.VMEM((16, n2), BF16), pltpu.VMEM((16, n2), F32)],
+        scratch_shapes=[pltpu.VMEM((16, n), F32), pltpu.VMEM((16, n), F32)],
         compiler_params=params(),
         name="band_second",
-    )(k_band, w_left, w, w_right, after)
+    )(k_left, k_own, w_left, w, w_right, after)
 
 
 def cross_second(table, k_caches, w, xw, sums, loc, row_left, row_own, w_left):
@@ -586,9 +578,10 @@
         arrived[k] = swap(x, k)
     k_b, row_b, *col_b = cross(STAGES[1], row_a)
     give_back(col_b, STAGES[1])
-    k_band, to_r, to_l, acc_band = band_first(left, own, right, [row_b])
+    k_own, col_own, acc_band = band_first(own, right, row_b, False)
+    k_left, to_r, to_l = band_first(left, right, col_own, True)
     from_left, from_right = left_of(to_r), right_of(to_l)
-    k_c, row_c, *col_c = cross(STAGES[2], acc_band)
+    k_c, row_c, *col_c = cross(STAGES[2], to_l)
     give_back(col_c, STAGES[2])
     w_own, w_relay, w, deg, sums = combine(
         table, targets, (acc_local, acc_band, from_left, from_right, row_a, row_b, row_c), [ret[k] for k in SWAPS]
@@ -598,7 +591,7 @@
     partner = swap(w_relay, 1)
     xw = [partner] + [swap(x, 2 * j + 2) for j, x in enumerate(relay(w_own, partner))]
     loc2 = local_second(k_local, w)
-    col_r, rowl_b, rowo_b = band_second(k_band, w_left, w, w_right, loc2)
+    col_r, rowl_b, rowo_b = band_second(k_left, k_own, w_left, w, w_right, loc2)
     from_left2 = left_of(col_r)
     from_right2 = right_of(rowl_b)
     col_x, row_x = cross_second(table, (k_a, k_b, k_c), w, xw, sums, loc2, rowl_b, rowo_b, w_left)

time: 143 us -> 145 us (1.014)
  Pallas kernels: 34 us -> 35.7 us
    pallas_call x1 -> x2, Pallas kernels: 13.8 us -> 15.3 us  [band_first(): pl.pallas_call(body, out_shape=(vmem_bf16(nt, n, TILE), f32(16, n), f32(1...]
  transfers between devices with their start and end apart: 27 -> 27, of which waited for: 9 -> 9; matrix products, arithmetic and copies ran while one was open for 0% -> 0% of each run, Pallas kernels for 19% -> 20%
where the time goes in v5:
time: 145 us; the launch traced here: 144 us
  starting transfers between devices  58.3 us (40%)
  Pallas kernels  35.7 us (25%)
  waiting for transfers between devices  30.5 us (21%)
  blocking collectives  18.7 us (13%)
    ppermute x18, waiting for transfers between devices, swap(): return lax.ppermute(x, 'group', [(i, i ^ k) for i in range(8)])  25.8 us
    ppermute x4, starting transfers between devices, left_of(): return lax.ppermute(x, 'dev', to_right)  24.9 us
    ppermute x18, starting transfers between devices, swap(): return lax.ppermute(x, 'group', [(i, i ^ k) for i in range(8)])  23.9 us
    all_to_all x1, blocking collectives, trade(): return lax.all_to_all(x, axis, split_axis=0, concat_axis=0, tiled=True)  18.7 us
    pallas_call x2, Pallas kernels, band_first(): pl.pallas_call(body, out_shape=(vmem_bf16(nt, n, TILE), f32(16, n), f32(1...  15.3 us
    pallas_call x1, Pallas kernels, local_first(): pl.pallas_call(body, out_shape=(vmem_bf16(nt, n, TILE), f32(16, n)), in_s...  6.09 us
    ppermute x4, starting transfers between devices, right_of(): return lax.ppermute(x, 'dev', to_left)  5.17 us
    all_to_all x1, starting transfers between devices, trade(): return lax.all_to_all(x, axis, split_axis=0, concat_axis=0, tiled=True)  4.34 us
  transfers between devices with their start and end apart: 27, of which 9 were waited for; matrix products, arithmetic and copies ran while one was open for 0% of the time, Pallas kernels for 20%

profile of v5, /device:TPU:0, one launch (start us, length us, event | category | flops | bytes accessed | tf_op | source)
XLA Modules:
  0.0 144.1 jit_solution(8495900707948874607)
XLA Ops:
  0.6 2.6 %prep.1 = (s32[32]{0:T(128)S(1)}, bf16[6,264,512]{2,1,0:T(8,128)(2,1)S(1)}, bf16[2,264,512]{2,1,0:T(8,128)(2,1)S(1)}, bf16[2,264,512]{2,1,0:T(8,128)(2,1)S(1)}, ...) custom-call(s32[8,8,2,16]{3,2,1,0:T(2,128)} %bitcast.1, ...), custom_call_target="tpu_custom_call" | custom-call | tf_op jit(solution)/shard_map/prep/pallas_call | solution.py:111
  3.2 1.3 collective-permute-start
  4.5 4.6 %collective-permute-start.6 = (bf16[6,264,512]{2,1,0:T(8,128)(2,1)S(1)}, bf16[6,264,512]{2,1,0:T(8,128)(2,1)S(1)}, u32[]{:S(2)}, u32[]{:S(2)}) collective-permute-start(bf16[6,264,512]{2,1,0:T(8,128)(2,1)S(1)} %get-tuple-element.50.a_ref), channel_id=1, source_target_pairs={{0,1},{1,2},{2,3},{3,4},{4,5},{5,6},{6,7},{7,8},{8,9},{9,10},{10,1... | collective-permute-start | bytes 4866056 | tf_op jit(solution)/shard_map/ppermute | solution.py:550
  9.1 2.1 %collective-permute-start.1 = (bf16[2,264,512]{2,1,0:T(8,128)(2,1)S(1)}, bf16[2,264,512]{2,1,0:T(8,128)(2,1)S(1)}, u32[]{:S(2)}, u32[]{:S(2)}) collective-permute-start(bf16[2,264,512]{2,1,0:T(8,128)(2,1)S(1)} %get-tuple-element.52), channel_id=1, source_target_pairs={{0,32},{16,48},{32,0},{48,16},{64,96},{80,112},{96,64},{112,80},{1... | collective-permute-start | bytes 1622024 | tf_op jit(solution)/shard_map/ppermute | solution.py:553
  11.3 2.5 %collective-permute-start.2 = (bf16[2,264,512]{2,1,0:T(8,128)(2,1)S(1)}, bf16[2,264,512]{2,1,0:T(8,128)(2,1)S(1)}, u32[]{:S(2)}, u32[]{:S(2)}) collective-permute-start(bf16[2,264,512]{2,1,0:T(8,128)(2,1)S(1)} %get-tuple-element.53), channel_id=1, source_target_pairs={{0,96},{16,112},{32,64},{48,80},{64,32},{80,48},{96,0},{112,16},{1... | collective-permute-start | bytes 1622024 | tf_op jit(solution)/shard_map/ppermute | solution.py:553
  13.8 9.2 %collective-permute-done.1.refs_0_ = bf16[2,264,512]{2,1,0:T(8,128)(2,1)S(1)} collective-permute-done((bf16[2,264,512]{2,1,0:T(8,128)(2,1)S(1)}, bf16[2,264,512]{2,1,0:T(8,128)(2,1)S(1)}, u32[]{:S(2)}, u32[]{:S(2)}) %collective-permute-start.1) | collective-permute-done | bytes 540704 | tf_op jit(solution)/shard_map/ppermute | solution.py:553
  23.0 2.7 %collective-permute-done.2.refs_1_ = bf16[2,264,512]{2,1,0:T(8,128)(2,1)S(1)} collective-permute-done((bf16[2,264,512]{2,1,0:T(8,128)(2,1)S(1)}, bf16[2,264,512]{2,1,0:T(8,128)(2,1)S(1)}, u32[]{:S(2)}, u32[]{:S(2)}) %collective-permute-start.2) | collective-permute-done | bytes 540704 | tf_op jit(solution)/shard_map/ppermute | solution.py:553
  25.6 1.3 collective-permute-start.5
  27.0 6.1 %local_first.1 = (bf16[6,1536,256]{2,1,0:T(8,128)(2,1)S(1)}, f32[16,1536]{1,0:T(8,128)S(1)}) custom-call(bf16[6,264,512]{2,1,0:T(8,128)(2,1)S(1)} %get-tuple-element.50.a_ref), custom_call_target="tpu_custom_call" | custom-call | tf_op jit(solution)/shard_map/local_first/pallas_call | solution.py:167
  33.0 1.1 shard_map.50
  34.1 3.1 %collective-permute-done.4.refs_0_.refs_3_ = bf16[2,264,512]{2,1,0:T(8,128)(2,1)S(1)} collective-permute-done((bf16[2,264,512]{2,1,0:T(8,128)(2,1)S(1)}, bf16[2,264,512]{2,1,0:T(8,128)(2,1)S(1)}, u32[]{:S(2)}, u32[]{:S(2)}) %collective-permute-start.4) | collective-permute-done | bytes 540704 | tf_op jit(solution)/shard_map/ppermute | solution.py:553
  37.3 4.0 %collective-permute-done.5.refs_1_.refs_4_ = bf16[2,264,512]{2,1,0:T(8,128)(2,1)S(1)} collective-permute-done((bf16[2,264,512]{2,1,0:T(8,128)(2,1)S(1)}, bf16[2,264,512]{2,1,0:T(8,128)(2,1)S(1)}, u32[]{:S(2)}, u32[]{:S(2)}) %collective-permute-start.5) | collective-permute-done | bytes 540704 | tf_op jit(solution)/shard_map/ppermute | solution.py:553
  41.3 0.7 collective-permute-start.9
  42.0 2.1 %collective-permute-start.10 = (bf16[2,264,512]{2,1,0:T(8,128)(2,1)S(1)}, bf16[2,264,512]{2,1,0:T(8,128)(2,1)S(1)}, u32[]{:S(2)}, u32[]{:S(2)}) collective-permute-start(bf16[2,264,512]{2,1,0:T(8,128)(2,1)S(1)} %get-tuple-element.66), channel_id=1, source_target_pairs={{0,80},{16,64},{32,112},{48,96},{64,16},{80,0},{96,48},{112,32},{1... | collective-permute-start | bytes 1622024 | tf_op jit(solution)/shard_map/ppermute | solution.py:553
  44.1 1.3 collective-permute-start.11
  45.4 1.2 shard_map.51
  46.6 7.7 %band_own.1 = (bf16[6,1536,256]{2,1,0:T(8,128)(2,1)S(1)}, f32[16,1536]{1,0:T(8,128)S(1)}, f32[16,1536]{1,0:T(8,128)S(1)}) custom-call(bf16[6,264,512]{2,1,0:T(8,128)(2,1)S(1)} %get-tuple-element.50.a_ref, bf16[6,264,512]{2,1,0:T(8,128)(2,1)S(1)} %collective-permute-done.b_ref, f32[16,1536]{1,0:T(8,128)S(1)} %get-tuple-element.58.before_ref.refs_5_), custom_call_target="tpu_custom_call" | custom-call | tf_op jit(solution)/shard_map/band_own/pallas_call | solution.py:209
  54.3 7.6 %band_left.1 = (bf16[6,1536,256]{2,1,0:T(8,128)(2,1)S(1)}, f32[16,1536]{1,0:T(8,128)S(1)}, f32[16,1536]{1,0:T(8,128)S(1)}) custom-call(bf16[6,264,512]{2,1,0:T(8,128)(2,1)S(1)} %collective-permute-done.6.a_ref, bf16[6,264,512]{2,1,0:T(8,128)(2,1)S(1)} %collective-permute-done.b_ref, f32[16,1536]{1,0:T(8,128)S(1)} %get-tuple-element.60.before_ref), custom_call_target="tpu_custom_call" | custom-call | tf_op jit(solution)/shard_map/band_left/pallas_call | solution.py:209
  61.9 6.8 %collective-permute-start.7 = (f32[16,1536]{1,0:T(8,128)S(1)}, f32[16,1536]{1,0:T(8,128)S(1)}, u32[]{:S(2)}, u32[]{:S(2)}) collective-permute-start(f32[16,1536]{1,0:T(8,128)S(1)} %get-tuple-element.61), channel_id=1, source_target_pairs={{0,1},{1,2},{2,3},{3,4},{4,5},{5,6},{6,7},{7,8},{8,9},{9,10},{10,1... | collective-permute-start | bytes 294920 | tf_op jit(solution)/shard_map/ppermute | solution.py:550
  68.8 1.3 collective-permute-start.8
  70.1 2.2 %collective-permute-start.12 = (f32[2,16,256]{2,1,0:T(8,128)S(1)}, f32[2,16,256]{2,1,0:T(8,128)S(1)}, u32[]{:S(2)}, u32[]{:S(2)}) collective-permute-start(f32[2,16,256]{2,1,0:T(8,128)S(1)} %get-tuple-element.69), channel_id=1, source_target_pairs={{0,96},{16,112},{32,64},{48,80},{64,32},{80,48},{96,0},{112,16},{1... | collective-permute-start | bytes 98312 | tf_op jit(solution)/shard_map/ppermute | solution.py:553
  72.3 0.1 collective-permute-start.14
  72.4 1.0 shard_map.52
  73.4 1.9 %collective-permute-done.12.refs_8_ = f32[2,16,256]{2,1,0:T(8,128)S(1)} collective-permute-done((f32[2,16,256]{2,1,0:T(8,128)S(1)}, f32[2,16,256]{2,1,0:T(8,128)S(1)}, u32[]{:S(2)}, u32[]{:S(2)}) %collective-permute-start.12) | collective-permute-done | bytes 32800 | tf_op jit(solution)/shard_map/ppermute | solution.py:553
  75.3 2.8 %collective-permute-start.15 = (f32[2,16,256]{2,1,0:T(8,128)S(1)}, f32[2,16,256]{2,1,0:T(8,128)S(1)}, u32[]{:S(2)}, u32[]{:S(2)}) collective-permute-start(f32[2,16,256]{2,1,0:T(8,128)S(1)} %get-tuple-element.72), channel_id=1, source_target_pairs={{0,112},{16,96},{32,80},{48,64},{64,48},{80,32},{96,16},{112,0},{1... | collective-permute-start | bytes 98312 | tf_op jit(solution)/shard_map/ppermute | solution.py:553
  78.1 4.0 %collective-permute-start.16 = (f32[2,16,256]{2,1,0:T(8,128)S(1)}, f32[2,16,256]{2,1,0:T(8,128)S(1)}, u32[]{:S(2)}, u32[]{:S(2)}) collective-permute-start(f32[2,16,256]{2,1,0:T(8,128)S(1)} %get-tuple-element.73), channel_id=1, source_target_pairs={{0,64},{16,80},{32,96},{48,112},{64,0},{80,16},{96,32},{112,48},{1... | collective-permute-start | bytes 98312 | tf_op jit(solution)/shard_map/ppermute | solution.py:553
  82.1 1.9 %collective-permute-done.16.refs_12_ = f32[2,16,256]{2,1,0:T(8,128)S(1)} collective-permute-done((f32[2,16,256]{2,1,0:T(8,128)S(1)}, f32[2,16,256]{2,1,0:T(8,128)S(1)}, u32[]{:S(2)}, u32[]{:S(2)}) %collective-permute-start.16) | collective-permute-done | bytes 32800 | tf_op jit(solution)/shard_map/ppermute | solution.py:553
  84.0 3.0 %collective-permute-done.17.refs_13_ = f32[2,16,256]{2,1,0:T(8,128)S(1)} collective-permute-done((f32[2,16,256]{2,1,0:T(8,128)S(1)}, f32[2,16,256]{2,1,0:T(8,128)S(1)}, u32[]{:S(2)}, u32[]{:S(2)}) %collective-permute-start.17) | collective-permute-done | bytes 32800 | tf_op jit(solution)/shard_map/ppermute | solution.py:553
  86.9 0.8 combine.1
  87.8 0.0 collective-permute-start.20
  87.8 1.3 collective-permute-start.19
  89.1 5.3 %collective-permute-start.18 = (f32[8,1536]{1,0:T(8,128)S(1)}, f32[8,1536]{1,0:T(8,128)S(1)}, u32[]{:S(2)}, u32[]{:S(2)}) collective-permute-start(f32[8,1536]{1,0:T(8,128)S(1)} %get-tuple-element.75.w_ref), channel_id=1, source_target_pairs={{0,1},{1,2},{2,3},{3,4},{4,5},{5,6},{6,7},{7,8},{8,9},{9,10},{10,1... | collective-permute-start | bytes 147464 | tf_op jit(solution)/shard_map/ppermute | solution.py:550
  94.4 0.1 collective-permute-start.21
  94.5 2.3 %collective-permute-start.22 = (f32[2,16,256]{2,1,0:T(8,128)S(1)}, f32[2,16,256]{2,1,0:T(8,128)S(1)}, u32[]{:S(2)}, u32[]{:S(2)}) collective-permute-start(f32[2,16,256]{2,1,0:T(8,128)S(1)} %get-tuple-element.89), channel_id=1, source_target_pairs={{0,64},{16,80},{32,96},{48,112},{64,0},{80,16},{96,32},{112,48},{1... | collective-permute-start | bytes 98312 | tf_op jit(solution)/shard_map/ppermute | solution.py:553
  96.9 2.3 %collective-permute-start.23 = (f32[2,16,256]{2,1,0:T(8,128)S(1)}, f32[2,16,256]{2,1,0:T(8,128)S(1)}, u32[]{:S(2)}, u32[]{:S(2)}) collective-permute-start(f32[2,16,256]{2,1,0:T(8,128)S(1)} %get-tuple-element.90), channel_id=1, source_target_pairs={{0,96},{16,112},{32,64},{48,80},{64,32},{80,48},{96,0},{112,16},{1... | collective-permute-start | bytes 98312 | tf_op jit(solution)/shard_map/ppermute | solution.py:553
  99.2 0.7 local_second.1._.loc_ref.refs_0_
  99.9 0.0 collective-permute-done.18.wl_ref
  99.9 3.8 %band_second.1 = (f32[8,1536]{1,0:T(8,128)S(1)}, f32[8,1536]{1,0:T(8,128)S(1)}, f32[8,1536]{1,0:T(8,128)S(1)}) custom-call(bf16[6,1536,256]{2,1,0:T(8,128)(2,1)S(1)} %get-tuple-element.78.kl_ref, bf16[6,1536,256]{2,1,0:T(8,128)(2,1)S(1)} %get-tuple-element.79.ko_ref, f32[8,1536]{1,0:T(8,128)S(1)} %collective-permute-done.18.wl_ref, ...), custom_call_target="tpu_custom_call" | custom-call | tf_op jit(solution)/shard_map/band_second/pallas_call | solution.py:397
  103.7 0.0 collective-permute-done.22.refs_2_
  103.8 1.4 cross_second.1
  105.2 4.3 %all-to-all-start = ((f32[8,24,256]{2,1,0:T(8,128)}), f32[8,24,256]{2,1,0:T(8,128)S(1)}, u32[]{:S(2)}, u32[]{:S(2)}) async-start(f32[8,24,256]{2,1,0:T(8,128)} %get-tuple-element.93), calls=%async_computation | async-start | bytes 393216 | tf_op jit(solution)/shard_map/all_to_all | solution.py:556
  109.5 8.1 %collective-permute-start.24 = (f32[8,1536]{1,0:T(8,128)S(1)}, f32[8,1536]{1,0:T(8,128)S(1)}, u32[]{:S(2)}, u32[]{:S(2)}) collective-permute-start(f32[8,1536]{1,0:T(8,128)S(1)} %get-tuple-element.92), channel_id=1, source_target_pairs={{0,1},{1,2},{2,3},{3,4},{4,5},{5,6},{6,7},{7,8},{8,9},{9,10},{10,1... | collective-permute-start | bytes 147464 | tf_op jit(solution)/shard_map/ppermute | solution.py:550
  117.6 1.3 collective-permute-start.25
  118.9 0.4 collective-permute-done.24.refs_3_
  119.3 4.3 %collective-permute-done.25.refs_4_ = f32[8,1536]{1,0:T(8,128)S(1)} collective-permute-done((f32[8,1536]{1,0:T(8,128)S(1)}, f32[8,1536]{1,0:T(8,128)S(1)}, u32[]{:S(2)}, u32[]{:S(2)}) %collective-permute-start.25) | collective-permute-done | bytes 49184 | tf_op jit(solution)/shard_map/ppermute | solution.py:547
  123.6 0.7 group_sum.1
  124.3 18.7 %all_to_all.10.g_ref = f32[16,8,128]{2,1,0:T(8,128)S(1)} all-to-all(f32[16,8,128]{2,1,0:T(8,128)S(1)} %get-tuple-element.94), channel_id=1, replica_groups=mesh['group'=8,'dev'=16] {'dev'}, dimensions={0} | all-to-all | bytes 131072 | tf_op jit(solution)/shard_map/all_to_all | solution.py:556
  143.0 1.1 finish.1
  (24 shorter events, 0.1 us)
Async XLA Ops:
  3.2 43.4 %collective-permute-start = (bf16[6,264,512]{2,1,0:T(8,128)(2,1)S(1)}, bf16[6,264,512]{2,1,0:T(8,128)(2,1)S(1)}, u32[]{:S(2)}, u32[]{:S(2)}) collective-permute-start(bf16[6,264,512]{2,1,0:T(8,128)(2,1)S(1)} %get-tuple-element.50.a_ref), channel_id=1, source_target_pairs={{1,0},{2,1},{3,2},{4,3},{5,4},{6,5},{7,6},{8,7},{9,8},{10,9},{11,1... | collective-permute-start | bytes 4866056 | tf_op jit(solution)/shard_map/ppermute | solution.py:547
  4.5 49.8 %collective-permute-start.6 = (bf16[6,264,512]{2,1,0:T(8,128)(2,1)S(1)}, bf16[6,264,512]{2,1,0:T(8,128)(2,1)S(1)}, u32[]{:S(2)}, u32[]{:S(2)}) collective-permute-start(bf16[6,264,512]{2,1,0:T(8,128)(2,1)S(1)} %get-tuple-element.50.a_ref), channel_id=1, source_target_pairs={{0,1},{1,2},{2,3},{3,4},{4,5},{5,6},{6,7},{7,8},{8,9},{9,10},{10,1... | collective-permute-start | bytes 4866056 | tf_op jit(solution)/shard_map/ppermute | solution.py:550
  9.1 13.8 %collective-permute-start.1 = (bf16[2,264,512]{2,1,0:T(8,128)(2,1)S(1)}, bf16[2,264,512]{2,1,0:T(8,128)(2,1)S(1)}, u32[]{:S(2)}, u32[]{:S(2)}) collective-permute-start(bf16[2,264,512]{2,1,0:T(8,128)(2,1)S(1)} %get-tuple-element.52), channel_id=1, source_target_pairs={{0,32},{16,48},{32,0},{48,16},{64,96},{80,112},{96,64},{112,80},{1... | collective-permute-start | bytes 1622024 | tf_op jit(solution)/shard_map/ppermute | solution.py:553
  11.3 14.4 %collective-permute-start.2 = (bf16[2,264,512]{2,1,0:T(8,128)(2,1)S(1)}, bf16[2,264,512]{2,1,0:T(8,128)(2,1)S(1)}, u32[]{:S(2)}, u32[]{:S(2)}) collective-permute-start(bf16[2,264,512]{2,1,0:T(8,128)(2,1)S(1)} %get-tuple-element.53), channel_id=1, source_target_pairs={{0,96},{16,112},{32,64},{48,80},{64,32},{80,48},{96,0},{112,16},{1... | collective-permute-start | bytes 1622024 | tf_op jit(solution)/shard_map/ppermute | solution.py:553
  13.8 19.3 %collective-permute-start.3 = (bf16[2,264,512]{2,1,0:T(8,128)(2,1)S(1)}, bf16[2,264,512]{2,1,0:T(8,128)(2,1)S(1)}, u32[]{:S(2)}, u32[]{:S(2)}) collective-permute-start(bf16[2,264,512]{2,1,0:T(8,128)(2,1)S(1)} %get-tuple-element.54), channel_id=1, source_target_pairs={{0,16},{16,0},{32,48},{48,32},{64,80},{80,64},{96,112},{112,96},{1... | collective-permute-start | bytes 1622024 | tf_op jit(solution)/shard_map/ppermute | solution.py:553
  23.0 14.3 %collective-permute-start.4 = (bf16[2,264,512]{2,1,0:T(8,128)(2,1)S(1)}, bf16[2,264,512]{2,1,0:T(8,128)(2,1)S(1)}, u32[]{:S(2)}, u32[]{:S(2)}) collective-permute-start(bf16[2,264,512]{2,1,0:T(8,128)(2,1)S(1)} %get-tuple-element.56), channel_id=1, source_target_pairs={{0,48},{16,32},{32,16},{48,0},{64,112},{80,96},{96,80},{112,64},{1... | collective-permute-start | bytes 1622024 | tf_op jit(solution)/shard_map/ppermute | solution.py:553
  25.6 15.7 %collective-permute-start.5 = (bf16[2,264,512]{2,1,0:T(8,128)(2,1)S(1)}, bf16[2,264,512]{2,1,0:T(8,128)(2,1)S(1)}, u32[]{:S(2)}, u32[]{:S(2)}) collective-permute-start(bf16[2,264,512]{2,1,0:T(8,128)(2,1)S(1)} %get-tuple-element.57), channel_id=1, source_target_pairs={{0,112},{16,96},{32,80},{48,64},{64,48},{80,32},{96,16},{112,0},{1... | collective-permute-start | bytes 1622024 | tf_op jit(solution)/shard_map/ppermute | solution.py:553
  41.3 31.0 %collective-permute-start.9 = (bf16[2,264,512]{2,1,0:T(8,128)(2,1)S(1)}, bf16[2,264,512]{2,1,0:T(8,128)(2,1)S(1)}, u32[]{:S(2)}, u32[]{:S(2)}) collective-permute-start(bf16[2,264,512]{2,1,0:T(8,128)(2,1)S(1)} %get-tuple-element.65), channel_id=1, source_target_pairs={{0,64},{16,80},{32,96},{48,112},{64,0},{80,16},{96,32},{112,48},{1... | collective-permute-start | bytes 1622024 | tf_op jit(solution)/shard_map/ppermute | solution.py:553
  42.0 30.3 %collective-permute-start.10 = (bf16[2,264,512]{2,1,0:T(8,128)(2,1)S(1)}, bf16[2,264,512]{2,1,0:T(8,128)(2,1)S(1)}, u32[]{:S(2)}, u32[]{:S(2)}) collective-permute-start(bf16[2,264,512]{2,1,0:T(8,128)(2,1)S(1)} %get-tuple-element.66), channel_id=1, source_target_pairs={{0,80},{16,64},{32,112},{48,96},{64,16},{80,0},{96,48},{112,32},{1... | collective-permute-start | bytes 1622024 | tf_op jit(solution)/shard_map/ppermute | solution.py:553
  44.1 26.0 %collective-permute-start.11 = (f32[2,16,256]{2,1,0:T(8,128)S(1)}, f32[2,16,256]{2,1,0:T(8,128)S(1)}, u32[]{:S(2)}, u32[]{:S(2)}) collective-permute-start(f32[2,16,256]{2,1,0:T(8,128)S(1)} %get-tuple-element.68), channel_id=1, source_target_pairs={{0,32},{16,48},{32,0},{48,16},{64,96},{80,112},{96,64},{112,80},{1... | collective-permute-start | bytes 98312 | tf_op jit(solution)/shard_map/ppermute | solution.py:553
  54.3 32.6 %copy-start = (f32[8,1536]{1,0:T(8,128)S(1)}, f32[8,1536]{1,0:T(8,128)}, u32[]{:S(2)}) copy-start(f32[8,1536]{1,0:T(8,128)} %r_ref.3) | copy-start | bytes 147460
  61.9 25.0 %collective-permute-start.7 = (f32[16,1536]{1,0:T(8,128)S(1)}, f32[16,1536]{1,0:T(8,128)S(1)}, u32[]{:S(2)}, u32[]{:S(2)}) collective-permute-start(f32[16,1536]{1,0:T(8,128)S(1)} %get-tuple-element.61), channel_id=1, source_target_pairs={{0,1},{1,2},{2,3},{3,4},{4,5},{5,6},{6,7},{7,8},{8,9},{9,10},{10,1... | collective-permute-start | bytes 294920 | tf_op jit(solution)/shard_map/ppermute | solution.py:550
  68.8 18.1 %collective-permute-start.8 = (f32[16,1536]{1,0:T(8,128)S(1)}, f32[16,1536]{1,0:T(8,128)S(1)}, u32[]{:S(2)}, u32[]{:S(2)}) collective-permute-start(f32[16,1536]{1,0:T(8,128)S(1)} %get-tuple-element.62._), channel_id=1, source_target_pairs={{1,0},{2,1},{3,2},{4,3},{5,4},{6,5},{7,6},{8,7},{9,8},{10,9},{11,1... | collective-permute-start | bytes 294920 | tf_op jit(solution)/shard_map/ppermute | solution.py:547
  70.1 5.2 %collective-permute-start.12 = (f32[2,16,256]{2,1,0:T(8,128)S(1)}, f32[2,16,256]{2,1,0:T(8,128)S(1)}, u32[]{:S(2)}, u32[]{:S(2)}) collective-permute-start(f32[2,16,256]{2,1,0:T(8,128)S(1)} %get-tuple-element.69), channel_id=1, source_target_pairs={{0,96},{16,112},{32,64},{48,80},{64,32},{80,48},{96,0},{112,16},{1... | collective-permute-start | bytes 98312 | tf_op jit(solution)/shard_map/ppermute | solution.py:553
  72.3 5.8 %collective-permute-start.13 = (f32[2,16,256]{2,1,0:T(8,128)S(1)}, f32[2,16,256]{2,1,0:T(8,128)S(1)}, u32[]{:S(2)}, u32[]{:S(2)}) collective-permute-start(f32[2,16,256]{2,1,0:T(8,128)S(1)} %get-tuple-element.70), channel_id=1, source_target_pairs={{0,16},{16,0},{32,48},{48,32},{64,80},{80,64},{96,112},{112,96},{1... | collective-permute-start | bytes 98312 | tf_op jit(solution)/shard_map/ppermute | solution.py:553
  72.3 9.8 %collective-permute-start.14 = (f32[2,16,256]{2,1,0:T(8,128)S(1)}, f32[2,16,256]{2,1,0:T(8,128)S(1)}, u32[]{:S(2)}, u32[]{:S(2)}) collective-permute-start(f32[2,16,256]{2,1,0:T(8,128)S(1)} %get-tuple-element.71), channel_id=1, source_target_pairs={{0,48},{16,32},{32,16},{48,0},{64,112},{80,96},{96,80},{112,64},{1... | collective-permute-start | bytes 98312 | tf_op jit(solution)/shard_map/ppermute | solution.py:553
  75.3 6.8 %collective-permute-start.15 = (f32[2,16,256]{2,1,0:T(8,128)S(1)}, f32[2,16,256]{2,1,0:T(8,128)S(1)}, u32[]{:S(2)}, u32[]{:S(2)}) collective-permute-start(f32[2,16,256]{2,1,0:T(8,128)S(1)} %get-tuple-element.72), channel_id=1, source_target_pairs={{0,112},{16,96},{32,80},{48,64},{64,48},{80,32},{96,16},{112,0},{1... | collective-permute-start | bytes 98312 | tf_op jit(solution)/shard_map/ppermute | solution.py:553
  78.1 5.9 %collective-permute-start.16 = (f32[2,16,256]{2,1,0:T(8,128)S(1)}, f32[2,16,256]{2,1,0:T(8,128)S(1)}, u32[]{:S(2)}, u32[]{:S(2)}) collective-permute-start(f32[2,16,256]{2,1,0:T(8,128)S(1)} %get-tuple-element.73), channel_id=1, source_target_pairs={{0,64},{16,80},{32,96},{48,112},{64,0},{80,16},{96,32},{112,48},{1... | collective-permute-start | bytes 98312 | tf_op jit(solution)/shard_map/ppermute | solution.py:553
  82.1 4.8 %collective-permute-start.17 = (f32[2,16,256]{2,1,0:T(8,128)S(1)}, f32[2,16,256]{2,1,0:T(8,128)S(1)}, u32[]{:S(2)}, u32[]{:S(2)}) collective-permute-start(f32[2,16,256]{2,1,0:T(8,128)S(1)} %get-tuple-element.74), channel_id=1, source_target_pairs={{0,80},{16,64},{32,112},{48,96},{64,16},{80,0},{96,48},{112,32},{1... | collective-permute-start | bytes 98312 | tf_op jit(solution)/shard_map/ppermute | solution.py:553
  87.8 6.6 %collective-permute-start.20 = (f32[4,16,256]{2,1,0:T(8,128)S(1)}, f32[4,16,256]{2,1,0:T(8,128)S(1)}, u32[]{:S(2)}, u32[]{:S(2)}) collective-permute-start(f32[4,16,256]{2,1,0:T(8,128)S(1)} %get-tuple-element.86), channel_id=1, source_target_pairs={{0,16},{16,0},{32,48},{48,32},{64,80},{80,64},{96,112},{112,96},{1... | collective-permute-start | bytes 196616 | tf_op jit(solution)/shard_map/ppermute | solution.py:553
  87.8 12.1 %collective-permute-start.19 = (f32[8,1536]{1,0:T(8,128)S(1)}, f32[8,1536]{1,0:T(8,128)S(1)}, u32[]{:S(2)}, u32[]{:S(2)}) collective-permute-start(f32[8,1536]{1,0:T(8,128)S(1)} %get-tuple-element.75.w_ref), channel_id=1, source_target_pairs={{1,0},{2,1},{3,2},{4,3},{5,4},{6,5},{7,6},{8,7},{9,8},{10,9},{11,1... | collective-permute-start | bytes 147464 | tf_op jit(solution)/shard_map/ppermute | solution.py:547
  89.1 10.8 %collective-permute-start.18 = (f32[8,1536]{1,0:T(8,128)S(1)}, f32[8,1536]{1,0:T(8,128)S(1)}, u32[]{:S(2)}, u32[]{:S(2)}) collective-permute-start(f32[8,1536]{1,0:T(8,128)S(1)} %get-tuple-element.75.w_ref), channel_id=1, source_target_pairs={{0,1},{1,2},{2,3},{3,4},{4,5},{5,6},{6,7},{7,8},{8,9},{9,10},{10,1... | collective-permute-start | bytes 147464 | tf_op jit(solution)/shard_map/ppermute | solution.py:550
  94.4 9.3 %collective-permute-start.21 = (f32[2,16,256]{2,1,0:T(8,128)S(1)}, f32[2,16,256]{2,1,0:T(8,128)S(1)}, u32[]{:S(2)}, u32[]{:S(2)}) collective-permute-start(f32[2,16,256]{2,1,0:T(8,128)S(1)} %get-tuple-element.88), channel_id=1, source_target_pairs={{0,32},{16,48},{32,0},{48,16},{64,96},{80,112},{96,64},{112,80},{1... | collective-permute-start | bytes 98312 | tf_op jit(solution)/shard_map/ppermute | solution.py:553
  94.5 9.2 %collective-permute-start.22 = (f32[2,16,256]{2,1,0:T(8,128)S(1)}, f32[2,16,256]{2,1,0:T(8,128)S(1)}, u32[]{:S(2)}, u32[]{:S(2)}) collective-permute-start(f32[2,16,256]{2,1,0:T(8,128)S(1)} %get-tuple-element.89), channel_id=1, source_target_pairs={{0,64},{16,80},{32,96},{48,112},{64,0},{80,16},{96,32},{112,48},{1... | collective-permute-start | bytes 98312 | tf_op jit(solution)/shard_map/ppermute | solution.py:553
  96.9 6.9 %collective-permute-start.23 = (f32[2,16,256]{2,1,0:T(8,128)S(1)}, f32[2,16,256]{2,1,0:T(8,128)S(1)}, u32[]{:S(2)}, u32[]{:S(2)}) collective-permute-start(f32[2,16,256]{2,1,0:T(8,128)S(1)} %get-tuple-element.90), channel_id=1, source_target_pairs={{0,96},{16,112},{32,64},{48,80},{64,32},{80,48},{96,0},{112,16},{1... | collective-permute-start | bytes 98312 | tf_op jit(solution)/shard_map/ppermute | solution.py:553
  105.2 18.4 %all-to-all-start = ((f32[8,24,256]{2,1,0:T(8,128)}), f32[8,24,256]{2,1,0:T(8,128)S(1)}, u32[]{:S(2)}, u32[]{:S(2)}) async-start(f32[8,24,256]{2,1,0:T(8,128)} %get-tuple-element.93), calls=%async_computation | async-start | bytes 393216 | tf_op jit(solution)/shard_map/all_to_all | solution.py:556
  109.5 9.8 %collective-permute-start.24 = (f32[8,1536]{1,0:T(8,128)S(1)}, f32[8,1536]{1,0:T(8,128)S(1)}, u32[]{:S(2)}, u32[]{:S(2)}) collective-permute-start(f32[8,1536]{1,0:T(8,128)S(1)} %get-tuple-element.92), channel_id=1, source_target_pairs={{0,1},{1,2},{2,3},{3,4},{4,5},{5,6},{6,7},{7,8},{8,9},{9,10},{10,1... | collective-permute-start | bytes 147464 | tf_op jit(solution)/shard_map/ppermute | solution.py:550
  117.6 6.0 %collective-permute-start.25 = (f32[8,1536]{1,0:T(8,128)S(1)}, f32[8,1536]{1,0:T(8,128)S(1)}, u32[]{:S(2)}, u32[]{:S(2)}) collective-permute-start(f32[8,1536]{1,0:T(8,128)S(1)} %get-tuple-element.85.rl_ref), channel_id=1, source_target_pairs={{1,0},{2,1},{3,2},{4,3},{5,4},{6,5},{7,6},{8,7},{9,8},{10,9},{11,1... | collective-permute-start | bytes 147464 | tf_op jit(solution)/shard_map/ppermute | solution.py:547

commit v6 on v5

--- a/solution.py
+++ b/solution.py
@@ -145,7 +145,7 @@
     nt, _, _ = own.shape
     n = nt * TILE
 
-    def body(a_ref, k_ref, acc_ref, na, nb, va):
+    def body(a_ref, k_ref, acc_ref, na, va, nb):
         for i in range(nt):
             s = slice(i * TILE, (i + 1) * TILE)
             x = col_norms(a_ref[i, 0:TILE, :])
@@ -166,73 +166,90 @@
 
     return pl.pallas_call(
         body,
-        out_shape=(vmem_bf16(nt, n, TILE), f32(16, n)),
+        out_shape=(vmem_bf16(nt, n, TILE), f32(16, n), pltpu.VMEM((n, 128), F32), vmem_bf16(32, n)),
         in_specs=[VM],
-        out_specs=(VM, VM),
-        scratch_shapes=[pltpu.VMEM((n, 128), F32), pltpu.VMEM((8, n), F32), pltpu.VMEM((32, n), BF16)],
+        out_specs=(VM,) * 4,
+        scratch_shapes=[pltpu.VMEM((8, n), F32)],
         compiler_params=params(),
         name="local_first",
     )(own)
 
 
-def band_first(rows, right, after, left_side):
-    nt, _, _ = rows.shape
+def band_step(nt, a_ref, b_ref, na, va, nb, vb, before_ref, k_ref, col_ref, row_ref, acc):
+    acc[...] = jnp.zeros_like(acc)
+
+    def step(t, carry):
+        s = span(t)
+        b = b_ref[t, 0:TILE, :] * jnp.asarray(-2.0, BF16)
+        for i in range(nt):
+            c = slice(i * TILE, (i + 1) * TILE)
+            k_ref[t, c, :] = kernel_tile(a_ref[i, 0:TILE, :], b, na[c, :], nb[0:1, s])
+        k = k_ref[t]
+        col = fold_ones(mm(va[...], k, NN))
+        col_ref[:, s] = col if before_ref is None else before_ref[:, s] + col
+        acc[...] += mm(vb[:, s], k, NT)
+        return carry
+
+    lax.fori_loop(0, nt, step, 0, unroll=3)
+    row_ref[...] = fold_ones(acc[...])
+
+
+def band_own(own, norms, rhs, right, after):
+    nt, _, _ = own.shape
     n = nt * TILE
 
-    def body(a_ref, b_ref, before_ref, k_ref, col_ref, row_ref, na, nb, va, vb, acc):
-        v = lax.axis_index("dev")
-        has_rows = (v > 0).astype(F32) if left_side else 1.0
-        has_right = (v < lax.axis_size("dev") - 1).astype(F32)
+    def body(a_ref, na, va, b_ref, _, k_ref, col_ref, row_ref, nb, vb, acc):
+        has_right = (lax.axis_index("dev") < lax.axis_size("dev") - 1).astype(F32)
+        for i in range(nt):
+            s = slice(i * TILE, (i + 1) * TILE)
+            nb[:, s] = col_norms(b_ref[i, 0:TILE, :]).T[0:8]
+            vb[:, s] = rhs_ones(b_ref[i, TILE:, :], has_right)
+        band_step(nt, a_ref, b_ref, na, va, nb, vb, None, k_ref, col_ref, row_ref, acc)
+
+    return pl.pallas_call(
+        body,
+        out_shape=(vmem_bf16(nt, n, TILE), f32(16, n), f32(16, n), pltpu.VMEM((8, n), F32), vmem_bf16(32, n)),
+        in_specs=[VM] * 4 + [ANY],
+        out_specs=(VM,) * 5,
+        scratch_shapes=[pltpu.VMEM((32, n), F32)],
+        compiler_params=params(),
+        name="band_own",
+    )(own, norms, rhs, right, after)
+
+
+def band_left(left, right, right_norms, right_rhs, before):
+    nt, _, _ = left.shape
+    n = nt * TILE
+
+    def body(a_ref, b_ref, nb, vb, before_ref, k_ref, col_ref, row_ref, na, va, acc):
+        has_left = (lax.axis_index("dev") > 0).astype(F32)
         for i in range(nt):
             s = slice(i * TILE, (i + 1) * TILE)
             na[s, :] = col_norms(a_ref[i, 0:TILE, :])
-            nb[:, s] = col_norms(b_ref[i, 0:TILE, :]).T[0:8]
-            va[:, s] = rhs_ones(a_ref[i, TILE:, :], has_rows)
-            vb[:, s] = rhs_ones(b_ref[i, TILE:, :], has_right)
-        acc[...] = jnp.zeros_like(acc)
-
-        def step(t, carry):
-            s = span(t)
-            b = b_ref[t, 0:TILE, :] * jnp.asarray(-2.0, BF16)
-            for i in range(nt):
-                c = slice(i * TILE, (i + 1) * TILE)
-                k_ref[t, c, :] = kernel_tile(a_ref[i, 0:TILE, :], b, na[c, :], nb[0:1, s])
-            k = k_ref[t]
-            col = fold_ones(mm(va[...], k, NN))
-            col_ref[:, s] = before_ref[:, s] + col if left_side else col
-            acc[...] += mm(vb[:, s], k, NT)
-            return carry
-
-        lax.fori_loop(0, nt, step, 0, unroll=2)
-        row_ref[...] = fold_ones(acc[...])
+            va[:, s] = rhs_ones(a_ref[i, TILE:, :], has_left)
+        band_step(nt, a_ref, b_ref, na, va, nb, vb, before_ref, k_ref, col_ref, row_ref, acc)
 
     return pl.pallas_call(
         body,
         out_shape=(vmem_bf16(nt, n, TILE), f32(16, n), f32(16, n)),
-        in_specs=[VM, VM, VM if left_side else ANY],
+        in_specs=[VM] * 5,
         out_specs=(VM,) * 3,
-        scratch_shapes=[
-            pltpu.VMEM((n, 128), F32),
-            pltpu.VMEM((8, n), F32),
-            pltpu.VMEM((32, n), BF16),
-            pltpu.VMEM((32, n), BF16),
-            pltpu.VMEM((32, n), F32),
-        ],
-        compiler_params=params(),
-        name="band_left" if left_side else "band_own",
-    )(rows, right, after)
-
-
-def cross_first(ks, table, own, tiles, after):
+        scratch_shapes=[pltpu.VMEM((n, 128), F32), pltpu.VMEM((32, n), BF16), pltpu.VMEM((32, n), F32)],
+        compiler_params=params(),
+        name="band_left",
+    )(left, right, right_norms, right_rhs, before)
+
+
+def cross_first(ks, table, own, norms, rhs, tiles, after):
     nt, _, d = own.shape
     n = nt * TILE
     m = len(ks)
     slots = 2 * m
 
-    def body(q_ref, a_ref, _, *refs):
+    def body(q_ref, a_ref, na, va, _, *refs):
         tile_refs = refs[:m]
         k_ref, row_ref, *cols = refs[m : 2 * m + 2]
-        buf, jobs, sems, na, va, acc, nb, col = refs[2 * m + 2 :]
+        buf, jobs, sems, acc, nb, col = refs[2 * m + 2 :]
         g = lax.axis_index("group")
         count = jnp.int32(0)
         for i, k in enumerate(ks):
@@ -245,10 +262,6 @@
                     jobs[count] = 2 * i + c
 
                 count = count + live.astype(jnp.int32)
-        for i in range(nt):
-            s = slice(i * TILE, (i + 1) * TILE)
-            na[s, :] = col_norms(a_ref[i, 0:TILE, :])
-            va[:, s] = rhs_ones(a_ref[i, TILE:, :], 1.0)
         acc[...] = jnp.zeros_like(acc)
 
         def arrive(j, carry):
@@ -281,20 +294,18 @@
     return pl.pallas_call(
         body,
         out_shape=[vmem_bf16(slots, n, TILE), f32(16, n)] + [f32(2, 16, TILE)] * m,
-        in_specs=[SMEM, VM, ANY] + [ANY] * m,
+        in_specs=[SMEM, VM, VM, VM, ANY] + [ANY] * m,
         out_specs=[VM] * (2 + m),
         scratch_shapes=[
             pltpu.VMEM((slots, TILE + EXTRA, d), BF16),
             pltpu.SMEM((slots,), jnp.int32),
             pltpu.SemaphoreType.DMA((slots,)),
-            pltpu.VMEM((n, 128), F32),
-            pltpu.VMEM((32, n), BF16),
             pltpu.VMEM((32, n), F32),
             pltpu.VMEM((2, 8, TILE), F32),
             pltpu.VMEM((slots, 16, TILE), F32),
         ],
         compiler_params=params(),
-    )(table, own, after, *tiles)
+    )(table, own, norms, rhs, after, *tiles)
 
 
 def combine(table, r, parts, ret):
@@ -561,10 +572,10 @@
         arrived[k] = swap(x, k)
     left = left_of(own)
     right = right_of(own)
-    k_local, acc_local = local_first(own)
+    k_local, acc_local, norms, rhs = local_first(own)
 
     def cross(stage, after):
-        return cross_first(stage, table, own, [arrived[k] for k in stage], after)
+        return cross_first(stage, table, own, norms, rhs, [arrived[k] for k in stage], after)
 
     ret = {}
 
@@ -578,8 +589,8 @@
         arrived[k] = swap(x, k)
     k_b, row_b, *col_b = cross(STAGES[1], row_a)
     give_back(col_b, STAGES[1])
-    k_own, col_own, acc_band = band_first(own, right, row_b, False)
-    k_left, to_r, to_l = band_first(left, right, col_own, True)
+    k_own, col_own, acc_band, right_norms, right_rhs = band_own(own, norms, rhs, right, row_b)
+    k_left, to_r, to_l = band_left(left, right, right_norms, right_rhs, col_own)
     from_left, from_right = left_of(to_r), right_of(to_l)
     k_c, row_c, *col_c = cross(STAGES[2], to_l)
     give_back(col_c, STAGES[2])

time: 145 us -> 141 us (0.972)
  Pallas kernels: 35.7 us -> 32.5 us
  waiting for transfers between devices: 30.5 us -> 32.1 us
  starting transfers between devices: 58.3 us -> 56.7 us
    pallas_call x3, Pallas kernels: 21.4 us -> 19.1 us  [the longest x1 6.69 us: band_own(): pl.pallas_call(body, out_shape=(vmem_bf16(nt, n, TILE), f32(16, n), f32(1...]
    ppermute x18, starting transfers between devices: 23.9 us -> 22 us  [swap(): return lax.ppermute(x, 'group', [(i, i ^ k) for i in range(8)])]
    ppermute x18, waiting for transfers between devices: 25.8 us -> 27.4 us  [swap(): return lax.ppermute(x, 'group', [(i, i ^ k) for i in range(8)])]
  transfers between devices with their start and end apart: 27 -> 27, of which waited for: 9 -> 10; matrix products, arithmetic and copies ran while one was open for 0% -> 0% of each run, Pallas kernels for 20% -> 18%
where the time goes in v6:
time: 141 us
  starting transfers between devices  56.7 us (40%)
  Pallas kernels  32.5 us (23%)
  waiting for transfers between devices  32.1 us (23%)
  blocking collectives  18.8 us (13%)
    ppermute x18, waiting for transfers between devices, swap(): return lax.ppermute(x, 'group', [(i, i ^ k) for i in range(8)])  27.4 us
    ppermute x4, starting transfers between devices, left_of(): return lax.ppermute(x, 'dev', to_right)  25.1 us
    ppermute x18, starting transfers between devices, swap(): return lax.ppermute(x, 'group', [(i, i ^ k) for i in range(8)])  22 us
    all_to_all x1, blocking collectives, trade(): return lax.all_to_all(x, axis, split_axis=0, concat_axis=0, tiled=True)  18.8 us
    pallas_call x1, Pallas kernels, band_own(): pl.pallas_call(body, out_shape=(vmem_bf16(nt, n, TILE), f32(16, n), f32(1...  6.69 us
    pallas_call x1, Pallas kernels, band_left(): pl.pallas_call(body, out_shape=(vmem_bf16(nt, n, TILE), f32(16, n), f32(1...  6.62 us
    pallas_call x1, Pallas kernels, local_first(): pl.pallas_call(body, out_shape=(vmem_bf16(nt, n, TILE), f32(16, n), pltpu...  5.84 us
    ppermute x4, starting transfers between devices, right_of(): return lax.ppermute(x, 'dev', to_left)  5.17 us
  transfers between devices with their start and end apart: 27, of which 10 were waited for; matrix products, arithmetic and copies ran while one was open for 0% of the time, Pallas kernels for 18%

profile of v6, /device:TPU:0, one launch (start us, length us, event | category | flops | bytes accessed | tf_op | source)
XLA Modules:
  0.0 141.0 jit_solution(3275406009357821211)
XLA Ops:
  0.6 2.6 %prep.1 = (s32[32]{0:T(128)S(1)}, bf16[6,264,512]{2,1,0:T(8,128)(2,1)S(1)}, bf16[2,264,512]{2,1,0:T(8,128)(2,1)S(1)}, bf16[2,264,512]{2,1,0:T(8,128)(2,1)S(1)}, ...) custom-call(s32[8,8,2,16]{3,2,1,0:T(2,128)} %bitcast.1, ...), custom_call_target="tpu_custom_call" | custom-call | tf_op jit(solution)/shard_map/prep/pallas_call | solution.py:111
  3.2 1.3 collective-permute-start
  4.5 4.6 %collective-permute-start.6 = (bf16[6,264,512]{2,1,0:T(8,128)(2,1)S(1)}, bf16[6,264,512]{2,1,0:T(8,128)(2,1)S(1)}, u32[]{:S(2)}, u32[]{:S(2)}) collective-permute-start(bf16[6,264,512]{2,1,0:T(8,128)(2,1)S(1)} %get-tuple-element.54.a_ref), channel_id=1, source_target_pairs={{0,1},{1,2},{2,3},{3,4},{4,5},{5,6},{6,7},{7,8},{8,9},{9,10},{10,1... | collective-permute-start | bytes 4866056 | tf_op jit(solution)/shard_map/ppermute | solution.py:561
  9.1 2.1 %collective-permute-start.1 = (bf16[2,264,512]{2,1,0:T(8,128)(2,1)S(1)}, bf16[2,264,512]{2,1,0:T(8,128)(2,1)S(1)}, u32[]{:S(2)}, u32[]{:S(2)}) collective-permute-start(bf16[2,264,512]{2,1,0:T(8,128)(2,1)S(1)} %get-tuple-element.58), channel_id=1, source_target_pairs={{0,32},{16,48},{32,0},{48,16},{64,96},{80,112},{96,64},{112,80},{1... | collective-permute-start | bytes 1622024 | tf_op jit(solution)/shard_map/ppermute | solution.py:564
  11.3 2.5 %collective-permute-start.2 = (bf16[2,264,512]{2,1,0:T(8,128)(2,1)S(1)}, bf16[2,264,512]{2,1,0:T(8,128)(2,1)S(1)}, u32[]{:S(2)}, u32[]{:S(2)}) collective-permute-start(bf16[2,264,512]{2,1,0:T(8,128)(2,1)S(1)} %get-tuple-element.59), channel_id=1, source_target_pairs={{0,96},{16,112},{32,64},{48,80},{64,32},{80,48},{96,0},{112,16},{1... | collective-permute-start | bytes 1622024 | tf_op jit(solution)/shard_map/ppermute | solution.py:564
  13.8 9.2 %collective-permute-done.1.refs_0_ = bf16[2,264,512]{2,1,0:T(8,128)(2,1)S(1)} collective-permute-done((bf16[2,264,512]{2,1,0:T(8,128)(2,1)S(1)}, bf16[2,264,512]{2,1,0:T(8,128)(2,1)S(1)}, u32[]{:S(2)}, u32[]{:S(2)}) %collective-permute-start.1) | collective-permute-done | bytes 540704 | tf_op jit(solution)/shard_map/ppermute | solution.py:564
  23.0 2.7 %collective-permute-done.2.refs_1_ = bf16[2,264,512]{2,1,0:T(8,128)(2,1)S(1)} collective-permute-done((bf16[2,264,512]{2,1,0:T(8,128)(2,1)S(1)}, bf16[2,264,512]{2,1,0:T(8,128)(2,1)S(1)}, u32[]{:S(2)}, u32[]{:S(2)}) %collective-permute-start.2) | collective-permute-done | bytes 540704 | tf_op jit(solution)/shard_map/ppermute | solution.py:564
  25.6 1.3 collective-permute-start.5
  27.0 5.8 %local_first.1 = (bf16[6,1536,256]{2,1,0:T(8,128)(2,1)S(1)}, f32[16,1536]{1,0:T(8,128)S(1)}, f32[1536,128]{1,0:T(8,128)S(1)}, bf16[32,1536]{1,0:T(8,128)(2,1)S(1)}) custom-call(bf16[6,264,512]{2,1,0:T(8,128)(2,1)S(1)} %get-tuple-element.54.a_ref), custom_call_target="tpu_custom_call" | custom-call | tf_op jit(solution)/shard_map/local_first/pallas_call | solution.py:167
  32.8 0.7 shard_map.50
  33.5 3.7 %collective-permute-done.4.refs_0_.refs_3_ = bf16[2,264,512]{2,1,0:T(8,128)(2,1)S(1)} collective-permute-done((bf16[2,264,512]{2,1,0:T(8,128)(2,1)S(1)}, bf16[2,264,512]{2,1,0:T(8,128)(2,1)S(1)}, u32[]{:S(2)}, u32[]{:S(2)}) %collective-permute-start.4) | collective-permute-done | bytes 540704 | tf_op jit(solution)/shard_map/ppermute | solution.py:564
  37.3 4.0 %collective-permute-done.5.refs_1_.refs_4_ = bf16[2,264,512]{2,1,0:T(8,128)(2,1)S(1)} collective-permute-done((bf16[2,264,512]{2,1,0:T(8,128)(2,1)S(1)}, bf16[2,264,512]{2,1,0:T(8,128)(2,1)S(1)}, u32[]{:S(2)}, u32[]{:S(2)}) %collective-permute-start.5) | collective-permute-done | bytes 540704 | tf_op jit(solution)/shard_map/ppermute | solution.py:564
  41.3 0.7 collective-permute-start.9
  42.0 2.1 %collective-permute-start.10 = (bf16[2,264,512]{2,1,0:T(8,128)(2,1)S(1)}, bf16[2,264,512]{2,1,0:T(8,128)(2,1)S(1)}, u32[]{:S(2)}, u32[]{:S(2)}) collective-permute-start(bf16[2,264,512]{2,1,0:T(8,128)(2,1)S(1)} %get-tuple-element.74), channel_id=1, source_target_pairs={{0,80},{16,64},{32,112},{48,96},{64,16},{80,0},{96,48},{112,32},{1... | collective-permute-start | bytes 1622024 | tf_op jit(solution)/shard_map/ppermute | solution.py:564
  44.1 0.4 collective-permute-start.11
  44.6 0.8 shard_map.51
  45.4 6.7 %band_own.1 = (bf16[6,1536,256]{2,1,0:T(8,128)(2,1)S(1)}, f32[16,1536]{1,0:T(8,128)S(1)}, f32[16,1536]{1,0:T(8,128)S(1)}, f32[8,1536]{1,0:T(8,128)S(1)}, bf16[32,1536]{1,0:T(8,128)(2,1)S(1)}) custom-call(bf16[6,264,512]{2,1,0:T(8,128)(2,1)S(1)} %get-tuple-element.54.a_ref, f32[1536,128]{1,0:T(8,128)S(1)} %get-tuple-element.56.na, ...), custom_call_target="tpu_custom_call" | custom-call | tf_op jit(solution)/shard_map/band_own/pallas_call | solution.py:209
  52.1 6.6 %band_left.1 = (bf16[6,1536,256]{2,1,0:T(8,128)(2,1)S(1)}, f32[16,1536]{1,0:T(8,128)S(1)}, f32[16,1536]{1,0:T(8,128)S(1)}) custom-call(bf16[6,264,512]{2,1,0:T(8,128)(2,1)S(1)} %collective-permute-done.6.a_ref, bf16[6,264,512]{2,1,0:T(8,128)(2,1)S(1)} %collective-permute-done.b_ref, f32[8,1536]{1,0:T(8,128)S(1)} %get-tuple-element.66.nb, ...), custom_call_target="tpu_custom_call" | custom-call | tf_op jit(solution)/shard_map/band_left/pallas_call | solution.py:232
  58.8 7.5 %collective-permute-start.7 = (f32[16,1536]{1,0:T(8,128)S(1)}, f32[16,1536]{1,0:T(8,128)S(1)}, u32[]{:S(2)}, u32[]{:S(2)}) collective-permute-start(f32[16,1536]{1,0:T(8,128)S(1)} %get-tuple-element.69), channel_id=1, source_target_pairs={{0,1},{1,2},{2,3},{3,4},{4,5},{5,6},{6,7},{7,8},{8,9},{9,10},{10,1... | collective-permute-start | bytes 294920 | tf_op jit(solution)/shard_map/ppermute | solution.py:561
  66.2 1.3 collective-permute-start.8
  67.5 0.6 collective-permute-done.11.refs_7_
  68.1 1.7 %collective-permute-start.12 = (f32[2,16,256]{2,1,0:T(8,128)S(1)}, f32[2,16,256]{2,1,0:T(8,128)S(1)}, u32[]{:S(2)}, u32[]{:S(2)}) collective-permute-start(f32[2,16,256]{2,1,0:T(8,128)S(1)} %get-tuple-element.77), channel_id=1, source_target_pairs={{0,96},{16,112},{32,64},{48,80},{64,32},{80,48},{96,0},{112,16},{1... | collective-permute-start | bytes 98312 | tf_op jit(solution)/shard_map/ppermute | solution.py:564
  69.8 0.4 collective-permute-start.14
  70.2 0.7 shard_map.52
  70.9 2.4 %collective-permute-done.12.refs_8_ = f32[2,16,256]{2,1,0:T(8,128)S(1)} collective-permute-done((f32[2,16,256]{2,1,0:T(8,128)S(1)}, f32[2,16,256]{2,1,0:T(8,128)S(1)}, u32[]{:S(2)}, u32[]{:S(2)}) %collective-permute-start.12) | collective-permute-done | bytes 32800 | tf_op jit(solution)/shard_map/ppermute | solution.py:564
  73.2 1.9 %collective-permute-start.15 = (f32[2,16,256]{2,1,0:T(8,128)S(1)}, f32[2,16,256]{2,1,0:T(8,128)S(1)}, u32[]{:S(2)}, u32[]{:S(2)}) collective-permute-start(f32[2,16,256]{2,1,0:T(8,128)S(1)} %get-tuple-element.80), channel_id=1, source_target_pairs={{0,112},{16,96},{32,80},{48,64},{64,48},{80,32},{96,16},{112,0},{1... | collective-permute-start | bytes 98312 | tf_op jit(solution)/shard_map/ppermute | solution.py:564
  75.1 4.0 %collective-permute-start.16 = (f32[2,16,256]{2,1,0:T(8,128)S(1)}, f32[2,16,256]{2,1,0:T(8,128)S(1)}, u32[]{:S(2)}, u32[]{:S(2)}) collective-permute-start(f32[2,16,256]{2,1,0:T(8,128)S(1)} %get-tuple-element.81), channel_id=1, source_target_pairs={{0,64},{16,80},{32,96},{48,112},{64,0},{80,16},{96,32},{112,48},{1... | collective-permute-start | bytes 98312 | tf_op jit(solution)/shard_map/ppermute | solution.py:564
  79.1 1.9 %collective-permute-done.16.refs_12_ = f32[2,16,256]{2,1,0:T(8,128)S(1)} collective-permute-done((f32[2,16,256]{2,1,0:T(8,128)S(1)}, f32[2,16,256]{2,1,0:T(8,128)S(1)}, u32[]{:S(2)}, u32[]{:S(2)}) %collective-permute-start.16) | collective-permute-done | bytes 32800 | tf_op jit(solution)/shard_map/ppermute | solution.py:564
  81.0 3.0 %collective-permute-done.17.refs_13_ = f32[2,16,256]{2,1,0:T(8,128)S(1)} collective-permute-done((f32[2,16,256]{2,1,0:T(8,128)S(1)}, f32[2,16,256]{2,1,0:T(8,128)S(1)}, u32[]{:S(2)}, u32[]{:S(2)}) %collective-permute-start.17) | collective-permute-done | bytes 32800 | tf_op jit(solution)/shard_map/ppermute | solution.py:564
  84.0 0.8 combine.1
  84.8 0.0 collective-permute-start.20
  84.8 1.3 collective-permute-start.19
  86.1 5.1 %collective-permute-start.18 = (f32[8,1536]{1,0:T(8,128)S(1)}, f32[8,1536]{1,0:T(8,128)S(1)}, u32[]{:S(2)}, u32[]{:S(2)}) collective-permute-start(f32[8,1536]{1,0:T(8,128)S(1)} %get-tuple-element.83.w_ref), channel_id=1, source_target_pairs={{0,1},{1,2},{2,3},{3,4},{4,5},{5,6},{6,7},{7,8},{8,9},{9,10},{10,1... | collective-permute-start | bytes 147464 | tf_op jit(solution)/shard_map/ppermute | solution.py:561
  91.2 0.2 collective-permute-start.21
  91.4 2.3 %collective-permute-start.22 = (f32[2,16,256]{2,1,0:T(8,128)S(1)}, f32[2,16,256]{2,1,0:T(8,128)S(1)}, u32[]{:S(2)}, u32[]{:S(2)}) collective-permute-start(f32[2,16,256]{2,1,0:T(8,128)S(1)} %get-tuple-element.97), channel_id=1, source_target_pairs={{0,64},{16,80},{32,96},{48,112},{64,0},{80,16},{96,32},{112,48},{1... | collective-permute-start | bytes 98312 | tf_op jit(solution)/shard_map/ppermute | solution.py:564
  93.8 2.2 %collective-permute-start.23 = (f32[2,16,256]{2,1,0:T(8,128)S(1)}, f32[2,16,256]{2,1,0:T(8,128)S(1)}, u32[]{:S(2)}, u32[]{:S(2)}) collective-permute-start(f32[2,16,256]{2,1,0:T(8,128)S(1)} %get-tuple-element.98), channel_id=1, source_target_pairs={{0,96},{16,112},{32,64},{48,80},{64,32},{80,48},{96,0},{112,16},{1... | collective-permute-start | bytes 98312 | tf_op jit(solution)/shard_map/ppermute | solution.py:564
  96.0 0.7 local_second.1._.loc_ref.refs_0_
  96.7 0.0 collective-permute-done.18.wl_ref
  96.7 3.8 %band_second.1 = (f32[8,1536]{1,0:T(8,128)S(1)}, f32[8,1536]{1,0:T(8,128)S(1)}, f32[8,1536]{1,0:T(8,128)S(1)}) custom-call(bf16[6,1536,256]{2,1,0:T(8,128)(2,1)S(1)} %get-tuple-element.86.kl_ref, bf16[6,1536,256]{2,1,0:T(8,128)(2,1)S(1)} %get-tuple-element.87.ko_ref, f32[8,1536]{1,0:T(8,128)S(1)} %collective-permute-done.18.wl_ref, ...), custom_call_target="tpu_custom_call" | custom-call | tf_op jit(solution)/shard_map/band_second/pallas_call | solution.py:408
  100.6 1.4 cross_second.1
  102.0 4.4 %all-to-all-start = ((f32[8,24,256]{2,1,0:T(8,128)}), f32[8,24,256]{2,1,0:T(8,128)S(1)}, u32[]{:S(2)}, u32[]{:S(2)}) async-start(f32[8,24,256]{2,1,0:T(8,128)} %get-tuple-element.101), calls=%async_computation | async-start | bytes 393216 | tf_op jit(solution)/shard_map/all_to_all | solution.py:567
  106.4 8.0 %collective-permute-start.24 = (f32[8,1536]{1,0:T(8,128)S(1)}, f32[8,1536]{1,0:T(8,128)S(1)}, u32[]{:S(2)}, u32[]{:S(2)}) collective-permute-start(f32[8,1536]{1,0:T(8,128)S(1)} %get-tuple-element.100), channel_id=1, source_target_pairs={{0,1},{1,2},{2,3},{3,4},{4,5},{5,6},{6,7},{7,8},{8,9},{9,10},{10,1... | collective-permute-start | bytes 147464 | tf_op jit(solution)/shard_map/ppermute | solution.py:561
  114.4 1.3 collective-permute-start.25
  115.7 0.4 collective-permute-done.24.refs_3_
  116.1 4.3 %collective-permute-done.25.refs_4_ = f32[8,1536]{1,0:T(8,128)S(1)} collective-permute-done((f32[8,1536]{1,0:T(8,128)S(1)}, f32[8,1536]{1,0:T(8,128)S(1)}, u32[]{:S(2)}, u32[]{:S(2)}) %collective-permute-start.25) | collective-permute-done | bytes 49184 | tf_op jit(solution)/shard_map/ppermute | solution.py:558
  120.4 0.7 group_sum.1
  121.1 18.8 %all_to_all.10.g_ref = f32[16,8,128]{2,1,0:T(8,128)S(1)} all-to-all(f32[16,8,128]{2,1,0:T(8,128)S(1)} %get-tuple-element.102), channel_id=1, replica_groups=mesh['group'=8,'dev'=16] {'dev'}, dimensions={0} | all-to-all | bytes 131072 | tf_op jit(solution)/shard_map/all_to_all | solution.py:567
  139.9 1.1 finish.1
  (24 shorter events, 0.1 us)
Async XLA Ops:
  3.2 42.2 %collective-permute-start = (bf16[6,264,512]{2,1,0:T(8,128)(2,1)S(1)}, bf16[6,264,512]{2,1,0:T(8,128)(2,1)S(1)}, u32[]{:S(2)}, u32[]{:S(2)}) collective-permute-start(bf16[6,264,512]{2,1,0:T(8,128)(2,1)S(1)} %get-tuple-element.54.a_ref), channel_id=1, source_target_pairs={{1,0},{2,1},{3,2},{4,3},{5,4},{6,5},{7,6},{8,7},{9,8},{10,9},{11,1... | collective-permute-start | bytes 4866056 | tf_op jit(solution)/shard_map/ppermute | solution.py:558
  4.5 47.6 %collective-permute-start.6 = (bf16[6,264,512]{2,1,0:T(8,128)(2,1)S(1)}, bf16[6,264,512]{2,1,0:T(8,128)(2,1)S(1)}, u32[]{:S(2)}, u32[]{:S(2)}) collective-permute-start(bf16[6,264,512]{2,1,0:T(8,128)(2,1)S(1)} %get-tuple-element.54.a_ref), channel_id=1, source_target_pairs={{0,1},{1,2},{2,3},{3,4},{4,5},{5,6},{6,7},{7,8},{8,9},{9,10},{10,1... | collective-permute-start | bytes 4866056 | tf_op jit(solution)/shard_map/ppermute | solution.py:561
  9.1 13.8 %collective-permute-start.1 = (bf16[2,264,512]{2,1,0:T(8,128)(2,1)S(1)}, bf16[2,264,512]{2,1,0:T(8,128)(2,1)S(1)}, u32[]{:S(2)}, u32[]{:S(2)}) collective-permute-start(bf16[2,264,512]{2,1,0:T(8,128)(2,1)S(1)} %get-tuple-element.58), channel_id=1, source_target_pairs={{0,32},{16,48},{32,0},{48,16},{64,96},{80,112},{96,64},{112,80},{1... | collective-permute-start | bytes 1622024 | tf_op jit(solution)/shard_map/ppermute | solution.py:564
  11.3 14.4 %collective-permute-start.2 = (bf16[2,264,512]{2,1,0:T(8,128)(2,1)S(1)}, bf16[2,264,512]{2,1,0:T(8,128)(2,1)S(1)}, u32[]{:S(2)}, u32[]{:S(2)}) collective-permute-start(bf16[2,264,512]{2,1,0:T(8,128)(2,1)S(1)} %get-tuple-element.59), channel_id=1, source_target_pairs={{0,96},{16,112},{32,64},{48,80},{64,32},{80,48},{96,0},{112,16},{1... | collective-permute-start | bytes 1622024 | tf_op jit(solution)/shard_map/ppermute | solution.py:564
  13.8 19.0 %collective-permute-start.3 = (bf16[2,264,512]{2,1,0:T(8,128)(2,1)S(1)}, bf16[2,264,512]{2,1,0:T(8,128)(2,1)S(1)}, u32[]{:S(2)}, u32[]{:S(2)}) collective-permute-start(bf16[2,264,512]{2,1,0:T(8,128)(2,1)S(1)} %get-tuple-element.60), channel_id=1, source_target_pairs={{0,16},{16,0},{32,48},{48,32},{64,80},{80,64},{96,112},{112,96},{1... | collective-permute-start | bytes 1622024 | tf_op jit(solution)/shard_map/ppermute | solution.py:564
  23.0 14.3 %collective-permute-start.4 = (bf16[2,264,512]{2,1,0:T(8,128)(2,1)S(1)}, bf16[2,264,512]{2,1,0:T(8,128)(2,1)S(1)}, u32[]{:S(2)}, u32[]{:S(2)}) collective-permute-start(bf16[2,264,512]{2,1,0:T(8,128)(2,1)S(1)} %get-tuple-element.62), channel_id=1, source_target_pairs={{0,48},{16,32},{32,16},{48,0},{64,112},{80,96},{96,80},{112,64},{1... | collective-permute-start | bytes 1622024 | tf_op jit(solution)/shard_map/ppermute | solution.py:564
  25.6 15.7 %collective-permute-start.5 = (bf16[2,264,512]{2,1,0:T(8,128)(2,1)S(1)}, bf16[2,264,512]{2,1,0:T(8,128)(2,1)S(1)}, u32[]{:S(2)}, u32[]{:S(2)}) collective-permute-start(bf16[2,264,512]{2,1,0:T(8,128)(2,1)S(1)} %get-tuple-element.63), channel_id=1, source_target_pairs={{0,112},{16,96},{32,80},{48,64},{64,48},{80,32},{96,16},{112,0},{1... | collective-permute-start | bytes 1622024 | tf_op jit(solution)/shard_map/ppermute | solution.py:564
  41.3 28.5 %collective-permute-start.9 = (bf16[2,264,512]{2,1,0:T(8,128)(2,1)S(1)}, bf16[2,264,512]{2,1,0:T(8,128)(2,1)S(1)}, u32[]{:S(2)}, u32[]{:S(2)}) collective-permute-start(bf16[2,264,512]{2,1,0:T(8,128)(2,1)S(1)} %get-tuple-element.73), channel_id=1, source_target_pairs={{0,64},{16,80},{32,96},{48,112},{64,0},{80,16},{96,32},{112,48},{1... | collective-permute-start | bytes 1622024 | tf_op jit(solution)/shard_map/ppermute | solution.py:564
  42.0 27.8 %collective-permute-start.10 = (bf16[2,264,512]{2,1,0:T(8,128)(2,1)S(1)}, bf16[2,264,512]{2,1,0:T(8,128)(2,1)S(1)}, u32[]{:S(2)}, u32[]{:S(2)}) collective-permute-start(bf16[2,264,512]{2,1,0:T(8,128)(2,1)S(1)} %get-tuple-element.74), channel_id=1, source_target_pairs={{0,80},{16,64},{32,112},{48,96},{64,16},{80,0},{96,48},{112,32},{1... | collective-permute-start | bytes 1622024 | tf_op jit(solution)/shard_map/ppermute | solution.py:564
  44.1 24.0 %collective-permute-start.11 = (f32[2,16,256]{2,1,0:T(8,128)S(1)}, f32[2,16,256]{2,1,0:T(8,128)S(1)}, u32[]{:S(2)}, u32[]{:S(2)}) collective-permute-start(f32[2,16,256]{2,1,0:T(8,128)S(1)} %get-tuple-element.76), channel_id=1, source_target_pairs={{0,32},{16,48},{32,0},{48,16},{64,96},{80,112},{96,64},{112,80},{1... | collective-permute-start | bytes 98312 | tf_op jit(solution)/shard_map/ppermute | solution.py:564
  52.1 31.8 %copy-start = (f32[8,1536]{1,0:T(8,128)S(1)}, f32[8,1536]{1,0:T(8,128)}, u32[]{:S(2)}) copy-start(f32[8,1536]{1,0:T(8,128)} %r_ref.3) | copy-start | bytes 147460
  58.8 25.2 %collective-permute-start.7 = (f32[16,1536]{1,0:T(8,128)S(1)}, f32[16,1536]{1,0:T(8,128)S(1)}, u32[]{:S(2)}, u32[]{:S(2)}) collective-permute-start(f32[16,1536]{1,0:T(8,128)S(1)} %get-tuple-element.69), channel_id=1, source_target_pairs={{0,1},{1,2},{2,3},{3,4},{4,5},{5,6},{6,7},{7,8},{8,9},{9,10},{10,1... | collective-permute-start | bytes 294920 | tf_op jit(solution)/shard_map/ppermute | solution.py:561
  66.2 17.7 %collective-permute-start.8 = (f32[16,1536]{1,0:T(8,128)S(1)}, f32[16,1536]{1,0:T(8,128)S(1)}, u32[]{:S(2)}, u32[]{:S(2)}) collective-permute-start(f32[16,1536]{1,0:T(8,128)S(1)} %get-tuple-element.70._), channel_id=1, source_target_pairs={{1,0},{2,1},{3,2},{4,3},{5,4},{6,5},{7,6},{8,7},{9,8},{10,9},{11,1... | collective-permute-start | bytes 294920 | tf_op jit(solution)/shard_map/ppermute | solution.py:558
  68.1 5.1 %collective-permute-start.12 = (f32[2,16,256]{2,1,0:T(8,128)S(1)}, f32[2,16,256]{2,1,0:T(8,128)S(1)}, u32[]{:S(2)}, u32[]{:S(2)}) collective-permute-start(f32[2,16,256]{2,1,0:T(8,128)S(1)} %get-tuple-element.77), channel_id=1, source_target_pairs={{0,96},{16,112},{32,64},{48,80},{64,32},{80,48},{96,0},{112,16},{1... | collective-permute-start | bytes 98312 | tf_op jit(solution)/shard_map/ppermute | solution.py:564
  69.8 5.3 %collective-permute-start.13 = (f32[2,16,256]{2,1,0:T(8,128)S(1)}, f32[2,16,256]{2,1,0:T(8,128)S(1)}, u32[]{:S(2)}, u32[]{:S(2)}) collective-permute-start(f32[2,16,256]{2,1,0:T(8,128)S(1)} %get-tuple-element.78), channel_id=1, source_target_pairs={{0,16},{16,0},{32,48},{48,32},{64,80},{80,64},{96,112},{112,96},{1... | collective-permute-start | bytes 98312 | tf_op jit(solution)/shard_map/ppermute | solution.py:564
  69.8 9.3 %collective-permute-start.14 = (f32[2,16,256]{2,1,0:T(8,128)S(1)}, f32[2,16,256]{2,1,0:T(8,128)S(1)}, u32[]{:S(2)}, u32[]{:S(2)}) collective-permute-start(f32[2,16,256]{2,1,0:T(8,128)S(1)} %get-tuple-element.79), channel_id=1, source_target_pairs={{0,48},{16,32},{32,16},{48,0},{64,112},{80,96},{96,80},{112,64},{1... | collective-permute-start | bytes 98312 | tf_op jit(solution)/shard_map/ppermute | solution.py:564
  73.2 5.9 %collective-permute-start.15 = (f32[2,16,256]{2,1,0:T(8,128)S(1)}, f32[2,16,256]{2,1,0:T(8,128)S(1)}, u32[]{:S(2)}, u32[]{:S(2)}) collective-permute-start(f32[2,16,256]{2,1,0:T(8,128)S(1)} %get-tuple-element.80), channel_id=1, source_target_pairs={{0,112},{16,96},{32,80},{48,64},{64,48},{80,32},{96,16},{112,0},{1... | collective-permute-start | bytes 98312 | tf_op jit(solution)/shard_map/ppermute | solution.py:564
  75.1 5.9 %collective-permute-start.16 = (f32[2,16,256]{2,1,0:T(8,128)S(1)}, f32[2,16,256]{2,1,0:T(8,128)S(1)}, u32[]{:S(2)}, u32[]{:S(2)}) collective-permute-start(f32[2,16,256]{2,1,0:T(8,128)S(1)} %get-tuple-element.81), channel_id=1, source_target_pairs={{0,64},{16,80},{32,96},{48,112},{64,0},{80,16},{96,32},{112,48},{1... | collective-permute-start | bytes 98312 | tf_op jit(solution)/shard_map/ppermute | solution.py:564
  79.1 4.8 %collective-permute-start.17 = (f32[2,16,256]{2,1,0:T(8,128)S(1)}, f32[2,16,256]{2,1,0:T(8,128)S(1)}, u32[]{:S(2)}, u32[]{:S(2)}) collective-permute-start(f32[2,16,256]{2,1,0:T(8,128)S(1)} %get-tuple-element.82), channel_id=1, source_target_pairs={{0,80},{16,64},{32,112},{48,96},{64,16},{80,0},{96,48},{112,32},{1... | collective-permute-start | bytes 98312 | tf_op jit(solution)/shard_map/ppermute | solution.py:564
  84.8 6.4 %collective-permute-start.20 = (f32[4,16,256]{2,1,0:T(8,128)S(1)}, f32[4,16,256]{2,1,0:T(8,128)S(1)}, u32[]{:S(2)}, u32[]{:S(2)}) collective-permute-start(f32[4,16,256]{2,1,0:T(8,128)S(1)} %get-tuple-element.94), channel_id=1, source_target_pairs={{0,16},{16,0},{32,48},{48,32},{64,80},{80,64},{96,112},{112,96},{1... | collective-permute-start | bytes 196616 | tf_op jit(solution)/shard_map/ppermute | solution.py:564
  84.8 11.9 %collective-permute-start.19 = (f32[8,1536]{1,0:T(8,128)S(1)}, f32[8,1536]{1,0:T(8,128)S(1)}, u32[]{:S(2)}, u32[]{:S(2)}) collective-permute-start(f32[8,1536]{1,0:T(8,128)S(1)} %get-tuple-element.83.w_ref), channel_id=1, source_target_pairs={{1,0},{2,1},{3,2},{4,3},{5,4},{6,5},{7,6},{8,7},{9,8},{10,9},{11,1... | collective-permute-start | bytes 147464 | tf_op jit(solution)/shard_map/ppermute | solution.py:558
  86.1 10.6 %collective-permute-start.18 = (f32[8,1536]{1,0:T(8,128)S(1)}, f32[8,1536]{1,0:T(8,128)S(1)}, u32[]{:S(2)}, u32[]{:S(2)}) collective-permute-start(f32[8,1536]{1,0:T(8,128)S(1)} %get-tuple-element.83.w_ref), channel_id=1, source_target_pairs={{0,1},{1,2},{2,3},{3,4},{4,5},{5,6},{6,7},{7,8},{8,9},{9,10},{10,1... | collective-permute-start | bytes 147464 | tf_op jit(solution)/shard_map/ppermute | solution.py:561
  91.2 9.3 %collective-permute-start.21 = (f32[2,16,256]{2,1,0:T(8,128)S(1)}, f32[2,16,256]{2,1,0:T(8,128)S(1)}, u32[]{:S(2)}, u32[]{:S(2)}) collective-permute-start(f32[2,16,256]{2,1,0:T(8,128)S(1)} %get-tuple-element.96), channel_id=1, source_target_pairs={{0,32},{16,48},{32,0},{48,16},{64,96},{80,112},{96,64},{112,80},{1... | collective-permute-start | bytes 98312 | tf_op jit(solution)/shard_map/ppermute | solution.py:564
  91.4 9.1 %collective-permute-start.22 = (f32[2,16,256]{2,1,0:T(8,128)S(1)}, f32[2,16,256]{2,1,0:T(8,128)S(1)}, u32[]{:S(2)}, u32[]{:S(2)}) collective-permute-start(f32[2,16,256]{2,1,0:T(8,128)S(1)} %get-tuple-element.97), channel_id=1, source_target_pairs={{0,64},{16,80},{32,96},{48,112},{64,0},{80,16},{96,32},{112,48},{1... | collective-permute-start | bytes 98312 | tf_op jit(solution)/shard_map/ppermute | solution.py:564
  93.8 6.8 %collective-permute-start.23 = (f32[2,16,256]{2,1,0:T(8,128)S(1)}, f32[2,16,256]{2,1,0:T(8,128)S(1)}, u32[]{:S(2)}, u32[]{:S(2)}) collective-permute-start(f32[2,16,256]{2,1,0:T(8,128)S(1)} %get-tuple-element.98), channel_id=1, source_target_pairs={{0,96},{16,112},{32,64},{48,80},{64,32},{80,48},{96,0},{112,16},{1... | collective-permute-start | bytes 98312 | tf_op jit(solution)/shard_map/ppermute | solution.py:564
  102.0 18.4 %all-to-all-start = ((f32[8,24,256]{2,1,0:T(8,128)}), f32[8,24,256]{2,1,0:T(8,128)S(1)}, u32[]{:S(2)}, u32[]{:S(2)}) async-start(f32[8,24,256]{2,1,0:T(8,128)} %get-tuple-element.101), calls=%async_computation | async-start | bytes 393216 | tf_op jit(solution)/shard_map/all_to_all | solution.py:567
  106.4 9.7 %collective-permute-start.24 = (f32[8,1536]{1,0:T(8,128)S(1)}, f32[8,1536]{1,0:T(8,128)S(1)}, u32[]{:S(2)}, u32[]{:S(2)}) collective-permute-start(f32[8,1536]{1,0:T(8,128)S(1)} %get-tuple-element.100), channel_id=1, source_target_pairs={{0,1},{1,2},{2,3},{3,4},{4,5},{5,6},{6,7},{7,8},{8,9},{9,10},{10,1... | collective-permute-start | bytes 147464 | tf_op jit(solution)/shard_map/ppermute | solution.py:561
  114.4 6.0 %collective-permute-start.25 = (f32[8,1536]{1,0:T(8,128)S(1)}, f32[8,1536]{1,0:T(8,128)S(1)}, u32[]{:S(2)}, u32[]{:S(2)}) collective-permute-start(f32[8,1536]{1,0:T(8,128)S(1)} %get-tuple-element.93.rl_ref), channel_id=1, source_target_pairs={{1,0},{2,1},{3,2},{4,3},{5,4},{6,5},{7,6},{8,7},{9,8},{10,9},{11,1... | collective-permute-start | bytes 147464 | tf_op jit(solution)/shard_map/ppermute | solution.py:558

commit v7 on v6

--- a/solution.py
+++ b/solution.py
@@ -153,16 +153,13 @@
             nb[:, s] = x.T[0:8]
             va[:, s] = rhs_ones(a_ref[i, TILE:, :], 1.0)
 
-        def step(t, carry):
-            s = span(t)
+        for t in range(nt):
+            s = slice(t * TILE, (t + 1) * TILE)
             b = a_ref[t, 0:TILE, :] * jnp.asarray(-2.0, BF16)
             for i in range(nt):
                 c = slice(i * TILE, (i + 1) * TILE)
                 k_ref[t, c, :] = kernel_tile(a_ref[i, 0:TILE, :], b, na[c, :], nb[0:1, s])
             acc_ref[:, s] = fold_ones(mm(va[...], k_ref[t], NN))
-            return carry
-
-        lax.fori_loop(0, nt, step, 0, unroll=2)
 
     return pl.pallas_call(
         body,
@@ -178,8 +175,8 @@
 def band_step(nt, a_ref, b_ref, na, va, nb, vb, before_ref, k_ref, col_ref, row_ref, acc):
     acc[...] = jnp.zeros_like(acc)
 
-    def step(t, carry):
-        s = span(t)
+    for t in range(nt):
+        s = slice(t * TILE, (t + 1) * TILE)
         b = b_ref[t, 0:TILE, :] * jnp.asarray(-2.0, BF16)
         for i in range(nt):
             c = slice(i * TILE, (i + 1) * TILE)
@@ -188,9 +185,6 @@
         col = fold_ones(mm(va[...], k, NN))
         col_ref[:, s] = col if before_ref is None else before_ref[:, s] + col
         acc[...] += mm(vb[:, s], k, NT)
-        return carry
-
-    lax.fori_loop(0, nt, step, 0, unroll=3)
     row_ref[...] = fold_ones(acc[...])
 
 

time: 141 us -> 141 us (level)
  waiting for transfers between devices: 32.1 us -> 34.2 us
  Pallas kernels: 32.5 us -> 30.5 us
    ppermute x18, waiting for transfers between devices: 27.4 us -> 29.4 us  [swap(): return lax.ppermute(x, 'group', [(i, i ^ k) for i in range(8)])]
  transfers between devices with their start and end apart: 27 -> 27, of which waited for: 10 -> 10; matrix products, arithmetic and copies ran while one was open for 0% -> 0% of each run, Pallas kernels for 18% -> 17%
where the time goes in v7:
time: 141 us; the launch traced here: 140 us
  starting transfers between devices  55.6 us (39%)
  waiting for transfers between devices  34.2 us (24%)
  Pallas kernels  30.5 us (22%)
  blocking collectives  19.1 us (14%)
    ppermute x18, waiting for transfers between devices, swap(): return lax.ppermute(x, 'group', [(i, i ^ k) for i in range(8)])  29.4 us
    ppermute x4, starting transfers between devices, left_of(): return lax.ppermute(x, 'dev', to_right)  23.8 us
    ppermute x18, starting transfers between devices, swap(): return lax.ppermute(x, 'group', [(i, i ^ k) for i in range(8)])  21.7 us
    all_to_all x1, blocking collectives, trade(): return lax.all_to_all(x, axis, split_axis=0, concat_axis=0, tiled=True)  19.1 us
    pallas_call x1, Pallas kernels, band_left(): pl.pallas_call(body, out_shape=(vmem_bf16(nt, n, TILE), f32(16, n), f32(1...  6.23 us
    pallas_call x1, Pallas kernels, band_own(): pl.pallas_call(body, out_shape=(vmem_bf16(nt, n, TILE), f32(16, n), f32(1...  5.97 us
    ppermute x4, starting transfers between devices, right_of(): return lax.ppermute(x, 'dev', to_left)  5.17 us
    pallas_call x1, Pallas kernels, local_first(): pl.pallas_call(body, out_shape=(vmem_bf16(nt, n, TILE), f32(16, n), pltpu...  4.98 us
  transfers between devices with their start and end apart: 27, of which 10 were waited for; matrix products, arithmetic and copies ran while one was open for 0% of the time, Pallas kernels for 17%

profile of v7, /device:TPU:0, one launch (start us, length us, event | category | flops | bytes accessed | tf_op | source)
XLA Modules:
  0.0 140.2 jit_solution(3130539554924350536)
XLA Ops:
  0.6 2.6 %prep.1 = (s32[32]{0:T(128)S(1)}, bf16[6,264,512]{2,1,0:T(8,128)(2,1)S(1)}, bf16[2,264,512]{2,1,0:T(8,128)(2,1)S(1)}, bf16[2,264,512]{2,1,0:T(8,128)(2,1)S(1)}, ...) custom-call(s32[8,8,2,16]{3,2,1,0:T(2,128)} %bitcast.1, ...), custom_call_target="tpu_custom_call" | custom-call | tf_op jit(solution)/shard_map/prep/pallas_call | solution.py:111
  3.2 1.3 collective-permute-start
  4.5 4.6 %collective-permute-start.6 = (bf16[6,264,512]{2,1,0:T(8,128)(2,1)S(1)}, bf16[6,264,512]{2,1,0:T(8,128)(2,1)S(1)}, u32[]{:S(2)}, u32[]{:S(2)}) collective-permute-start(bf16[6,264,512]{2,1,0:T(8,128)(2,1)S(1)} %get-tuple-element.54.a_ref), channel_id=1, source_target_pairs={{0,1},{1,2},{2,3},{3,4},{4,5},{5,6},{6,7},{7,8},{8,9},{9,10},{10,1... | collective-permute-start | bytes 4866056 | tf_op jit(solution)/shard_map/ppermute | solution.py:555
  9.1 2.1 %collective-permute-start.1 = (bf16[2,264,512]{2,1,0:T(8,128)(2,1)S(1)}, bf16[2,264,512]{2,1,0:T(8,128)(2,1)S(1)}, u32[]{:S(2)}, u32[]{:S(2)}) collective-permute-start(bf16[2,264,512]{2,1,0:T(8,128)(2,1)S(1)} %get-tuple-element.58), channel_id=1, source_target_pairs={{0,32},{16,48},{32,0},{48,16},{64,96},{80,112},{96,64},{112,80},{1... | collective-permute-start | bytes 1622024 | tf_op jit(solution)/shard_map/ppermute | solution.py:558
  11.3 2.5 %collective-permute-start.2 = (bf16[2,264,512]{2,1,0:T(8,128)(2,1)S(1)}, bf16[2,264,512]{2,1,0:T(8,128)(2,1)S(1)}, u32[]{:S(2)}, u32[]{:S(2)}) collective-permute-start(bf16[2,264,512]{2,1,0:T(8,128)(2,1)S(1)} %get-tuple-element.59), channel_id=1, source_target_pairs={{0,96},{16,112},{32,64},{48,80},{64,32},{80,48},{96,0},{112,16},{1... | collective-permute-start | bytes 1622024 | tf_op jit(solution)/shard_map/ppermute | solution.py:558
  13.8 9.2 %collective-permute-done.1.refs_0_ = bf16[2,264,512]{2,1,0:T(8,128)(2,1)S(1)} collective-permute-done((bf16[2,264,512]{2,1,0:T(8,128)(2,1)S(1)}, bf16[2,264,512]{2,1,0:T(8,128)(2,1)S(1)}, u32[]{:S(2)}, u32[]{:S(2)}) %collective-permute-start.1) | collective-permute-done | bytes 540704 | tf_op jit(solution)/shard_map/ppermute | solution.py:558
  23.0 2.7 %collective-permute-done.2.refs_1_ = bf16[2,264,512]{2,1,0:T(8,128)(2,1)S(1)} collective-permute-done((bf16[2,264,512]{2,1,0:T(8,128)(2,1)S(1)}, bf16[2,264,512]{2,1,0:T(8,128)(2,1)S(1)}, u32[]{:S(2)}, u32[]{:S(2)}) %collective-permute-start.2) | collective-permute-done | bytes 540704 | tf_op jit(solution)/shard_map/ppermute | solution.py:558
  25.6 1.3 collective-permute-start.5
  27.0 5.0 %local_first.1 = (bf16[6,1536,256]{2,1,0:T(8,128)(2,1)S(1)}, f32[16,1536]{1,0:T(8,128)S(1)}, f32[1536,128]{1,0:T(8,128)S(1)}, bf16[32,1536]{1,0:T(8,128)(2,1)S(1)}) custom-call(bf16[6,264,512]{2,1,0:T(8,128)(2,1)S(1)} %get-tuple-element.54.a_ref), custom_call_target="tpu_custom_call" | custom-call | tf_op jit(solution)/shard_map/local_first/pallas_call | solution.py:164
  31.9 0.7 shard_map.50
  32.7 4.6 %collective-permute-done.4.refs_0_.refs_3_ = bf16[2,264,512]{2,1,0:T(8,128)(2,1)S(1)} collective-permute-done((bf16[2,264,512]{2,1,0:T(8,128)(2,1)S(1)}, bf16[2,264,512]{2,1,0:T(8,128)(2,1)S(1)}, u32[]{:S(2)}, u32[]{:S(2)}) %collective-permute-start.4) | collective-permute-done | bytes 540704 | tf_op jit(solution)/shard_map/ppermute | solution.py:558
  37.3 4.0 %collective-permute-done.5.refs_1_.refs_4_ = bf16[2,264,512]{2,1,0:T(8,128)(2,1)S(1)} collective-permute-done((bf16[2,264,512]{2,1,0:T(8,128)(2,1)S(1)}, bf16[2,264,512]{2,1,0:T(8,128)(2,1)S(1)}, u32[]{:S(2)}, u32[]{:S(2)}) %collective-permute-start.5) | collective-permute-done | bytes 540704 | tf_op jit(solution)/shard_map/ppermute | solution.py:558
  41.3 0.7 collective-permute-start.9
  42.0 2.1 %collective-permute-start.10 = (bf16[2,264,512]{2,1,0:T(8,128)(2,1)S(1)}, bf16[2,264,512]{2,1,0:T(8,128)(2,1)S(1)}, u32[]{:S(2)}, u32[]{:S(2)}) collective-permute-start(bf16[2,264,512]{2,1,0:T(8,128)(2,1)S(1)} %get-tuple-element.74), channel_id=1, source_target_pairs={{0,80},{16,64},{32,112},{48,96},{64,16},{80,0},{96,48},{112,32},{1... | collective-permute-start | bytes 1622024 | tf_op jit(solution)/shard_map/ppermute | solution.py:558
  44.1 0.1 collective-permute-start.11
  44.2 0.8 shard_map.51
  45.0 6.0 %band_own.1 = (bf16[6,1536,256]{2,1,0:T(8,128)(2,1)S(1)}, f32[16,1536]{1,0:T(8,128)S(1)}, f32[16,1536]{1,0:T(8,128)S(1)}, f32[8,1536]{1,0:T(8,128)S(1)}, bf16[32,1536]{1,0:T(8,128)(2,1)S(1)}) custom-call(bf16[6,264,512]{2,1,0:T(8,128)(2,1)S(1)} %get-tuple-element.54.a_ref, f32[1536,128]{1,0:T(8,128)S(1)} %get-tuple-element.56.na, ...), custom_call_target="tpu_custom_call" | custom-call | tf_op jit(solution)/shard_map/band_own/pallas_call | solution.py:203
  51.0 0.0 collective-permute-done.6.a_ref
  51.0 6.2 %band_left.1 = (bf16[6,1536,256]{2,1,0:T(8,128)(2,1)S(1)}, f32[16,1536]{1,0:T(8,128)S(1)}, f32[16,1536]{1,0:T(8,128)S(1)}) custom-call(bf16[6,264,512]{2,1,0:T(8,128)(2,1)S(1)} %collective-permute-done.6.a_ref, bf16[6,264,512]{2,1,0:T(8,128)(2,1)S(1)} %collective-permute-done.b_ref, f32[8,1536]{1,0:T(8,128)S(1)} %get-tuple-element.66.nb, ...), custom_call_target="tpu_custom_call" | custom-call | tf_op jit(solution)/shard_map/band_left/pallas_call | solution.py:226
  57.3 7.8 %collective-permute-start.7 = (f32[16,1536]{1,0:T(8,128)S(1)}, f32[16,1536]{1,0:T(8,128)S(1)}, u32[]{:S(2)}, u32[]{:S(2)}) collective-permute-start(f32[16,1536]{1,0:T(8,128)S(1)} %get-tuple-element.69), channel_id=1, source_target_pairs={{0,1},{1,2},{2,3},{3,4},{4,5},{5,6},{6,7},{7,8},{8,9},{9,10},{10,1... | collective-permute-start | bytes 294920 | tf_op jit(solution)/shard_map/ppermute | solution.py:555
  65.1 1.3 collective-permute-start.8
  66.4 1.7 %collective-permute-done.11.refs_7_ = f32[2,16,256]{2,1,0:T(8,128)S(1)} collective-permute-done((f32[2,16,256]{2,1,0:T(8,128)S(1)}, f32[2,16,256]{2,1,0:T(8,128)S(1)}, u32[]{:S(2)}, u32[]{:S(2)}) %collective-permute-start.11) | collective-permute-done | bytes 32800 | tf_op jit(solution)/shard_map/ppermute | solution.py:558
  68.1 1.7 %collective-permute-start.12 = (f32[2,16,256]{2,1,0:T(8,128)S(1)}, f32[2,16,256]{2,1,0:T(8,128)S(1)}, u32[]{:S(2)}, u32[]{:S(2)}) collective-permute-start(f32[2,16,256]{2,1,0:T(8,128)S(1)} %get-tuple-element.77), channel_id=1, source_target_pairs={{0,96},{16,112},{32,64},{48,80},{64,32},{80,48},{96,0},{112,16},{1... | collective-permute-start | bytes 98312 | tf_op jit(solution)/shard_map/ppermute | solution.py:558
  69.8 0.3 collective-permute-start.14
  70.1 0.7 shard_map.52
  70.8 2.4 %collective-permute-done.12.refs_8_ = f32[2,16,256]{2,1,0:T(8,128)S(1)} collective-permute-done((f32[2,16,256]{2,1,0:T(8,128)S(1)}, f32[2,16,256]{2,1,0:T(8,128)S(1)}, u32[]{:S(2)}, u32[]{:S(2)}) %collective-permute-start.12) | collective-permute-done | bytes 32800 | tf_op jit(solution)/shard_map/ppermute | solution.py:558
  73.2 1.7 %collective-permute-start.15 = (f32[2,16,256]{2,1,0:T(8,128)S(1)}, f32[2,16,256]{2,1,0:T(8,128)S(1)}, u32[]{:S(2)}, u32[]{:S(2)}) collective-permute-start(f32[2,16,256]{2,1,0:T(8,128)S(1)} %get-tuple-element.80), channel_id=1, source_target_pairs={{0,112},{16,96},{32,80},{48,64},{64,48},{80,32},{96,16},{112,0},{1... | collective-permute-start | bytes 98312 | tf_op jit(solution)/shard_map/ppermute | solution.py:558
  74.9 4.4 %collective-permute-start.16 = (f32[2,16,256]{2,1,0:T(8,128)S(1)}, f32[2,16,256]{2,1,0:T(8,128)S(1)}, u32[]{:S(2)}, u32[]{:S(2)}) collective-permute-start(f32[2,16,256]{2,1,0:T(8,128)S(1)} %get-tuple-element.81), channel_id=1, source_target_pairs={{0,64},{16,80},{32,96},{48,112},{64,0},{80,16},{96,32},{112,48},{1... | collective-permute-start | bytes 98312 | tf_op jit(solution)/shard_map/ppermute | solution.py:558
  79.3 1.9 %collective-permute-done.16.refs_12_ = f32[2,16,256]{2,1,0:T(8,128)S(1)} collective-permute-done((f32[2,16,256]{2,1,0:T(8,128)S(1)}, f32[2,16,256]{2,1,0:T(8,128)S(1)}, u32[]{:S(2)}, u32[]{:S(2)}) %collective-permute-start.16) | collective-permute-done | bytes 32800 | tf_op jit(solution)/shard_map/ppermute | solution.py:558
  81.2 3.0 %collective-permute-done.17.refs_13_ = f32[2,16,256]{2,1,0:T(8,128)S(1)} collective-permute-done((f32[2,16,256]{2,1,0:T(8,128)S(1)}, f32[2,16,256]{2,1,0:T(8,128)S(1)}, u32[]{:S(2)}, u32[]{:S(2)}) %collective-permute-start.17) | collective-permute-done | bytes 32800 | tf_op jit(solution)/shard_map/ppermute | solution.py:558
  84.2 0.8 combine.1
  85.0 0.0 collective-permute-start.20
  85.1 1.3 collective-permute-start.19
  86.4 4.5 %collective-permute-start.18 = (f32[8,1536]{1,0:T(8,128)S(1)}, f32[8,1536]{1,0:T(8,128)S(1)}, u32[]{:S(2)}, u32[]{:S(2)}) collective-permute-start(f32[8,1536]{1,0:T(8,128)S(1)} %get-tuple-element.83.w_ref), channel_id=1, source_target_pairs={{0,1},{1,2},{2,3},{3,4},{4,5},{5,6},{6,7},{7,8},{8,9},{9,10},{10,1... | collective-permute-start | bytes 147464 | tf_op jit(solution)/shard_map/ppermute | solution.py:555
  90.9 0.1 collective-permute-start.21
  91.0 3.0 %collective-permute-start.22 = (f32[2,16,256]{2,1,0:T(8,128)S(1)}, f32[2,16,256]{2,1,0:T(8,128)S(1)}, u32[]{:S(2)}, u32[]{:S(2)}) collective-permute-start(f32[2,16,256]{2,1,0:T(8,128)S(1)} %get-tuple-element.97), channel_id=1, source_target_pairs={{0,64},{16,80},{32,96},{48,112},{64,0},{80,16},{96,32},{112,48},{1... | collective-permute-start | bytes 98312 | tf_op jit(solution)/shard_map/ppermute | solution.py:558
  94.0 1.7 %collective-permute-start.23 = (f32[2,16,256]{2,1,0:T(8,128)S(1)}, f32[2,16,256]{2,1,0:T(8,128)S(1)}, u32[]{:S(2)}, u32[]{:S(2)}) collective-permute-start(f32[2,16,256]{2,1,0:T(8,128)S(1)} %get-tuple-element.98), channel_id=1, source_target_pairs={{0,96},{16,112},{32,64},{48,80},{64,32},{80,48},{96,0},{112,16},{1... | collective-permute-start | bytes 98312 | tf_op jit(solution)/shard_map/ppermute | solution.py:558
  95.7 0.7 local_second.1._.loc_ref.refs_0_
  96.5 3.8 %band_second.1 = (f32[8,1536]{1,0:T(8,128)S(1)}, f32[8,1536]{1,0:T(8,128)S(1)}, f32[8,1536]{1,0:T(8,128)S(1)}) custom-call(bf16[6,1536,256]{2,1,0:T(8,128)(2,1)S(1)} %get-tuple-element.86.kl_ref, bf16[6,1536,256]{2,1,0:T(8,128)(2,1)S(1)} %get-tuple-element.87.ko_ref, f32[8,1536]{1,0:T(8,128)S(1)} %collective-permute-done.18.wl_ref, ...), custom_call_target="tpu_custom_call" | custom-call | tf_op jit(solution)/shard_map/band_second/pallas_call | solution.py:402
  100.3 1.4 cross_second.1
  101.7 5.0 %all-to-all-start = ((f32[8,24,256]{2,1,0:T(8,128)}), f32[8,24,256]{2,1,0:T(8,128)S(1)}, u32[]{:S(2)}, u32[]{:S(2)}) async-start(f32[8,24,256]{2,1,0:T(8,128)} %get-tuple-element.101), calls=%async_computation | async-start | bytes 393216 | tf_op jit(solution)/shard_map/all_to_all | solution.py:561
  106.6 6.7 %collective-permute-start.24 = (f32[8,1536]{1,0:T(8,128)S(1)}, f32[8,1536]{1,0:T(8,128)S(1)}, u32[]{:S(2)}, u32[]{:S(2)}) collective-permute-start(f32[8,1536]{1,0:T(8,128)S(1)} %get-tuple-element.100), channel_id=1, source_target_pairs={{0,1},{1,2},{2,3},{3,4},{4,5},{5,6},{6,7},{7,8},{8,9},{9,10},{10,1... | collective-permute-start | bytes 147464 | tf_op jit(solution)/shard_map/ppermute | solution.py:555
  113.4 1.3 collective-permute-start.25
  114.7 0.4 collective-permute-done.24.refs_3_
  115.1 4.3 %collective-permute-done.25.refs_4_ = f32[8,1536]{1,0:T(8,128)S(1)} collective-permute-done((f32[8,1536]{1,0:T(8,128)S(1)}, f32[8,1536]{1,0:T(8,128)S(1)}, u32[]{:S(2)}, u32[]{:S(2)}) %collective-permute-start.25) | collective-permute-done | bytes 49184 | tf_op jit(solution)/shard_map/ppermute | solution.py:552
  119.3 0.7 group_sum.1
  120.0 19.1 %all_to_all.10.g_ref = f32[16,8,128]{2,1,0:T(8,128)S(1)} all-to-all(f32[16,8,128]{2,1,0:T(8,128)S(1)} %get-tuple-element.102), channel_id=1, replica_groups=mesh['group'=8,'dev'=16] {'dev'}, dimensions={0} | all-to-all | bytes 131072 | tf_op jit(solution)/shard_map/all_to_all | solution.py:561
  139.1 1.1 finish.1
  (24 shorter events, 0.1 us)
Async XLA Ops:
  3.2 41.8 %collective-permute-start = (bf16[6,264,512]{2,1,0:T(8,128)(2,1)S(1)}, bf16[6,264,512]{2,1,0:T(8,128)(2,1)S(1)}, u32[]{:S(2)}, u32[]{:S(2)}) collective-permute-start(bf16[6,264,512]{2,1,0:T(8,128)(2,1)S(1)} %get-tuple-element.54.a_ref), channel_id=1, source_target_pairs={{1,0},{2,1},{3,2},{4,3},{5,4},{6,5},{7,6},{8,7},{9,8},{10,9},{11,1... | collective-permute-start | bytes 4866056 | tf_op jit(solution)/shard_map/ppermute | solution.py:552
  4.5 46.5 %collective-permute-start.6 = (bf16[6,264,512]{2,1,0:T(8,128)(2,1)S(1)}, bf16[6,264,512]{2,1,0:T(8,128)(2,1)S(1)}, u32[]{:S(2)}, u32[]{:S(2)}) collective-permute-start(bf16[6,264,512]{2,1,0:T(8,128)(2,1)S(1)} %get-tuple-element.54.a_ref), channel_id=1, source_target_pairs={{0,1},{1,2},{2,3},{3,4},{4,5},{5,6},{6,7},{7,8},{8,9},{9,10},{10,1... | collective-permute-start | bytes 4866056 | tf_op jit(solution)/shard_map/ppermute | solution.py:555
  9.1 13.8 %collective-permute-start.1 = (bf16[2,264,512]{2,1,0:T(8,128)(2,1)S(1)}, bf16[2,264,512]{2,1,0:T(8,128)(2,1)S(1)}, u32[]{:S(2)}, u32[]{:S(2)}) collective-permute-start(bf16[2,264,512]{2,1,0:T(8,128)(2,1)S(1)} %get-tuple-element.58), channel_id=1, source_target_pairs={{0,32},{16,48},{32,0},{48,16},{64,96},{80,112},{96,64},{112,80},{1... | collective-permute-start | bytes 1622024 | tf_op jit(solution)/shard_map/ppermute | solution.py:558
  11.3 14.4 %collective-permute-start.2 = (bf16[2,264,512]{2,1,0:T(8,128)(2,1)S(1)}, bf16[2,264,512]{2,1,0:T(8,128)(2,1)S(1)}, u32[]{:S(2)}, u32[]{:S(2)}) collective-permute-start(bf16[2,264,512]{2,1,0:T(8,128)(2,1)S(1)} %get-tuple-element.59), channel_id=1, source_target_pairs={{0,96},{16,112},{32,64},{48,80},{64,32},{80,48},{96,0},{112,16},{1... | collective-permute-start | bytes 1622024 | tf_op jit(solution)/shard_map/ppermute | solution.py:558
  13.8 18.2 %collective-permute-start.3 = (bf16[2,264,512]{2,1,0:T(8,128)(2,1)S(1)}, bf16[2,264,512]{2,1,0:T(8,128)(2,1)S(1)}, u32[]{:S(2)}, u32[]{:S(2)}) collective-permute-start(bf16[2,264,512]{2,1,0:T(8,128)(2,1)S(1)} %get-tuple-element.60), channel_id=1, source_target_pairs={{0,16},{16,0},{32,48},{48,32},{64,80},{80,64},{96,112},{112,96},{1... | collective-permute-start | bytes 1622024 | tf_op jit(solution)/shard_map/ppermute | solution.py:558
  23.0 14.3 %collective-permute-start.4 = (bf16[2,264,512]{2,1,0:T(8,128)(2,1)S(1)}, bf16[2,264,512]{2,1,0:T(8,128)(2,1)S(1)}, u32[]{:S(2)}, u32[]{:S(2)}) collective-permute-start(bf16[2,264,512]{2,1,0:T(8,128)(2,1)S(1)} %get-tuple-element.62), channel_id=1, source_target_pairs={{0,48},{16,32},{32,16},{48,0},{64,112},{80,96},{96,80},{112,64},{1... | collective-permute-start | bytes 1622024 | tf_op jit(solution)/shard_map/ppermute | solution.py:558
  25.6 15.7 %collective-permute-start.5 = (bf16[2,264,512]{2,1,0:T(8,128)(2,1)S(1)}, bf16[2,264,512]{2,1,0:T(8,128)(2,1)S(1)}, u32[]{:S(2)}, u32[]{:S(2)}) collective-permute-start(bf16[2,264,512]{2,1,0:T(8,128)(2,1)S(1)} %get-tuple-element.63), channel_id=1, source_target_pairs={{0,112},{16,96},{32,80},{48,64},{64,48},{80,32},{96,16},{112,0},{1... | collective-permute-start | bytes 1622024 | tf_op jit(solution)/shard_map/ppermute | solution.py:558
  41.3 28.5 %collective-permute-start.9 = (bf16[2,264,512]{2,1,0:T(8,128)(2,1)S(1)}, bf16[2,264,512]{2,1,0:T(8,128)(2,1)S(1)}, u32[]{:S(2)}, u32[]{:S(2)}) collective-permute-start(bf16[2,264,512]{2,1,0:T(8,128)(2,1)S(1)} %get-tuple-element.73), channel_id=1, source_target_pairs={{0,64},{16,80},{32,96},{48,112},{64,0},{80,16},{96,32},{112,48},{1... | collective-permute-start | bytes 1622024 | tf_op jit(solution)/shard_map/ppermute | solution.py:558
  42.0 27.8 %collective-permute-start.10 = (bf16[2,264,512]{2,1,0:T(8,128)(2,1)S(1)}, bf16[2,264,512]{2,1,0:T(8,128)(2,1)S(1)}, u32[]{:S(2)}, u32[]{:S(2)}) collective-permute-start(bf16[2,264,512]{2,1,0:T(8,128)(2,1)S(1)} %get-tuple-element.74), channel_id=1, source_target_pairs={{0,80},{16,64},{32,112},{48,96},{64,16},{80,0},{96,48},{112,32},{1... | collective-permute-start | bytes 1622024 | tf_op jit(solution)/shard_map/ppermute | solution.py:558
  44.1 24.0 %collective-permute-start.11 = (f32[2,16,256]{2,1,0:T(8,128)S(1)}, f32[2,16,256]{2,1,0:T(8,128)S(1)}, u32[]{:S(2)}, u32[]{:S(2)}) collective-permute-start(f32[2,16,256]{2,1,0:T(8,128)S(1)} %get-tuple-element.76), channel_id=1, source_target_pairs={{0,32},{16,48},{32,0},{48,16},{64,96},{80,112},{96,64},{112,80},{1... | collective-permute-start | bytes 98312 | tf_op jit(solution)/shard_map/ppermute | solution.py:558
  51.0 33.1 %copy-start = (f32[8,1536]{1,0:T(8,128)S(1)}, f32[8,1536]{1,0:T(8,128)}, u32[]{:S(2)}) copy-start(f32[8,1536]{1,0:T(8,128)} %r_ref.3) | copy-start | bytes 147460
  57.3 26.9 %collective-permute-start.7 = (f32[16,1536]{1,0:T(8,128)S(1)}, f32[16,1536]{1,0:T(8,128)S(1)}, u32[]{:S(2)}, u32[]{:S(2)}) collective-permute-start(f32[16,1536]{1,0:T(8,128)S(1)} %get-tuple-element.69), channel_id=1, source_target_pairs={{0,1},{1,2},{2,3},{3,4},{4,5},{5,6},{6,7},{7,8},{8,9},{9,10},{10,1... | collective-permute-start | bytes 294920 | tf_op jit(solution)/shard_map/ppermute | solution.py:555
  65.1 19.0 %collective-permute-start.8 = (f32[16,1536]{1,0:T(8,128)S(1)}, f32[16,1536]{1,0:T(8,128)S(1)}, u32[]{:S(2)}, u32[]{:S(2)}) collective-permute-start(f32[16,1536]{1,0:T(8,128)S(1)} %get-tuple-element.70._), channel_id=1, source_target_pairs={{1,0},{2,1},{3,2},{4,3},{5,4},{6,5},{7,6},{8,7},{9,8},{10,9},{11,1... | collective-permute-start | bytes 294920 | tf_op jit(solution)/shard_map/ppermute | solution.py:552
  68.1 5.1 %collective-permute-start.12 = (f32[2,16,256]{2,1,0:T(8,128)S(1)}, f32[2,16,256]{2,1,0:T(8,128)S(1)}, u32[]{:S(2)}, u32[]{:S(2)}) collective-permute-start(f32[2,16,256]{2,1,0:T(8,128)S(1)} %get-tuple-element.77), channel_id=1, source_target_pairs={{0,96},{16,112},{32,64},{48,80},{64,32},{80,48},{96,0},{112,16},{1... | collective-permute-start | bytes 98312 | tf_op jit(solution)/shard_map/ppermute | solution.py:558
  69.8 5.1 %collective-permute-start.13 = (f32[2,16,256]{2,1,0:T(8,128)S(1)}, f32[2,16,256]{2,1,0:T(8,128)S(1)}, u32[]{:S(2)}, u32[]{:S(2)}) collective-permute-start(f32[2,16,256]{2,1,0:T(8,128)S(1)} %get-tuple-element.78), channel_id=1, source_target_pairs={{0,16},{16,0},{32,48},{48,32},{64,80},{80,64},{96,112},{112,96},{1... | collective-permute-start | bytes 98312 | tf_op jit(solution)/shard_map/ppermute | solution.py:558
  69.8 9.5 %collective-permute-start.14 = (f32[2,16,256]{2,1,0:T(8,128)S(1)}, f32[2,16,256]{2,1,0:T(8,128)S(1)}, u32[]{:S(2)}, u32[]{:S(2)}) collective-permute-start(f32[2,16,256]{2,1,0:T(8,128)S(1)} %get-tuple-element.79), channel_id=1, source_target_pairs={{0,48},{16,32},{32,16},{48,0},{64,112},{80,96},{96,80},{112,64},{1... | collective-permute-start | bytes 98312 | tf_op jit(solution)/shard_map/ppermute | solution.py:558
  73.2 6.1 %collective-permute-start.15 = (f32[2,16,256]{2,1,0:T(8,128)S(1)}, f32[2,16,256]{2,1,0:T(8,128)S(1)}, u32[]{:S(2)}, u32[]{:S(2)}) collective-permute-start(f32[2,16,256]{2,1,0:T(8,128)S(1)} %get-tuple-element.80), channel_id=1, source_target_pairs={{0,112},{16,96},{32,80},{48,64},{64,48},{80,32},{96,16},{112,0},{1... | collective-permute-start | bytes 98312 | tf_op jit(solution)/shard_map/ppermute | solution.py:558
  74.9 6.3 %collective-permute-start.16 = (f32[2,16,256]{2,1,0:T(8,128)S(1)}, f32[2,16,256]{2,1,0:T(8,128)S(1)}, u32[]{:S(2)}, u32[]{:S(2)}) collective-permute-start(f32[2,16,256]{2,1,0:T(8,128)S(1)} %get-tuple-element.81), channel_id=1, source_target_pairs={{0,64},{16,80},{32,96},{48,112},{64,0},{80,16},{96,32},{112,48},{1... | collective-permute-start | bytes 98312 | tf_op jit(solution)/shard_map/ppermute | solution.py:558
  79.3 4.8 %collective-permute-start.17 = (f32[2,16,256]{2,1,0:T(8,128)S(1)}, f32[2,16,256]{2,1,0:T(8,128)S(1)}, u32[]{:S(2)}, u32[]{:S(2)}) collective-permute-start(f32[2,16,256]{2,1,0:T(8,128)S(1)} %get-tuple-element.82), channel_id=1, source_target_pairs={{0,80},{16,64},{32,112},{48,96},{64,16},{80,0},{96,48},{112,32},{1... | collective-permute-start | bytes 98312 | tf_op jit(solution)/shard_map/ppermute | solution.py:558
  85.0 5.9 %collective-permute-start.20 = (f32[4,16,256]{2,1,0:T(8,128)S(1)}, f32[4,16,256]{2,1,0:T(8,128)S(1)}, u32[]{:S(2)}, u32[]{:S(2)}) collective-permute-start(f32[4,16,256]{2,1,0:T(8,128)S(1)} %get-tuple-element.94), channel_id=1, source_target_pairs={{0,16},{16,0},{32,48},{48,32},{64,80},{80,64},{96,112},{112,96},{1... | collective-permute-start | bytes 196616 | tf_op jit(solution)/shard_map/ppermute | solution.py:558
  85.1 11.4 %collective-permute-start.19 = (f32[8,1536]{1,0:T(8,128)S(1)}, f32[8,1536]{1,0:T(8,128)S(1)}, u32[]{:S(2)}, u32[]{:S(2)}) collective-permute-start(f32[8,1536]{1,0:T(8,128)S(1)} %get-tuple-element.83.w_ref), channel_id=1, source_target_pairs={{1,0},{2,1},{3,2},{4,3},{5,4},{6,5},{7,6},{8,7},{9,8},{10,9},{11,1... | collective-permute-start | bytes 147464 | tf_op jit(solution)/shard_map/ppermute | solution.py:552
  86.4 10.1 %collective-permute-start.18 = (f32[8,1536]{1,0:T(8,128)S(1)}, f32[8,1536]{1,0:T(8,128)S(1)}, u32[]{:S(2)}, u32[]{:S(2)}) collective-permute-start(f32[8,1536]{1,0:T(8,128)S(1)} %get-tuple-element.83.w_ref), channel_id=1, source_target_pairs={{0,1},{1,2},{2,3},{3,4},{4,5},{5,6},{6,7},{7,8},{8,9},{9,10},{10,1... | collective-permute-start | bytes 147464 | tf_op jit(solution)/shard_map/ppermute | solution.py:555
  90.9 9.3 %collective-permute-start.21 = (f32[2,16,256]{2,1,0:T(8,128)S(1)}, f32[2,16,256]{2,1,0:T(8,128)S(1)}, u32[]{:S(2)}, u32[]{:S(2)}) collective-permute-start(f32[2,16,256]{2,1,0:T(8,128)S(1)} %get-tuple-element.96), channel_id=1, source_target_pairs={{0,32},{16,48},{32,0},{48,16},{64,96},{80,112},{96,64},{112,80},{1... | collective-permute-start | bytes 98312 | tf_op jit(solution)/shard_map/ppermute | solution.py:558
  91.0 9.2 %collective-permute-start.22 = (f32[2,16,256]{2,1,0:T(8,128)S(1)}, f32[2,16,256]{2,1,0:T(8,128)S(1)}, u32[]{:S(2)}, u32[]{:S(2)}) collective-permute-start(f32[2,16,256]{2,1,0:T(8,128)S(1)} %get-tuple-element.97), channel_id=1, source_target_pairs={{0,64},{16,80},{32,96},{48,112},{64,0},{80,16},{96,32},{112,48},{1... | collective-permute-start | bytes 98312 | tf_op jit(solution)/shard_map/ppermute | solution.py:558
  94.0 6.3 %collective-permute-start.23 = (f32[2,16,256]{2,1,0:T(8,128)S(1)}, f32[2,16,256]{2,1,0:T(8,128)S(1)}, u32[]{:S(2)}, u32[]{:S(2)}) collective-permute-start(f32[2,16,256]{2,1,0:T(8,128)S(1)} %get-tuple-element.98), channel_id=1, source_target_pairs={{0,96},{16,112},{32,64},{48,80},{64,32},{80,48},{96,0},{112,16},{1... | collective-permute-start | bytes 98312 | tf_op jit(solution)/shard_map/ppermute | solution.py:558
  101.7 17.7 %all-to-all-start = ((f32[8,24,256]{2,1,0:T(8,128)}), f32[8,24,256]{2,1,0:T(8,128)S(1)}, u32[]{:S(2)}, u32[]{:S(2)}) async-start(f32[8,24,256]{2,1,0:T(8,128)} %get-tuple-element.101), calls=%async_computation | async-start | bytes 393216 | tf_op jit(solution)/shard_map/all_to_all | solution.py:561
  106.6 8.5 %collective-permute-start.24 = (f32[8,1536]{1,0:T(8,128)S(1)}, f32[8,1536]{1,0:T(8,128)S(1)}, u32[]{:S(2)}, u32[]{:S(2)}) collective-permute-start(f32[8,1536]{1,0:T(8,128)S(1)} %get-tuple-element.100), channel_id=1, source_target_pairs={{0,1},{1,2},{2,3},{3,4},{4,5},{5,6},{6,7},{7,8},{8,9},{9,10},{10,1... | collective-permute-start | bytes 147464 | tf_op jit(solution)/shard_map/ppermute | solution.py:555
  113.4 6.0 %collective-permute-start.25 = (f32[8,1536]{1,0:T(8,128)S(1)}, f32[8,1536]{1,0:T(8,128)S(1)}, u32[]{:S(2)}, u32[]{:S(2)}) collective-permute-start(f32[8,1536]{1,0:T(8,128)S(1)} %get-tuple-element.93.rl_ref), channel_id=1, source_target_pairs={{1,0},{2,1},{3,2},{4,3},{5,4},{6,5},{7,6},{8,7},{9,8},{10,9},{11,1... | collective-permute-start | bytes 147464 | tf_op jit(solution)/shard_map/ppermute | solution.py:552
